TPU v7x, 32 devices: a whole 2x2x4 slice. The times are simulated.
32 devices in a mesh: slides: 2 (over y), rows: 4 (over z), cols: 2 (over x), chan: 2 (over core).
Axes of the slice: x: 2, y: 2, z: 4, core: 2. Of those that a mesh axis runs over, the one named last changes fastest.
Arguments:
- features: bfloat16 [128, 64, 384], P(('slides', 'rows'), 'cols', 'chan'), parts along dimension 0, may hold values from -6 to 6
- gate_input: bfloat16 [128, 64, 384], P(('slides', 'rows'), 'cols', 'chan'), parts along dimension 0, may hold values from -6 to 6
- decay_idx: int32 [128, 64], P(('slides', 'rows'), 'cols'), parts along dimension 0, may hold values from 0 to 15
- log_table: float32 [16, 384], P(None, 'chan'), may hold values from -1 to 0, as said below
- state_rate: float32 [16], replicated, may hold values from 0.5 to 2
- proj_row: bfloat16 [384, 32], P('chan'), may hold values from -0.0390625 to 0.0390625
- proj_col: bfloat16 [384, 32], P('chan'), may hold values from -0.0390625 to 0.0390625
- conv_w: float32 [3, 3, 384], P(None, None, 'chan'), may hold values from -0.5 to 0.5
- conv_b: float32 [384], P('chan'), may hold values from -0.5 to 0.5
- d_skip: float32 [384], P('chan'), may hold values from 0.5 to 1.5
Outputs:
- output: bfloat16 [128, 64, 384], P(('slides', 'rows'), 'cols', 'chan'), parts along dimension 0
There are 2 independent parts, one for each index of `slides`. A program takes and returns all parts, laid end to end along the dimension named above; an argument that names none is the same for every part. Nothing has to cross between parts.
Inputs may be any that keep to these rules, and one draw needn't show every extreme that they name: `log_table`: every entry is negative.
All inputs are finite; a program needn't handle non-finite values.
Results may differ from a plain program's by a relative error of at most 0.0061.
Values may be sent and summed in bfloat16 or wider, within the bound.
No kernel may reach another device: no remote copies, remote signals or barrier semaphores. Data moves between devices by JAX's collectives and lax.ppermute only.
A program may use at most 128 MiB of HBM per device.

v0:
```python
import jax
import jax.numpy as jnp
from jax import lax
from jax.sharding import PartitionSpec as P


def entering(shard, axis, combine, identity):
    size, position = (lax.axis_size(axis), lax.axis_index(axis))
    everything = jax.tree.map(lambda part: lax.all_gather(part, axis), shard)
    start = jax.tree.map(
        lambda part, zero: jnp.broadcast_to(jnp.asarray(zero, part.dtype), part.shape),
        shard,
        identity,
    )

    def step(k, before):
        reached = k < position
        new = combine(before, jax.tree.map(lambda part: part[k], everything))
        return jax.tree.map(lambda a, b: jnp.where(reached, a, b), new, before)

    return lax.fori_loop(0, size, step, start)


def extended(block, sides, width):
    for axis, dim in sides:
        count = lax.axis_size(axis)
        forward = [(i, i + 1) for i in range(count - 1)]
        backward = [(target, source) for source, target in forward]
        low = lax.ppermute(
            lax.slice_in_dim(block, block.shape[dim] - width, None, axis=dim), axis, forward
        )
        high = lax.ppermute(lax.slice_in_dim(block, 0, width, axis=dim), axis, backward)
        block = jnp.concatenate([low, block, high], axis=dim)
    return block


def combine_pair(earlier, latter):
    return (earlier[0] + latter[0], latter[1] + jnp.exp(latter[0]) * earlier[1])


def make_carry_combine(state_rate):
    rates = state_rate[:, None, None]

    def combine_carry(earlier, latter):
        return (earlier[0] + latter[0], latter[1] + jnp.exp(rates * latter[0][None]) * earlier[1])

    return combine_carry


def lookup(decay_idx, log_table):
    entries = log_table.shape[0]
    onehot = (decay_idx[..., None] == jnp.arange(entries, dtype=jnp.int32)).astype(jnp.float32)
    return jnp.einsum("hwk,ke->hwe", onehot, log_table, precision=lax.Precision.HIGHEST)


def tile_states(values, log_decays, coeffs, state_rate, scan_axis):
    num_states = state_rate.shape[0]
    drive_cols = jnp.moveaxis(coeffs[..., :num_states], -1, 0)[..., None]
    log_sums = jnp.cumsum(log_decays, axis=scan_axis)

    def one_state(inputs):
        state_scale, drive_col = inputs
        unused, states = lax.associative_scan(
            combine_pair, (log_decays * state_scale, drive_col * values), axis=scan_axis
        )
        return states

    return (log_sums, lax.map(one_state, (state_rate, drive_cols)))


def finish(log_sums, states, inflow, coeffs, state_rate):
    num_states = states.shape[0]
    outputs = jnp.moveaxis(coeffs[..., num_states:], -1, 0)[..., None]
    carried = jnp.exp(state_rate[:, None, None, None] * log_sums[None]) * inflow
    return jnp.sum(outputs * (states + carried), axis=0)


def column_coeffs(middle, proj_col):
    return lax.psum(jnp.dot(middle, proj_col, preferred_element_type=jnp.float32), "chan")


def shards(
    features,
    gate_input,
    decay_idx,
    log_table,
    state_rate,
    proj_row,
    proj_col,
    conv_w,
    conv_b,
    d_skip,
):
    combine_carry = make_carry_combine(state_rate)
    log_decays = lookup(decay_idx, log_table)
    feats_wide = features.astype(jnp.float32)
    coeff_row = lax.psum(jnp.dot(features, proj_row, preferred_element_type=jnp.float32), "chan")
    row_sums, states = tile_states(feats_wide, log_decays, coeff_row, state_rate, 1)
    tile_ends = (row_sums[:, -1, :], states[:, :, -1, :])
    incoming = entering(
        tile_ends,
        "cols",
        combine_carry,
        (jnp.zeros_like(tile_ends[0]), jnp.zeros_like(tile_ends[1])),
    )
    swept_rows = finish(row_sums, states, incoming[1][:, :, None, :], coeff_row, state_rate)
    row_out = (swept_rows + d_skip * feats_wide).astype(jnp.bfloat16)
    padded = extended(row_out, (("rows", 0), ("cols", 1)), 1).astype(jnp.float32)
    tile_rows = row_out.shape[0]
    tile_cols = row_out.shape[1]
    convolved = jnp.zeros(row_out.shape, jnp.float32) + conv_b
    for offset_row in range(3):
        for offset_col in range(3):
            convolved = (
                convolved
                + conv_w[offset_row, offset_col]
                * padded[offset_row : offset_row + tile_rows, offset_col : offset_col + tile_cols]
            )
    middle = jax.nn.silu(convolved).astype(jnp.bfloat16)
    strip_vals = lax.all_to_all(middle, "rows", split_axis=1, concat_axis=0, tiled=True)
    strip_index = lax.all_to_all(decay_idx, "rows", split_axis=1, concat_axis=0, tiled=True)
    strip_decays = lookup(strip_index, log_table)
    strip_wide = strip_vals.astype(jnp.float32)
    coeff_col = column_coeffs(strip_vals, proj_col)
    col_sums, states = tile_states(strip_wide, strip_decays, coeff_col, state_rate, 0)
    strip_out = (
        finish(col_sums, states, jnp.zeros((), jnp.float32), coeff_col, state_rate)
        + d_skip * strip_wide
    )
    combined = lax.all_to_all(strip_out, "rows", split_axis=0, concat_axis=1, tiled=True)
    return (combined * jax.nn.silu(gate_input.astype(jnp.float32))).astype(jnp.bfloat16)


def solution(mesh):
    placed = (
        P(("slides", "rows"), "cols", "chan"),
        P(("slides", "rows"), "cols", "chan"),
        P(("slides", "rows"), "cols"),
        P(None, "chan"),
        P(),
        P("chan", None),
        P("chan", None),
        P(None, None, "chan"),
        P("chan"),
        P("chan"),
    )
    return jax.shard_map(
        shards,
        mesh=mesh,
        in_specs=placed,
        out_specs=P(("slides", "rows"), "cols", "chan"),
        check_vma=False,
    )
```

profile of v0, /device:TPU:0, one launch (start us, length us, event | category | flops | bytes accessed | tf_op | source)
XLA Modules:
  0.0 399.4 jit_solution(8053558625621068115)
XLA Ops:
  6.5 1.9 fusion.42
  9.9 6.3 %all-to-all-start.1 = ((s32[4,1,128]{2,1,0:T(1,128)}), s32[4,1,128]{2,1,0:T(1,128)S(1)}, u32[]{:S(2)}, u32[]{:S(2)}) async-start(s32[4,1,128]{2,1,0:T(1,128)} %reshape.23), calls=%async_computation.1 | async-start | bytes 4096 | tf_op jit(solution)/shard_map/all_to_all | solution.py:121
  17.8 1.8 convert_element_type.23
  20.7 4.4 %all-gather.1 = f32[32,1,192]{2,0,1:T(8,128)S(1)} all-gather(f32[16,1,192]{2,0,1:T(8,128)S(1)} %slice.400), channel_id=3, replica_groups=mesh['slides'=2,'rows'=4,'cols'=2,'chan'=2] {'cols'}, dimensions={0}, use_global_device_ids=true | all-gather | bytes 36864 | tf_op jit(solution)/shard_map/all_gather | solution.py:9
  25.1 5.5 %all-reduce.25.cloned.1.call-done = f32[16,32,32]{2,1,0:T(8,128)} async-done(((f32[16,32,32]{2,1,0:T(8,128)}), f32[16,32,32]{2,1,0:T(8,128)}) %all-reduce.25.cloned.1.call-update) | async-done | bytes 65552 | tf_op jit(solution)/shard_map/psum | solution.py:97
  30.6 1.9 slice_bitcast_fusion.3
  33.3 179.7 %while.37 = (s32[]{:T(128)}, f32[16,16,32,192]{3,2,1,0:T(8,128)}, f32[16,16,32,1]{2,1,3,0:T(8,128)}, f32[16,32,192]{2,1,0:T(8,128)}, f32[16]{0:T(128)}, /*index=5*/f32[16,32,192]{2,1,0:T(8,128)S(1)}) while((s32[]{:T(128)}, f32[16,16,32,192]{3,2,1,0:T(8,128)}, f32[16,16,32,1]{2,1,3,0:T(8,128)}, f32[16,32,192]{2,1,0:T(8,128)}, ...), condition=%wide.region_2.3_spmd.clone, body=%wide.region_1.0_spmd.sunk.clone | while | flops 998402 | bytes 15030905 | solution.py:68
  34.0 1.3 dynamic_slice.48
  35.3 1.9 broadcast_multiply_fusion.8
  45.2 1.3 dynamic_slice.48
  46.5 1.9 broadcast_multiply_fusion.8
  56.5 1.3 dynamic_slice.48
  57.8 1.9 broadcast_multiply_fusion.8
  69.0 1.9 broadcast_multiply_fusion.8
  78.9 1.3 dynamic_slice.48
  80.2 1.9 broadcast_multiply_fusion.8
  91.4 1.9 broadcast_multiply_fusion.8
  102.6 1.9 broadcast_multiply_fusion.8
  113.9 1.9 broadcast_multiply_fusion.8
  123.8 1.3 dynamic_slice.48
  125.1 1.9 broadcast_multiply_fusion.8
  135.0 1.3 dynamic_slice.48
  136.3 1.9 broadcast_multiply_fusion.8
  146.2 1.3 dynamic_slice.48
  147.5 1.9 broadcast_multiply_fusion.8
  157.5 1.3 dynamic_slice.48
  158.8 1.9 broadcast_multiply_fusion.8
  168.7 1.3 dynamic_slice.48
  170.0 1.9 broadcast_multiply_fusion.8
  179.9 1.3 dynamic_slice.48
  181.2 1.9 broadcast_multiply_fusion.8
  192.4 1.9 broadcast_multiply_fusion.8
  203.7 1.9 broadcast_multiply_fusion.8
  212.9 9.9 %copy.50 = f32[16,16,32,192]{3,1,2,0:T(8,128)S(1)} copy(f32[16,16,32,192]{3,2,1,0:T(8,128)} %get-tuple-element.178) | data formatting | bytes 12582912 | tf_op jit(solution)/shard_map/while | solution.py:68
  223.0 9.5 %all-gather = f32[32,16,1,192]{3,1,2,0:T(8,128)S(1)} all-gather(f32[16,16,1,192]{3,1,2,0:T(8,128)S(1)} %slice.399), channel_id=2, replica_groups=mesh['slides'=2,'rows'=4,'cols'=2,'chan'=2] {'cols'}, dimensions={0}, use_global_device_ids=true | all-gather | bytes 589824 | tf_op jit(solution)/shard_map/all_gather | solution.py:9
  232.9 4.8 %multiply_reduce_fusion.1 = f32[16,32,192]{2,1,0:T(8,128)S(1)} fusion(f32[16,16,32,192]{3,2,1,0:T(8,128)} %get-tuple-element.178, f32[16,16,192]{2,1,0:T(8,128)S(1)} %get-tuple-element.179, f32[16,32,192]{2,1,0:T(8,128)S(1)} %copy-done.4, f32[16]{0:T(128)S(1)} %bitcast.166, f32[16,16,32]{2,1,0:T(8,128)S(1)} %copy.46), kind=kLoop, calls=%fused_computation.70 | loop fusion | flops 7766016 | bytes 7307328 | tf_op jit(solution)/shard_map/reduce_sum | solution.py:75
  237.9 3.7 collective-permute-start
  244.2 3.0 collective-permute-done.1
  247.2 3.4 collective-permute-start.2
  252.0 4.2 %collective-permute-done.3 = bf16[18,1,192]{2,1,0:T(2,128)(2,1)S(1)} collective-permute-done((bf16[18,1,192]{2,1,0:T(2,128)(2,1)S(1)}, bf16[18,1,192]{2,1,0:T(2,128)(2,1)S(1)}, u32[]{:S(2)}, u32[]{:S(2)}) %collective-permute-start.3) | collective-permute-done | bytes 6944 | tf_op jit(solution)/shard_map/ppermute | solution.py:32
  257.8 3.7 all-to-all-start
  262.8 5.4 %all-to-all-done = bf16[16,32,192]{2,0,1:T(8,128)(2,1)S(1)} async-done(((bf16[16,32,192]{2,0,1:T(8,128)(2,1)}), bf16[16,32,192]{2,0,1:T(8,128)(2,1)S(1)}, u32[]{:S(2)}, u32[]{:S(2)}) %all-to-all-start) | async-done | bytes 196640 | tf_op jit(solution)/shard_map/all_to_all | solution.py:120
  269.3 17.2 %all-reduce.27.cloned.1.call-done = f32[64,8,32]{2,1,0:T(8,128)} async-done(((f32[64,8,32]{2,1,0:T(8,128)}), f32[64,8,32]{2,1,0:T(8,128)}) %all-reduce.27.cloned.1.call-update) | async-done | bytes 65552 | tf_op jit(solution)/shard_map/psum | solution.py:79
  286.5 1.9 slice_bitcast_fusion.1
  289.6 76.2 %while.38 = (s32[]{:T(128)}, f32[16,64,8,192]{3,2,1,0:T(8,128)}, f32[16,64,8,1]{2,1,3,0:T(8,128)}, f32[64,8,192]{2,1,0:T(8,128)S(1)}, f32[16]{0:T(128)S(1)}, /*index=5*/f32[64,8,192]{2,1,0:T(8,128)S(1)}) while((s32[]{:T(128)}, f32[16,64,8,192]{3,2,1,0:T(8,128)}, f32[16,64,8,1]{2,1,3,0:T(8,128)}, f32[64,8,192]{2,1,0:T(8,128)S(1)}, ...), condition=%wide.region_9.10_spmd.clone, body=%wide.region_8.9_spmd.sunk.clone | while | flops 1035266 | bytes 11215489 | solution.py:68
  365.8 1.5 copy.53
  367.3 4.7 %multiply_reduce_fusion = f32[64,8,192]{2,1,0:T(8,128)S(1)} fusion(f32[16,64,8,192]{3,2,1,0:T(8,128)} %get-tuple-element.180, f32[64,8,192]{2,1,0:T(8,128)} %fusion.52, f32[16]{0:T(128)S(1)} %get-tuple-element.646, f32[16,64,8]{2,1,0:T(8,128)S(1)} %copy.53), kind=kLoop, calls=%fused_computation.69 | loop fusion | flops 7766016 | bytes 7110720 | tf_op jit(solution)/shard_map/reduce_sum | solution.py:75
  372.1 19.6 %all_to_all.52 = f32[64,8,192]{2,1,0:T(8,128)S(1)} all-to-all(f32[64,8,192]{2,1,0:T(8,128)S(1)} %multiply_add_fusion.9), channel_id=1, replica_groups=mesh['slides'=2,'rows'=4,'cols'=2,'chan'=2] {'rows'}, dimensions={0} | all-to-all | bytes 786432 | tf_op jit(solution)/shard_map/all_to_all | solution.py:130
  (1533 shorter events, 218.9 us)
Async XLA Ops:
  6.5 9.7 %copy-start = (f32[16,192]{1,0:T(8,128)S(1)}, f32[16,192]{1,0:T(8,128)}, u32[]{:S(2)}) copy-start(f32[16,192]{1,0:T(8,128)} %param.19) | copy-start | bytes 36868
  6.5 24.1 %all-reduce.25.cloned.1.call-start = ((), (), s32[]{:S(2)}) async-start(), calls=%async_computation.3 | async-start | bytes 524288 | tf_op jit(solution)/shard_map/psum | solution.py:97
  9.9 233.0 %all-to-all-start.1 = ((s32[4,1,128]{2,1,0:T(1,128)}), s32[4,1,128]{2,1,0:T(1,128)S(1)}, u32[]{:S(2)}, u32[]{:S(2)}) async-start(s32[4,1,128]{2,1,0:T(1,128)} %reshape.23), calls=%async_computation.1 | async-start | bytes 4096 | tf_op jit(solution)/shard_map/all_to_all | solution.py:121
  212.9 19.5 %copy-start.7 = (f32[16]{0:T(128)S(1)}, f32[16]{0:T(128)}, u32[]{:S(2)}) copy-start(f32[16]{0:T(128)} %get-tuple-element.644) | copy-start | bytes 196
  212.9 19.8 %copy-start.5 = (f32[16,16,32]{0,2,1:T(8,128)S(1)}, f32[16,16,32]{0,2,1:T(8,128)}, u32[]{:S(2)}) copy-start(f32[16,16,32]{0,2,1:T(8,128)} %get-tuple-element.321) | copy-start | bytes 98308
  212.9 20.0 %copy-start.4 = (f32[16,32,192]{2,1,0:T(8,128)S(1)}, f32[16,32,192]{2,1,0:T(8,128)}, u32[]{:S(2)}) copy-start(f32[16,32,192]{2,1,0:T(8,128)} %copy.49) | copy-start | bytes 1179652
  222.9 14.9 %copy-start.3 = (bf16[16,32,192]{2,1,0:T(8,128)(2,1)S(1)}, bf16[16,32,192]{2,1,0:T(8,128)(2,1)}, u32[]{:S(2)}) copy-start(bf16[16,32,192]{2,1,0:T(8,128)(2,1)} %param.16) | copy-start | bytes 589828
  222.9 14.9 %copy-start.10 = (f32[192]{0:T(256)S(1)}, f32[192]{0:T(256)}, u32[]{:S(2)}) copy-start(f32[192]{0:T(256)} %param.25) | copy-start | bytes 2308
  222.9 19.9 %copy-start.9 = (f32[3,3,192]{2,1,0:T(4,128)S(1)}, f32[3,3,192]{2,1,0:T(4,128)}, u32[]{:S(2)}) copy-start(f32[3,3,192]{2,1,0:T(4,128)} %param.23) | copy-start | bytes 20740
  232.4 24.0 %copy-start.11 = (f32[192]{0:T(256)S(1)}, f32[192]{0:T(256)}, u32[]{:S(2)}) copy-start(f32[192]{0:T(256)} %param.24) | copy-start | bytes 2308
  232.9 35.4 %copy-start.8 = (bf16[192,32]{0,1:T(8,128)(2,1)S(1)}, bf16[192,32]{0,1:T(8,128)(2,1)}, u32[]{:S(2)}) copy-start(bf16[192,32]{0,1:T(8,128)(2,1)} %param.22) | copy-start | bytes 36868
  237.9 6.3 %collective-permute-start = (bf16[1,32,192]{2,1,0:T(8,128)(2,1)S(1)}, bf16[1,32,192]{2,1,0:T(8,128)(2,1)S(1)}, u32[]{:S(2)}, u32[]{:S(2)}) collective-permute-start(bf16[1,32,192]{2,1,0:T(8,128)(2,1)S(1)} %get-tuple-element.319), channel_id=1, source_target_pairs={{0,4},{4,8},{8,12},{1,5},{5,9},{9,13},{2,6},{6,10},{10,14},{3,7},{... | collective-permute-start | bytes 36872 | tf_op jit(solution)/shard_map/ppermute | solution.py:29
  241.5 5.6 %collective-permute-start.1 = (bf16[1,32,192]{2,1,0:T(8,128)(2,1)S(1)}, bf16[1,32,192]{2,1,0:T(8,128)(2,1)S(1)}, u32[]{:S(2)}, u32[]{:S(2)}) collective-permute-start(bf16[1,32,192]{2,1,0:T(8,128)(2,1)S(1)} %get-tuple-element.320), channel_id=1, source_target_pairs={{4,0},{8,4},{12,8},{5,1},{9,5},{13,9},{6,2},{10,6},{14,10},{7,3},{... | collective-permute-start | bytes 36872 | tf_op jit(solution)/shard_map/ppermute | solution.py:32
  247.2 4.8 %collective-permute-start.2 = (bf16[18,1,192]{2,1,0:T(2,128)(2,1)S(1)}, bf16[18,1,192]{2,1,0:T(2,128)(2,1)S(1)}, u32[]{:S(2)}, u32[]{:S(2)}) collective-permute-start(bf16[18,1,192]{2,1,0:T(2,128)(2,1)S(1)} %get-tuple-element.315), channel_id=1, source_target_pairs={{0,2},{1,3},{4,6},{5,7},{8,10},{9,11},{12,14},{13,15},{16,18},{17,... | collective-permute-start | bytes 20744 | tf_op jit(solution)/shard_map/ppermute | solution.py:29
  250.6 5.7 %collective-permute-start.3 = (bf16[18,1,192]{2,1,0:T(2,128)(2,1)S(1)}, bf16[18,1,192]{2,1,0:T(2,128)(2,1)S(1)}, u32[]{:S(2)}, u32[]{:S(2)}) collective-permute-start(bf16[18,1,192]{2,1,0:T(2,128)(2,1)S(1)} %get-tuple-element.316), channel_id=1, source_target_pairs={{2,0},{3,1},{6,4},{7,5},{10,8},{11,9},{14,12},{15,13},{18,16},{19,... | collective-permute-start | bytes 20744 | tf_op jit(solution)/shard_map/ppermute | solution.py:32
  257.8 10.5 %all-to-all-start = ((bf16[16,32,192]{2,0,1:T(8,128)(2,1)}), bf16[16,32,192]{2,0,1:T(8,128)(2,1)S(1)}, u32[]{:S(2)}, u32[]{:S(2)}) async-start(bf16[16,32,192]{2,0,1:T(8,128)(2,1)} %copy.51), calls=%async_computation | async-start | bytes 524288 | tf_op jit(solution)/shard_map/all_to_all | solution.py:120
  261.4 25.0 %all-reduce.27.cloned.1.call-start = ((), (), s32[]{:S(2)}) async-start(), calls=%async_computation.4 | async-start | bytes 524288 | tf_op jit(solution)/shard_map/psum | solution.py:79
  268.3 21.3 %copy-start.1 = (bf16[16,4,8,192]{3,2,0,1:T(8,128)(2,1)}, bf16[16,4,8,192]{3,2,0,1:T(8,128)(2,1)S(1)}, u32[]{:S(2)}) copy-start(bf16[16,4,8,192]{3,2,0,1:T(8,128)(2,1)S(1)} %copy.52) | copy-start | bytes 589828
  365.8 6.2 %copy-start.2 = (bf16[16,4,8,192]{3,2,0,1:T(8,128)(2,1)S(1)}, bf16[16,4,8,192]{3,2,0,1:T(8,128)(2,1)}, u32[]{:S(2)}) copy-start(bf16[16,4,8,192]{3,2,0,1:T(8,128)(2,1)} %copy-done.1) | copy-start | bytes 589828
  365.8 25.9 %copy-start.6 = (bf16[16,32,192]{2,1,0:T(8,128)(2,1)S(1)}, bf16[16,32,192]{2,1,0:T(8,128)(2,1)}, u32[]{:S(2)}) copy-start(bf16[16,32,192]{2,1,0:T(8,128)(2,1)} %param.17) | copy-start | bytes 589828
Sparse Core Ops, SparseCore 0:
  9.7 20.9 all-reduce.24
  269.4 17.0 all-reduce.26
where the time goes:
time: 403 us; the launch traced here: 399 us
  local copies, waits for them, and re-layouts  178 us (44%)
  other arithmetic  104 us (26%)
  waiting for transfers between devices  35.4 us (9%)
  blocking collectives  33.5 us (8%)
  starting transfers between devices  19.6 us (5%)
  between operations  13.7 us (3%)
  loops' own time  10.1 us (3%)
  matrix products  4.34 us (1%)
    slice x464, local copies, waits for them, and re-layouts, one_state(): lax.associative_scan(combine_pair, (log_decays * state_scale, drive_col *...  66 us
    mul x32, other arithmetic, one_state(): log_decays * state_scale  41.8 us
    pad x288, local copies, waits for them, and re-layouts, one_state(): lax.associative_scan(combine_pair, (log_decays * state_scale, drive_col *...  36.8 us
    dynamic_slice x32, local copies, waits for them, and re-layouts, tile_states(): return (log_sums, lax.map(one_state, (state_rate, drive_cols)))  30.6 us
    dynamic_update_slice x32, other arithmetic, tile_states(): return (log_sums, lax.map(one_state, (state_rate, drive_cols)))  28.1 us
    mul x32, local copies, waits for them, and re-layouts, one_state(): drive_col * values  23.3 us
    all_to_all x1, blocking collectives, shards(): lax.all_to_all(strip_out, 'rows', split_axis=0, concat_axis=1, tiled=True)  19.6 us
    psum x1, waiting for transfers between devices, column_coeffs(): lax.psum(jnp.dot(middle, proj_col, preferred_element_type=jnp.float32), '...  17.2 us
  transfers between devices with their start and end apart: 8, of which 6 were waited for; matrix products, arithmetic and copies ran while one was open for 50% of the time, Pallas kernels for 0%

commit v1 on v0

v1 whole, which is shorter than its diff:
```python
import jax
import jax.numpy as jnp
from jax import lax
from jax.experimental import pallas as pl
from jax.experimental.pallas import tpu as pltpu
from jax.sharding import PartitionSpec as P

LANES = 128
SUB = 8
LOG2E = 1.4426950408889634
F32 = jnp.float32
BF16 = jnp.bfloat16


def low_half(shape):
    return lax.broadcasted_iota(jnp.int32, shape, len(shape) - 1) < LANES // 2


def twice(v):
    return jnp.concatenate([v, v], axis=-1)


def split3(t):
    hi = t.astype(BF16)
    rest = t - hi.astype(F32)
    mid = rest.astype(BF16)
    low = (rest - mid.astype(F32)).astype(BF16)
    return jnp.concatenate([hi, mid, low], axis=0)


def tables(table_ref):
    t = table_ref[...] * LOG2E
    return split3(t[:, :LANES]), split3(twice(t[:, LANES:]))


def dot(a, b):
    return jnp.dot(a, b, preferred_element_type=F32)


def pair_rates(rate_ref, rows):
    half = low_half((rows, LANES))
    states = rate_ref.shape[0]
    return [jnp.where(half, rate_ref[2 * j], rate_ref[2 * j + 1]) for j in range(states // 2)]


def advance(carry, xa, xb, la, lb, coeff, rate_ref, rates_b, wanted):
    states = rate_ref.shape[0]
    shape = xa.shape
    half = low_half(shape)

    def spread(col):
        return jnp.broadcast_to(coeff[:, col : col + 1], shape)

    drive = [spread(s) for s in range(states)]
    out = [spread(states + s) for s in range(states)] if wanted else None
    new, ya, yb = [], [], []
    for s in range(states):
        st = jnp.exp2(la * rate_ref[s]) * carry[s] + drive[s] * xa
        new.append(st)
        if wanted:
            ya.append(out[s] * st)
    for j in range(states // 2):
        b = jnp.where(half, drive[2 * j], drive[2 * j + 1])
        st = jnp.exp2(lb * rates_b[j]) * carry[states + j] + b * xb
        new.append(st)
        if wanted:
            yb.append(jnp.where(half, out[2 * j], out[2 * j + 1]) * st)
    if not wanted:
        return tuple(new), None, None

    def tree(v):
        while len(v) > 1:
            v = [v[i] + v[i + 1] for i in range(0, len(v) - 1, 2)] + v[len(v) & ~1 :]
        return v[0]

    yb = tree(yb)
    return tuple(new), tree(ya), yb + pltpu.roll(yb, LANES // 2, 1)


def row_kernel(dims, dest, *refs):
    tiles, strips, height, width, strip = dims
    rate_ref = refs[0]
    own, other = refs[1 : 1 + tiles], refs[1 + tiles : 1 + 2 * tiles]
    hots = refs[1 + 2 * tiles : 1 + 3 * tiles]
    table_ref, proj_ref, proj2_ref, skip_ref = refs[1 + 3 * tiles : 5 + 3 * tiles]
    outs = refs[5 + 3 * tiles : 5 + 3 * tiles + strips]
    xa_ref, xb_ref, la_ref, lb_ref, cf_ref, ya_ref, yb_ref = refs[5 + 3 * tiles + strips :]
    states = rate_ref.shape[0]
    cells = height * width
    col = lax.axis_index("cols")
    row = lax.axis_index("rows")

    ta, tb = tables(table_ref)
    for d in range(tiles):
        x = own[d][...].reshape(cells, -1)
        part = pl.ds(d * cells, cells)
        cf_ref[part, : 2 * states] = dot(x, proj_ref[...]) + dot(
            other[d][...].reshape(cells, -1), proj2_ref[...]
        )
        xf = x.astype(F32)
        xa_ref[part, :] = xf[:, :LANES]
        xb_ref[part, :] = twice(xf[:, LANES:])
        hot = hots[d][...]
        la_ref[part, :] = dot(hot, ta)
        lb_ref[part, :] = dot(hot, tb)

    rates_b = pair_rates(rate_ref, SUB)
    skip = skip_ref[...]
    skip_a, skip_b = skip[:, :LANES], twice(skip[:, LANES:])
    last_left = (col >= tiles - 1).astype(F32)

    for g in range(height // SUB):

        def step(carry, d, w, scale, wanted, g=g):
            place = pl.ds(d * cells + g * SUB * width + w, SUB, stride=width)
            ordered = pl.ds(pl.multiple_of(d * cells + w * height + g * SUB, SUB), SUB)
            xa, xb = xa_ref[place, :], xb_ref[place, :]
            if scale is not None:
                xa, xb = xa * scale, xb * scale
            carry, ya, yb = advance(
                carry, xa, xb, la_ref[ordered, :], lb_ref[ordered, :], cf_ref[place, :], rate_ref, rates_b, wanted
            )
            if wanted:
                ya, yb = ya + skip_a * xa, yb + skip_b * xb
            return carry, ya, yb

        def put(c, ya, yb, g=g):
            at = pl.ds(pl.multiple_of(c * height + g * SUB, SUB), SUB)
            ya_ref[at, :] = ya
            yb_ref[at, :] = yb

        carry = tuple(jnp.zeros((SUB, LANES), F32) for _ in range(states + states // 2))
        for d in range(tiles - 1, 0, -1):
            scale = (col >= d).astype(F32)
            carry = lax.fori_loop(
                0,
                width - (d == 1),
                lambda w, s, d=d, scale=scale: step(s, d, w, scale, False)[0],
                carry,
            )
        carry, ya, yb = step(carry, 1, width - 1, (col >= 1).astype(F32), True)
        put(0, ya, yb)

        def body(w, s):
            s, ya, yb = step(s, 0, w, None, True)
            put(w + 1, ya, yb)
            return s

        carry = lax.fori_loop(0, width, body, carry)
        _, ya, yb = step(carry, tiles - 1, 0, None, True)
        inside = 1.0 - last_left
        put(width + 1, ya * inside, yb * inside)

    count = strip + 2
    for d in range(strips):
        start = pl.multiple_of(dest(row, d) * strip * height, SUB)
        from_ = pl.ds(start, count * height)
        outs[d][: count * height, :] = ya_ref[from_, :].astype(BF16)
        yb = yb_ref[from_, :].reshape(count, 2, height // 2, LANES)
        low, high = yb[:, 0], yb[:, 1]
        packed = jnp.where(low_half(low.shape), low, high).reshape(count * height // 2, LANES)
        outs[d][count * height :, :] = packed.astype(BF16)


def unpack(v):
    half = low_half(v.shape)
    turned = pltpu.roll(v, LANES // 2, 1)
    return jnp.where(half, v, turned), jnp.where(half, turned, v)


def column_kernel(dims, dest, *refs):
    strips, height, strip = dims
    rate_ref = refs[0]
    blocks = (refs[1 : 1 + strips], refs[1 + strips : 1 + 2 * strips])
    at = 1 + 2 * strips
    hot_ref, table_ref = refs[at : at + 2]
    projs = refs[at + 2 : at + 4]
    conv_ws = refs[at + 4 : at + 6]
    conv_bs = refs[at + 6 : at + 8]
    skip_ref = refs[at + 8]
    outs = refs[at + 9 : at + 9 + strips]
    ra_ref, rb_ref, ma_ref, mb_ref, la_ref, lb_ref, cf_ref, ya_ref, yb_ref = refs[at + 9 + strips :]
    states = rate_ref.shape[0]
    row = lax.axis_index("rows")
    total = strips * height
    pitch = total + 2 * SUB
    count = strip + 2

    ta, tb = tables(table_ref)
    hot = hot_ref[...]
    la_ref[...] = dot(hot, ta)
    lb_ref[...] = dot(hot, tb)
    zero = jnp.zeros((SUB, LANES), F32)
    for k in range(count):
        for ref in (ra_ref, rb_ref):
            ref[pl.ds(k * pitch, SUB), :] = zero
            ref[pl.ds(k * pitch + SUB + total, SUB), :] = zero

    coeff = None
    for side in (1, 0):
        for d in range(strips):
            base = pl.multiple_of(dest(row, d) * height, SUB) + SUB
            va = blocks[side][d][: count * height, :].astype(F32)
            low, high = unpack(blocks[side][d][count * height :, :].astype(F32))
            h2 = height // 2
            for k in range(count):
                to = pl.multiple_of(base + k * pitch, SUB)
                ra_ref[pl.ds(to, height), :] = va[k * height : (k + 1) * height]
                rb_ref[pl.ds(to, h2), :] = low[k * h2 : (k + 1) * h2]
                rb_ref[pl.ds(pl.multiple_of(to + h2, SUB), h2), :] = high[k * h2 : (k + 1) * h2]
        taps = conv_ws[side][...]
        bias = conv_bs[side][...]
        for src, dst, cut in (
            (ra_ref, ma_ref, lambda v: v[..., :LANES]),
            (rb_ref, mb_ref, lambda v: twice(v[..., LANES:])),
        ):
            weights, add = cut(taps), cut(bias)
            spread = [[jnp.broadcast_to(weights[a, b][None, :], (SUB, LANES)) for b in range(3)] for a in range(3)]
            start = jnp.broadcast_to(add, (SUB, LANES))

            def conv(i, unused, src=src, dst=dst, spread=spread, start=start):
                sums = [start] * strip
                for k in range(count):
                    for a in range(3):
                        v = src[pl.ds(k * pitch + i * SUB + SUB - 1 + a, SUB), :]
                        for b in range(3):
                            if 0 <= k - b < strip:
                                sums[k - b] = sums[k - b] + spread[a][b] * v
                for k in range(strip):
                    v = sums[k] / (1.0 + jnp.exp(-sums[k]))
                    dst[pl.ds(pl.multiple_of(k * total + i * SUB, SUB), SUB), :] = v.astype(BF16).astype(F32)
                return unused

            lax.fori_loop(0, total // SUB, conv, 0)
        proj = projs[side][...]
        part = dot(ma_ref[...].astype(BF16), proj[:LANES]) + dot(
            mb_ref[:, : LANES // 2].astype(BF16), proj[LANES:]
        )
        coeff = part if coeff is None else coeff + part
    cf_ref[:, : 2 * states] = coeff

    rates_b = pair_rates(rate_ref, strip)
    skip = skip_ref[...]
    skip_a, skip_b = skip[:, :LANES], twice(skip[:, LANES:])

    def body(h, carry):
        place = pl.ds(h, strip, stride=total)
        ordered = pl.ds(h * strip if strip % SUB else pl.multiple_of(h * strip, SUB), strip)
        xa, xb = ma_ref[place, :], mb_ref[place, :]
        carry, ya, yb = advance(
            carry, xa, xb, la_ref[ordered, :], lb_ref[ordered, :], cf_ref[place, :], rate_ref, rates_b, True
        )
        ya_ref[ordered, :] = ya + skip_a * xa
        yb_ref[ordered, :] = yb + skip_b * xb
        return carry

    zeros = tuple(jnp.zeros((strip, LANES), F32) for _ in range(states + states // 2))
    lax.fori_loop(0, total, body, zeros)

    cells = height * strip
    for d in range(strips):
        start = pl.multiple_of(dest(row, d) * cells, SUB)
        from_ = pl.ds(start, cells)
        outs[d][:cells, :] = ya_ref[from_, :].astype(BF16)
        yb = yb_ref[from_, :]
        low, high = yb[: cells // 2], yb[cells // 2 :]
        outs[d][cells:, :] = jnp.where(low_half(low.shape), low, high).astype(BF16)


def gate_kernel(dims, dest, *refs):
    strips, height, width, strip = dims
    blocks, gate_ref, out_ref, ya_ref, yb_ref = refs[:strips], *refs[strips:]
    row = lax.axis_index("rows")
    cells = height * strip
    for d in range(strips):
        va = blocks[d][:cells, :].astype(F32)
        low, high = unpack(blocks[d][cells:, :].astype(F32))
        left = dest(row, d) * strip
        for h in range(height):
            to = left + h * width
            to = pl.ds(to if strip % SUB else pl.multiple_of(to, SUB), strip)
            ya_ref[to, :] = va[h * strip : (h + 1) * strip]
            b, i = (low, h) if h < height // 2 else (high, h - height // 2)
            yb_ref[to, :] = b[i * strip : (i + 1) * strip]
    gate = gate_ref[...].astype(F32)
    gate = gate / (1.0 + jnp.exp(-gate))
    out_ref[:, :, :LANES] = (ya_ref[...].reshape(height, width, LANES) * gate[:, :, :LANES]).astype(BF16)
    yb = yb_ref[...].reshape(height, width, LANES)[:, :, : LANES // 2]
    out_ref[:, :, LANES:] = (yb * gate[:, :, LANES:]).astype(BF16)


def smem():
    return pl.BlockSpec(memory_space=pltpu.SMEM)


def vmem():
    return pl.BlockSpec(memory_space=pltpu.VMEM)


def call(kernel, args, outs, scratch, name):
    return pl.pallas_call(
        kernel,
        out_shape=outs,
        in_specs=[smem() if a.ndim == 1 else vmem() for a in args],
        out_specs=jax.tree.map(lambda _: vmem(), outs),
        scratch_shapes=[pltpu.VMEM(s, F32) for s in scratch],
        name=name,
    )(*args)


def onehot(idx, entries):
    spots = jnp.arange(3 * entries, dtype=jnp.int32) % entries
    return (idx.reshape(-1, 1) == spots).astype(BF16)


def make_shards(strips, tiles):
    few = strips <= 8 and strips & (strips - 1) == 0
    swap = [(0, 1), (1, 0)]

    def dest(row, d):
        return row ^ d if few else d

    def exchange(blocks, axis="rows"):
        if few:
            return [blocks[0]] + [
                lax.ppermute(blocks[d], axis, [(i, i ^ d) for i in range(strips)]) for d in range(1, strips)
            ]
        moved = lax.all_to_all(jnp.stack(blocks), axis, 0, 0)
        return [moved[d] for d in range(strips)]

    def across(v):
        return lax.ppermute(v, "chan", swap)

    def shards(features, gate, decay_idx, log_table, rate, proj_row, proj_col, conv_w, conv_b, d_skip):
        height, width, channels = features.shape
        entries, states = log_table.shape[0], rate.shape[0]
        strip = width // strips
        cells, total, count = height * width, strips * height, strip + 2
        skip, bias = d_skip.reshape(1, channels), conv_b.reshape(1, channels)

        rounds = [[(i, (i + d) % tiles) for i in range(tiles)] for d in range(1, tiles)]
        own = [features] + [lax.ppermute(features, "cols", pairs) for pairs in rounds]
        idx = [decay_idx] + [lax.ppermute(decay_idx, "cols", pairs) for pairs in rounds]
        other = [across(f) for f in own]
        proj_row2, proj_col2 = across(proj_row), across(proj_col)
        conv_w2, bias2 = across(conv_w), across(bias)
        hots = [onehot(i.T, entries) for i in idx]
        if few:
            whole = exchange([decay_idx] * strips)
            row = lax.axis_index("rows")
            order = jnp.arange(strips) ^ row
            parts = jnp.stack([w.reshape(height, strips, strip) for w in whole])
            mine = lax.dynamic_index_in_dim(parts, row, 2, keepdims=False)
            mine = sum(
                jnp.where((order == k)[:, None, None], mine[k][None], 0) for k in range(strips)
            )
        else:
            mine = lax.all_to_all(
                decay_idx.reshape(height, strips, strip).transpose(1, 0, 2), "rows", 0, 0
            )
        hot_strip = onehot(mine, entries)

        block = jax.ShapeDtypeStruct((count * height * 3 // 2, LANES), BF16)
        sent = call(
            lambda *r: row_kernel((tiles, strips, height, width, strip), dest, *r),
            [rate, *own, *other, *hots, log_table, proj_row, proj_row2, skip],
            [block] * strips,
            [(tiles * cells, LANES)] * 5 + [((width + 2) * height, LANES)] * 2,
            "rows",
        )
        got = exchange(sent)
        got2 = [across(b) for b in got]
        back = jax.ShapeDtypeStruct((height * strip * 3 // 2, LANES), BF16)
        pitch = total + 2 * SUB
        sent = call(
            lambda *r: column_kernel((strips, height, strip), dest, *r),
            [rate, *got, *got2, hot_strip, log_table, proj_col, proj_col2, conv_w, conv_w2, bias, bias2, skip],
            [back] * strips,
            [(count * pitch, LANES)] * 2 + [(total * strip, LANES)] * 7,
            "columns",
        )
        got = exchange(sent)
        return call(
            lambda *r: gate_kernel((strips, height, width, strip), dest, *r),
            [*got, gate],
            jax.ShapeDtypeStruct(features.shape, BF16),
            [(cells, LANES)] * 2,
            "gate",
        )

    return shards


def solution(mesh):
    placed = (
        P(("slides", "rows"), "cols", "chan"),
        P(("slides", "rows"), "cols", "chan"),
        P(("slides", "rows"), "cols"),
        P(None, "chan"),
        P(),
        P("chan", None),
        P("chan", None),
        P(None, None, "chan"),
        P("chan"),
        P("chan"),
    )
    return jax.shard_map(
        make_shards(mesh.shape["rows"], mesh.shape["cols"]),
        mesh=mesh,
        in_specs=placed,
        out_specs=P(("slides", "rows"), "cols", "chan"),
        check_vma=False,
    )
```

time: 403 us -> 83 us (0.21)
  local copies, waits for them, and re-layouts: 178 us -> 3.87 us
  other arithmetic: 104 us -> 1.14 us
  Pallas kernels: 0 us -> 42.3 us
  blocking collectives: 33.5 us -> 0 us
  waiting for transfers between devices: 35.4 us -> 16.7 us
  between operations: 13.7 us -> 0.22 us
  loops' own time: 10.1 us -> 0 us
  matrix products: 4.34 us -> 0 us
    slice x468 -> x0, local copies, waits for them, and re-layouts: 66 us -> none  [the longest x464 66 us: one_state(): lax.associative_scan(combine_pair, (log_decays * state_scale, drive_col *...]
    pallas_call x0 -> x3, Pallas kernels: none -> 42.3 us  [call(): pl.pallas_call(kernel, out_shape=outs, in_specs=[smem() if a.ndim == 1 el...]
    mul x32 -> x0, other arithmetic: 41.8 us -> none  [one_state(): log_decays * state_scale]
    pad x288 -> x0, local copies, waits for them, and re-layouts: 36.8 us -> none  [one_state(): lax.associative_scan(combine_pair, (log_decays * state_scale, drive_col *...]
    dynamic_slice x32 -> x0, local copies, waits for them, and re-layouts: 30.6 us -> none  [tile_states(): return (log_sums, lax.map(one_state, (state_rate, drive_cols)))]
    dynamic_update_slice x32 -> x0, other arithmetic: 28.1 us -> none  [tile_states(): return (log_sums, lax.map(one_state, (state_rate, drive_cols)))]
    mul x34 -> x0, local copies, waits for them, and re-layouts: 23.3 us -> none  [the longest x32 23.3 us: one_state(): drive_col * values]
    psum x2 -> x0, waiting for transfers between devices: 22.7 us -> none  [the longest x1 17.2 us: column_coeffs(): lax.psum(jnp.dot(middle, proj_col, preferred_element_type=jnp.float32), '...]
  transfers between devices with their start and end apart: 8 -> 21, of which waited for: 6 -> 10; matrix products, arithmetic and copies ran while one was open for 50% -> 3% of each run, Pallas kernels for 0% -> 0%
where the time goes in v1:
time: 83 us; the launch traced here: 82.7 us
  Pallas kernels  42.3 us (51%)
  starting transfers between devices  18.5 us (22%)
  waiting for transfers between devices  16.7 us (20%)
  local copies, waits for them, and re-layouts  3.87 us (5%)
  other arithmetic  1.14 us (1%)
    pallas_call x3, Pallas kernels, call(): pl.pallas_call(kernel, out_shape=outs, in_specs=[smem() if a.ndim == 1 el...  42.3 us
    ppermute x9, starting transfers between devices, exchange(): lax.ppermute(blocks[d], axis, [(i, i ^ d) for i in range(strips)])  14.2 us
    ppermute x9, waiting for transfers between devices, exchange(): lax.ppermute(blocks[d], axis, [(i, i ^ d) for i in range(strips)])  11.3 us
    unnamed x51, local copies, waits for them, and re-layouts  2.95 us
    ppermute x10, waiting for transfers between devices, across(): return lax.ppermute(v, 'chan', swap)  2.79 us
    ppermute x1, waiting for transfers between devices, shards(): lax.ppermute(features, 'cols', pairs)  2.6 us
    ppermute x10, starting transfers between devices, across(): return lax.ppermute(v, 'chan', swap)  2.27 us
    ppermute x1, starting transfers between devices, shards(): lax.ppermute(decay_idx, 'cols', pairs)  1.71 us
  transfers between devices with their start and end apart: 21, of which 10 were waited for; matrix products, arithmetic and copies ran while one was open for 3% of the time, Pallas kernels for 0%

profile of v1, /device:TPU:0, one launch (start us, length us, event | category | flops | bytes accessed | tf_op | source)
XLA Modules:
  0.0 82.7 jit_solution(5500969356787892639)
XLA Ops:
  0.0 3.1 %collective-permute-start.12 = (s32[16,32]{1,0:T(8,128)}, s32[16,32]{1,0:T(8,128)S(1)}, u32[]{:S(2)}, u32[]{:S(2)}) collective-permute-start(s32[16,32]{1,0:T(8,128)} %param.12), channel_id=1, source_target_pairs={{0,4},{4,0},{8,12},{12,8},{1,5},{5,1},{9,13},{13,9},{2,6},{6,2},{1... | collective-permute-start | bytes 6152 | tf_op jit(solution)/shard_map/ppermute | solution.py:326
  3.1 2.6 %collective-permute-start.13 = (s32[16,32]{1,0:T(8,128)}, s32[16,32]{1,0:T(8,128)S(1)}, u32[]{:S(2)}, u32[]{:S(2)}) collective-permute-start(s32[16,32]{1,0:T(8,128)} %param.12), channel_id=1, source_target_pairs={{0,8},{4,12},{8,0},{12,4},{1,9},{5,13},{9,1},{13,5},{2,10},{6,14},... | collective-permute-start | bytes 6152 | tf_op jit(solution)/shard_map/ppermute | solution.py:326
  5.6 1.7 %collective-permute-start.3 = (s32[16,32]{1,0:T(8,128)}, s32[16,32]{1,0:T(8,128)S(1)}, u32[]{:S(2)}, u32[]{:S(2)}) collective-permute-start(s32[16,32]{1,0:T(8,128)} %param.12), channel_id=1, source_target_pairs={{0,2},{2,0},{1,3},{3,1},{4,6},{6,4},{5,7},{7,5},{8,10},{10,8},{9,1... | collective-permute-start | bytes 6152 | tf_op jit(solution)/shard_map/ppermute | solution.py:343
  7.4 0.3 collective-permute-start
  7.7 0.1 copy.27
  7.8 0.1 copy.23
  7.9 0.1 eq.75
  7.9 0.6 copy-done.18
  8.5 0.1 copy.26.r_8_
  8.7 0.1 copy.28
  8.8 0.5 collective-permute-start.4
  9.3 0.1 copy.29
  9.4 1.9 %collective-permute-done.14 = s32[16,32]{1,0:T(8,128)S(1)} collective-permute-done((s32[16,32]{1,0:T(8,128)}, s32[16,32]{1,0:T(8,128)S(1)}, u32[]{:S(2)}, u32[]{:S(2)}) %collective-permute-start.14) | collective-permute-done | bytes 2080 | tf_op jit(solution)/shard_map/ppermute | solution.py:326
  11.3 0.1 copy.30
  11.7 0.1 select_add_fusion
  11.8 0.1 add.53
  11.9 0.1 copy.24
  12.0 0.1 eq.79
  12.0 2.6 %collective-permute-done.r_2_ = bf16[16,32,192]{2,1,0:T(8,128)(2,1)S(1)} collective-permute-done((bf16[16,32,192]{2,1,0:T(8,128)(2,1)}, bf16[16,32,192]{2,1,0:T(8,128)(2,1)S(1)}, u32[]{:S(2)}, u32[]{:S(2)}) %collective-permute-start) | collective-permute-done | bytes 196640 | tf_op jit(solution)/shard_map/ppermute | solution.py:342
  14.6 1.0 %compare_convert_fusion = (bf16[512,48]{1,0:T(8,128)(2,1)}, bf16[512,48]{1,0:T(8,128)(2,1)}, bf16[512,48]{1,0:T(8,128)(2,1)}) fusion(s32[48]{0:T(128)S(1)} %and_select_fusion, s32[512]{0:T(512)S(1)} %add.53, s32[512]{0:T(512)S(1)} %eq.79, s32[512]{0:T(512)S(1)} %eq.75), kind=kLoop, calls=%fused_computation | loop fusion | flops 147456 | bytes 153792 | tf_op jit(solution)/shard_map/convert_element_type | solution.py:313
  15.7 0.5 collective-permute-done.2.r_4_
  16.2 0.1 copy-done.12
  16.3 0.1 copy-done.1
  16.4 0.5 copy-done.2
  16.9 22.8 %rows.1 = (bf16[240,128]{1,0:T(8,128)(2,1)}, bf16[240,128]{1,0:T(8,128)(2,1)}, bf16[240,128]{1,0:T(8,128)(2,1)}, bf16[240,128]{1,0:T(8,128)(2,1)}) custom-call(f32[16]{0:T(128)} %r_0_.3, bf16[16,32,192]{2,1,0:T(8,128)(2,1)} %r_1_.1, bf16[16,32,192]{2,1,0:T(8,128)(2,1)} %copy-done, bf16[16,32,192]{2,1,0:T(8,128)(2,1)} %copy-done.1, ...), custom_call_target="tpu_custom_call" | custom-call | tf_op jit(solution)/shard_map/rows/pallas_call | solution.py:301
  39.7 1.6 %collective-permute-start.6 = (bf16[240,128]{1,0:T(8,128)(2,1)}, bf16[240,128]{1,0:T(8,128)(2,1)S(1)}, u32[]{:S(2)}, u32[]{:S(2)}) collective-permute-start(bf16[240,128]{1,0:T(8,128)(2,1)} %get-tuple-element.15), channel_id=1, source_target_pairs={{0,8},{4,12},{8,0},{12,4},{1,9},{5,13},{9,1},{13,5},{2,10},{6,14},... | collective-permute-start | bytes 184328 | tf_op jit(solution)/shard_map/ppermute | solution.py:326
  41.4 2.0 %collective-permute-start.7 = (bf16[240,128]{1,0:T(8,128)(2,1)}, bf16[240,128]{1,0:T(8,128)(2,1)S(1)}, u32[]{:S(2)}, u32[]{:S(2)}) collective-permute-start(bf16[240,128]{1,0:T(8,128)(2,1)} %get-tuple-element.16), channel_id=1, source_target_pairs={{0,12},{4,8},{8,4},{12,0},{1,13},{5,9},{9,5},{13,1},{2,14},{6,10},... | collective-permute-start | bytes 184328 | tf_op jit(solution)/shard_map/ppermute | solution.py:326
  43.3 0.5 collective-permute-start.5
  43.8 4.3 %collective-permute-done.6.r_3_ = bf16[240,128]{1,0:T(8,128)(2,1)S(1)} collective-permute-done((bf16[240,128]{1,0:T(8,128)(2,1)}, bf16[240,128]{1,0:T(8,128)(2,1)S(1)}, u32[]{:S(2)}, u32[]{:S(2)}) %collective-permute-start.6) | collective-permute-done | bytes 61472 | tf_op jit(solution)/shard_map/ppermute | solution.py:326
  48.2 0.5 collective-permute-start.11
  48.7 0.3 collective-permute-done.5.r_2_
  49.0 0.5 collective-permute-start.17
  49.5 0.8 collective-permute-done.17.r_16_
  50.3 0.3 collective-permute-start.16
  50.7 0.1 copy.36.r_11_
  50.8 0.1 copy-done.23
  50.9 0.6 collective-permute-done.16.r_14_
  51.5 0.3 collective-permute-start.15
  51.9 0.9 %collective-permute-done.15.r_12_ = bf16[192,32]{1,0:T(8,128)(2,1)S(1)} collective-permute-done((bf16[192,32]{1,0:T(8,128)(2,1)S(1)}, bf16[192,32]{1,0:T(8,128)(2,1)S(1)}, u32[]{:S(2)}, u32[]{:S(2)}) %collective-permute-start.15) | collective-permute-done | bytes 12320 | tf_op jit(solution)/shard_map/ppermute | solution.py:332
  52.9 0.5 copy-done.16
  53.5 17.5 %columns.1 = (bf16[192,128]{1,0:T(8,128)(2,1)}, bf16[192,128]{1,0:T(8,128)(2,1)}, bf16[192,128]{1,0:T(8,128)(2,1)}, bf16[192,128]{1,0:T(8,128)(2,1)}) custom-call(f32[16]{0:T(128)} %r_0_.3, bf16[240,128]{1,0:T(8,128)(2,1)} %get-tuple-element.13.r_1_, bf16[240,128]{1,0:T(8,128)(2,1)} %copy-done.7, bf16[240,128]{1,0:T(8,128)(2,1)} %copy-done.5, ...), custom_call_target="tpu_custom_call" | custom-call | tf_op jit(solution)/shard_map/columns/pallas_call | solution.py:301
  70.9 1.0 %collective-permute-start.18 = (bf16[192,128]{1,0:T(8,128)(2,1)}, bf16[192,128]{1,0:T(8,128)(2,1)S(1)}, u32[]{:S(2)}, u32[]{:S(2)}) collective-permute-start(bf16[192,128]{1,0:T(8,128)(2,1)} %get-tuple-element.18), channel_id=1, source_target_pairs={{0,4},{4,0},{8,12},{12,8},{1,5},{5,1},{9,13},{13,9},{2,6},{6,2},{1... | collective-permute-start | bytes 147464 | tf_op jit(solution)/shard_map/ppermute | solution.py:326
  71.9 2.1 %collective-permute-start.19 = (bf16[192,128]{1,0:T(8,128)(2,1)}, bf16[192,128]{1,0:T(8,128)(2,1)S(1)}, u32[]{:S(2)}, u32[]{:S(2)}) collective-permute-start(bf16[192,128]{1,0:T(8,128)(2,1)} %get-tuple-element.19), channel_id=1, source_target_pairs={{0,8},{4,12},{8,0},{12,4},{1,9},{5,13},{9,1},{13,5},{2,10},{6,14},... | collective-permute-start | bytes 147464 | tf_op jit(solution)/shard_map/ppermute | solution.py:326
  74.0 1.4 %collective-permute-start.20 = (bf16[192,128]{1,0:T(8,128)(2,1)}, bf16[192,128]{1,0:T(8,128)(2,1)S(1)}, u32[]{:S(2)}, u32[]{:S(2)}) collective-permute-start(bf16[192,128]{1,0:T(8,128)(2,1)} %get-tuple-element.20), channel_id=1, source_target_pairs={{0,12},{4,8},{8,4},{12,0},{1,13},{5,9},{9,5},{13,1},{2,14},{6,10},... | collective-permute-start | bytes 147464 | tf_op jit(solution)/shard_map/ppermute | solution.py:326
  75.4 3.0 %collective-permute-done.19.r_2_ = bf16[192,128]{1,0:T(8,128)(2,1)S(1)} collective-permute-done((bf16[192,128]{1,0:T(8,128)(2,1)}, bf16[192,128]{1,0:T(8,128)(2,1)S(1)}, u32[]{:S(2)}, u32[]{:S(2)}) %collective-permute-start.19) | collective-permute-done | bytes 49184 | tf_op jit(solution)/shard_map/ppermute | solution.py:326
  78.3 1.8 %collective-permute-done.20.r_3_ = bf16[192,128]{1,0:T(8,128)(2,1)S(1)} collective-permute-done((bf16[192,128]{1,0:T(8,128)(2,1)}, bf16[192,128]{1,0:T(8,128)(2,1)S(1)}, u32[]{:S(2)}, u32[]{:S(2)}) %collective-permute-start.20) | collective-permute-done | bytes 49184 | tf_op jit(solution)/shard_map/ppermute | solution.py:326
  80.1 0.6 copy-done.15
  80.7 2.0 %gate.1 = bf16[16,32,192]{2,1,0:T(8,128)(2,1)} custom-call(bf16[192,128]{1,0:T(8,128)(2,1)} %get-tuple-element.17.r_0_, bf16[192,128]{1,0:T(8,128)(2,1)} %copy-done.13, bf16[192,128]{1,0:T(8,128)(2,1)} %copy-done.14, bf16[192,128]{1,0:T(8,128)(2,1)} %copy-done.15, bf16[16,32,192]{2,1,0:T(8,128)(2,1)} %r_4_.1), custom_call_target="tpu_custom_call" | custom-call | tf_op jit(solution)/shard_map/gate/pallas_call | solution.py:301
  (67 shorter events, 0.6 us)
Async XLA Ops:
  0.0 7.7 %copy-start.17 = (s32[16,32]{1,0:T(8,128)S(1)}, s32[16,32]{1,0:T(8,128)}, u32[]{:S(2)}) copy-start(s32[16,32]{1,0:T(8,128)} %param.12) | copy-start | bytes 6148
  0.0 8.6 %collective-permute-start.12 = (s32[16,32]{1,0:T(8,128)}, s32[16,32]{1,0:T(8,128)S(1)}, u32[]{:S(2)}, u32[]{:S(2)}) collective-permute-start(s32[16,32]{1,0:T(8,128)} %param.12), channel_id=1, source_target_pairs={{0,4},{4,0},{8,12},{12,8},{1,5},{5,1},{9,13},{13,9},{2,6},{6,2},{1... | collective-permute-start | bytes 6152 | tf_op jit(solution)/shard_map/ppermute | solution.py:326
  3.1 5.7 %collective-permute-start.13 = (s32[16,32]{1,0:T(8,128)}, s32[16,32]{1,0:T(8,128)S(1)}, u32[]{:S(2)}, u32[]{:S(2)}) collective-permute-start(s32[16,32]{1,0:T(8,128)} %param.12), channel_id=1, source_target_pairs={{0,8},{4,12},{8,0},{12,4},{1,9},{5,13},{9,1},{13,5},{2,10},{6,14},... | collective-permute-start | bytes 6152 | tf_op jit(solution)/shard_map/ppermute | solution.py:326
  5.6 5.7 %collective-permute-start.14 = (s32[16,32]{1,0:T(8,128)}, s32[16,32]{1,0:T(8,128)S(1)}, u32[]{:S(2)}, u32[]{:S(2)}) collective-permute-start(s32[16,32]{1,0:T(8,128)} %param.12), channel_id=1, source_target_pairs={{0,12},{4,8},{8,4},{12,0},{1,13},{5,9},{9,5},{13,1},{2,14},{6,10},... | collective-permute-start | bytes 6152 | tf_op jit(solution)/shard_map/ppermute | solution.py:326
  5.6 6.2 %collective-permute-start.3 = (s32[16,32]{1,0:T(8,128)}, s32[16,32]{1,0:T(8,128)S(1)}, u32[]{:S(2)}, u32[]{:S(2)}) collective-permute-start(s32[16,32]{1,0:T(8,128)} %param.12), channel_id=1, source_target_pairs={{0,2},{2,0},{1,3},{3,1},{4,6},{6,4},{5,7},{7,5},{8,10},{10,8},{9,1... | collective-permute-start | bytes 6152 | tf_op jit(solution)/shard_map/ppermute | solution.py:343
  7.4 7.3 %collective-permute-start = (bf16[16,32,192]{2,1,0:T(8,128)(2,1)}, bf16[16,32,192]{2,1,0:T(8,128)(2,1)S(1)}, u32[]{:S(2)}, u32[]{:S(2)}) collective-permute-start(bf16[16,32,192]{2,1,0:T(8,128)(2,1)} %r_1_.1), channel_id=1, source_target_pairs={{0,2},{2,0},{1,3},{3,1},{4,6},{6,4},{5,7},{7,5},{8,10},{10,8},{9,1... | collective-permute-start | bytes 589832 | tf_op jit(solution)/shard_map/ppermute | solution.py:342
  7.8 0.7 copy-start.18
  8.6 2.8 %copy-start.3 = (bf16[192,32]{1,0:T(8,128)(2,1)}, bf16[192,32]{1,0:T(8,128)(2,1)S(1)}, u32[]{:S(2)}) copy-start(bf16[192,32]{1,0:T(8,128)(2,1)S(1)} %copy.26.r_8_) | copy-start | bytes 36868
  8.6 7.1 %collective-permute-start.1 = (bf16[16,32,192]{2,1,0:T(8,128)(2,1)}, bf16[16,32,192]{2,1,0:T(8,128)(2,1)S(1)}, u32[]{:S(2)}, u32[]{:S(2)}) collective-permute-start(bf16[16,32,192]{2,1,0:T(8,128)(2,1)} %r_1_.1), channel_id=1, source_target_pairs={{0,1},{1,0},{2,3},{3,2},{4,5},{5,4},{6,7},{7,6},{8,9},{9,8},{10,11... | collective-permute-start | bytes 589832 | tf_op jit(solution)/shard_map/ppermute | solution.py:332
  8.8 6.9 %collective-permute-start.4 = (bf16[192,32]{1,0:T(8,128)(2,1)S(1)}, bf16[192,32]{1,0:T(8,128)(2,1)S(1)}, u32[]{:S(2)}, u32[]{:S(2)}) collective-permute-start(bf16[192,32]{1,0:T(8,128)(2,1)S(1)} %copy.26.r_8_), channel_id=1, source_target_pairs={{0,1},{1,0},{2,3},{3,2},{4,5},{5,4},{6,7},{7,6},{8,9},{9,8},{10,11... | collective-permute-start | bytes 36872 | tf_op jit(solution)/shard_map/ppermute | solution.py:332
  14.6 1.5 %copy-start = (bf16[16,32,192]{2,1,0:T(8,128)(2,1)}, bf16[16,32,192]{2,1,0:T(8,128)(2,1)S(1)}, u32[]{:S(2)}) copy-start(bf16[16,32,192]{2,1,0:T(8,128)(2,1)S(1)} %collective-permute-done.r_2_) | copy-start | bytes 589828
  14.6 1.5 %collective-permute-start.2 = (bf16[16,32,192]{2,1,0:T(8,128)(2,1)S(1)}, bf16[16,32,192]{2,1,0:T(8,128)(2,1)S(1)}, u32[]{:S(2)}, u32[]{:S(2)}) collective-permute-start(bf16[16,32,192]{2,1,0:T(8,128)(2,1)S(1)} %collective-permute-done.r_2_), channel_id=1, source_target_pairs={{0,1},{1,0},{2,3},{3,2},{4,5},{5,4},{6,7},{7,6},{8,9},{9,8},{10,11... | collective-permute-start | bytes 589832 | tf_op jit(solution)/shard_map/ppermute | solution.py:332
  15.7 0.6 copy-start.12
  15.7 0.7 copy-start.1
  16.2 0.7 copy-start.2
  16.9 33.5 %copy-start.20 = (f32[3,3,192]{2,1,0:T(4,128)S(1)}, f32[3,3,192]{2,1,0:T(4,128)}, u32[]{:S(2)}) copy-start(f32[3,3,192]{2,1,0:T(4,128)} %r_13_.1) | copy-start | bytes 20740
  16.9 33.8 %copy-start.19 = (bf16[192,32]{0,1:T(8,128)(2,1)S(1)}, bf16[192,32]{0,1:T(8,128)(2,1)}, u32[]{:S(2)}) copy-start(bf16[192,32]{0,1:T(8,128)(2,1)} %param.16) | copy-start | bytes 36868
  39.7 8.5 %collective-permute-start.6 = (bf16[240,128]{1,0:T(8,128)(2,1)}, bf16[240,128]{1,0:T(8,128)(2,1)S(1)}, u32[]{:S(2)}, u32[]{:S(2)}) collective-permute-start(bf16[240,128]{1,0:T(8,128)(2,1)} %get-tuple-element.15), channel_id=1, source_target_pairs={{0,8},{4,12},{8,0},{12,4},{1,9},{5,13},{9,1},{13,5},{2,10},{6,14},... | collective-permute-start | bytes 184328 | tf_op jit(solution)/shard_map/ppermute | solution.py:326
  41.4 6.8 %collective-permute-start.7 = (bf16[240,128]{1,0:T(8,128)(2,1)}, bf16[240,128]{1,0:T(8,128)(2,1)S(1)}, u32[]{:S(2)}, u32[]{:S(2)}) collective-permute-start(bf16[240,128]{1,0:T(8,128)(2,1)} %get-tuple-element.16), channel_id=1, source_target_pairs={{0,12},{4,8},{8,4},{12,0},{1,13},{5,9},{9,5},{13,1},{2,14},{6,10},... | collective-permute-start | bytes 184328 | tf_op jit(solution)/shard_map/ppermute | solution.py:326
  43.3 5.7 %collective-permute-start.5 = (bf16[240,128]{1,0:T(8,128)(2,1)}, bf16[240,128]{1,0:T(8,128)(2,1)S(1)}, u32[]{:S(2)}, u32[]{:S(2)}) collective-permute-start(bf16[240,128]{1,0:T(8,128)(2,1)} %get-tuple-element.14), channel_id=1, source_target_pairs={{0,4},{4,0},{8,12},{12,8},{1,5},{5,1},{9,13},{13,9},{2,6},{6,2},{1... | collective-permute-start | bytes 184328 | tf_op jit(solution)/shard_map/ppermute | solution.py:326
  43.8 5.2 %copy-start.22 = (f32[192]{0:T(256)S(1)}, f32[192]{0:T(256)}, u32[]{:S(2)}) copy-start(f32[192]{0:T(256)} %param.18) | copy-start | bytes 2308
  43.8 8.9 %collective-permute-start.8 = (bf16[240,128]{1,0:T(8,128)(2,1)}, bf16[240,128]{1,0:T(8,128)(2,1)S(1)}, u32[]{:S(2)}, u32[]{:S(2)}) collective-permute-start(bf16[240,128]{1,0:T(8,128)(2,1)} %get-tuple-element.13.r_1_), channel_id=1, source_target_pairs={{0,1},{1,0},{2,3},{3,2},{4,5},{5,4},{6,7},{7,6},{8,9},{9,8},{10,11... | collective-permute-start | bytes 184328 | tf_op jit(solution)/shard_map/ppermute | solution.py:332
  48.2 4.6 %copy-start.5 = (bf16[240,128]{1,0:T(8,128)(2,1)}, bf16[240,128]{1,0:T(8,128)(2,1)S(1)}, u32[]{:S(2)}) copy-start(bf16[240,128]{1,0:T(8,128)(2,1)S(1)} %collective-permute-done.6.r_3_) | copy-start | bytes 184324
  48.2 4.6 %collective-permute-start.10 = (bf16[240,128]{1,0:T(8,128)(2,1)S(1)}, bf16[240,128]{1,0:T(8,128)(2,1)S(1)}, u32[]{:S(2)}, u32[]{:S(2)}) collective-permute-start(bf16[240,128]{1,0:T(8,128)(2,1)S(1)} %collective-permute-done.6.r_3_), channel_id=1, source_target_pairs={{0,1},{1,0},{2,3},{3,2},{4,5},{5,4},{6,7},{7,6},{8,9},{9,8},{10,11... | collective-permute-start | bytes 184328 | tf_op jit(solution)/shard_map/ppermute | solution.py:332
  48.2 4.6 %copy-start.6 = (bf16[240,128]{1,0:T(8,128)(2,1)}, bf16[240,128]{1,0:T(8,128)(2,1)S(1)}, u32[]{:S(2)}) copy-start(bf16[240,128]{1,0:T(8,128)(2,1)S(1)} %collective-permute-done.7.r_4_) | copy-start | bytes 184324
  48.2 4.6 %collective-permute-start.11 = (bf16[240,128]{1,0:T(8,128)(2,1)S(1)}, bf16[240,128]{1,0:T(8,128)(2,1)S(1)}, u32[]{:S(2)}, u32[]{:S(2)}) collective-permute-start(bf16[240,128]{1,0:T(8,128)(2,1)S(1)} %collective-permute-done.7.r_4_), channel_id=1, source_target_pairs={{0,1},{1,0},{2,3},{3,2},{4,5},{5,4},{6,7},{7,6},{8,9},{9,8},{10,11... | collective-permute-start | bytes 184328 | tf_op jit(solution)/shard_map/ppermute | solution.py:332
  49.0 3.8 %copy-start.7 = (bf16[240,128]{1,0:T(8,128)(2,1)}, bf16[240,128]{1,0:T(8,128)(2,1)S(1)}, u32[]{:S(2)}) copy-start(bf16[240,128]{1,0:T(8,128)(2,1)S(1)} %collective-permute-done.5.r_2_) | copy-start | bytes 184324
  49.0 3.8 %collective-permute-start.9 = (bf16[240,128]{1,0:T(8,128)(2,1)S(1)}, bf16[240,128]{1,0:T(8,128)(2,1)S(1)}, u32[]{:S(2)}, u32[]{:S(2)}) collective-permute-start(bf16[240,128]{1,0:T(8,128)(2,1)S(1)} %collective-permute-done.5.r_2_), channel_id=1, source_target_pairs={{0,1},{1,0},{2,3},{3,2},{4,5},{5,4},{6,7},{7,6},{8,9},{9,8},{10,11... | collective-permute-start | bytes 184328 | tf_op jit(solution)/shard_map/ppermute | solution.py:332
  49.0 1.3 %collective-permute-start.17 = (f32[1,192]{1,0:T(1,128)S(1)}, f32[1,192]{1,0:T(1,128)S(1)}, u32[]{:S(2)}, u32[]{:S(2)}) collective-permute-start(f32[1,192]{1,0:T(1,128)S(1)} %bitcast.25), channel_id=1, source_target_pairs={{0,1},{1,0},{2,3},{3,2},{4,5},{5,4},{6,7},{7,6},{8,9},{9,8},{10,11... | collective-permute-start | bytes 2312 | tf_op jit(solution)/shard_map/ppermute | solution.py:332
  50.3 0.6 copy-start.23
  50.3 1.2 %collective-permute-start.16 = (f32[3,3,192]{2,1,0:T(4,128)S(1)}, f32[3,3,192]{2,1,0:T(4,128)S(1)}, u32[]{:S(2)}, u32[]{:S(2)}) collective-permute-start(f32[3,3,192]{2,1,0:T(4,128)S(1)} %copy-done.20), channel_id=1, source_target_pairs={{0,1},{1,0},{2,3},{3,2},{4,5},{5,4},{6,7},{7,6},{8,9},{9,8},{10,11... | collective-permute-start | bytes 20744 | tf_op jit(solution)/shard_map/ppermute | solution.py:332
  50.9 1.9 %copy-start.4 = (bf16[192,32]{1,0:T(8,128)(2,1)}, bf16[192,32]{1,0:T(8,128)(2,1)S(1)}, u32[]{:S(2)}) copy-start(bf16[192,32]{1,0:T(8,128)(2,1)S(1)} %copy.36.r_11_) | copy-start | bytes 36868
  51.5 1.3 %copy-start.21 = (f32[3,3,192]{2,1,0:T(4,128)}, f32[3,3,192]{2,1,0:T(4,128)S(1)}, u32[]{:S(2)}) copy-start(f32[3,3,192]{2,1,0:T(4,128)S(1)} %collective-permute-done.16.r_14_) | copy-start | bytes 20740
  51.5 1.2 %collective-permute-start.15 = (bf16[192,32]{1,0:T(8,128)(2,1)S(1)}, bf16[192,32]{1,0:T(8,128)(2,1)S(1)}, u32[]{:S(2)}, u32[]{:S(2)}) collective-permute-start(bf16[192,32]{1,0:T(8,128)(2,1)S(1)} %copy.36.r_11_), channel_id=1, source_target_pairs={{0,1},{1,0},{2,3},{3,2},{4,5},{5,4},{6,7},{7,6},{8,9},{9,8},{10,11... | collective-permute-start | bytes 36872 | tf_op jit(solution)/shard_map/ppermute | solution.py:332
  52.8 0.6 copy-start.16
  52.8 0.6 copy-start.8
  52.8 0.7 copy-start.9
  52.8 0.7 copy-start.10
  52.8 0.7 copy-start.11
  70.9 4.4 %collective-permute-start.18 = (bf16[192,128]{1,0:T(8,128)(2,1)}, bf16[192,128]{1,0:T(8,128)(2,1)S(1)}, u32[]{:S(2)}, u32[]{:S(2)}) collective-permute-start(bf16[192,128]{1,0:T(8,128)(2,1)} %get-tuple-element.18), channel_id=1, source_target_pairs={{0,4},{4,0},{8,12},{12,8},{1,5},{5,1},{9,13},{13,9},{2,6},{6,2},{1... | collective-permute-start | bytes 147464 | tf_op jit(solution)/shard_map/ppermute | solution.py:326
  71.9 6.4 %collective-permute-start.19 = (bf16[192,128]{1,0:T(8,128)(2,1)}, bf16[192,128]{1,0:T(8,128)(2,1)S(1)}, u32[]{:S(2)}, u32[]{:S(2)}) collective-permute-start(bf16[192,128]{1,0:T(8,128)(2,1)} %get-tuple-element.19), channel_id=1, source_target_pairs={{0,8},{4,12},{8,0},{12,4},{1,9},{5,13},{9,1},{13,5},{2,10},{6,14},... | collective-permute-start | bytes 147464 | tf_op jit(solution)/shard_map/ppermute | solution.py:326
  74.0 6.1 %collective-permute-start.20 = (bf16[192,128]{1,0:T(8,128)(2,1)}, bf16[192,128]{1,0:T(8,128)(2,1)S(1)}, u32[]{:S(2)}, u32[]{:S(2)}) collective-permute-start(bf16[192,128]{1,0:T(8,128)(2,1)} %get-tuple-element.20), channel_id=1, source_target_pairs={{0,12},{4,8},{8,4},{12,0},{1,13},{5,9},{9,5},{13,1},{2,14},{6,10},... | collective-permute-start | bytes 147464 | tf_op jit(solution)/shard_map/ppermute | solution.py:326
  75.4 4.7 %copy-start.13 = (bf16[192,128]{1,0:T(8,128)(2,1)}, bf16[192,128]{1,0:T(8,128)(2,1)S(1)}, u32[]{:S(2)}) copy-start(bf16[192,128]{1,0:T(8,128)(2,1)S(1)} %collective-permute-done.18.r_1_) | copy-start | bytes 147460
  78.3 1.8 %copy-start.14 = (bf16[192,128]{1,0:T(8,128)(2,1)}, bf16[192,128]{1,0:T(8,128)(2,1)S(1)}, u32[]{:S(2)}) copy-start(bf16[192,128]{1,0:T(8,128)(2,1)S(1)} %collective-permute-done.19.r_2_) | copy-start | bytes 147460
  80.1 0.6 copy-start.15

commit v2 on v1

--- a/solution.py
+++ b/solution.py
@@ -5,8 +5,10 @@
 from jax.experimental.pallas import tpu as pltpu
 from jax.sharding import PartitionSpec as P
 
+
 LANES = 128
 SUB = 8
+UNROLL = 4
 LOG2E = 1.4426950408889634
 F32 = jnp.float32
 BF16 = jnp.bfloat16
@@ -37,44 +39,85 @@
     return jnp.dot(a, b, preferred_element_type=F32)
 
 
-def pair_rates(rate_ref, rows):
-    half = low_half((rows, LANES))
+def fill_rates(rate_ref, rates):
+    half = low_half((SUB, LANES))
     states = rate_ref.shape[0]
-    return [jnp.where(half, rate_ref[2 * j], rate_ref[2 * j + 1]) for j in range(states // 2)]
-
-
-def advance(carry, xa, xb, la, lb, coeff, rate_ref, rates_b, wanted):
-    states = rate_ref.shape[0]
+    for s in range(states):
+        rates[s * SUB : (s + 1) * SUB, :] = jnp.full((SUB, LANES), rate_ref[s], F32)
+    for j in range(states // 2):
+        at = (states + j) * SUB
+        rates[at : at + SUB, :] = jnp.where(half, rate_ref[2 * j], rate_ref[2 * j + 1])
+
+
+def steps(count, step, carry):
+    first = count % UNROLL
+    for i in range(first):
+        carry = step(i, carry)
+
+    def body(i, carry):
+        for k in range(UNROLL):
+            carry = step(first + i * UNROLL + k, carry)
+        return carry
+
+    return lax.fori_loop(0, count // UNROLL, body, carry)
+
+
+def pitch_of(rows):
+    return rows + SUB // 2 if rows % SUB == 0 else rows
+
+
+def advance(carry, xa, xb, la, lb, drive, out, rates):
+    states = rates.shape[0] // SUB * 2 // 3
     shape = xa.shape
     half = low_half(shape)
-
-    def spread(col):
-        return jnp.broadcast_to(coeff[:, col : col + 1], shape)
-
-    drive = [spread(s) for s in range(states)]
-    out = [spread(states + s) for s in range(states)] if wanted else None
+    drive = [drive(s) for s in range(states)]
+    out = None if out is None else [out(s) for s in range(states)]
     new, ya, yb = [], [], []
     for s in range(states):
-        st = jnp.exp2(la * rate_ref[s]) * carry[s] + drive[s] * xa
+        st = jnp.exp2(la * rates[s * SUB : s * SUB + shape[0], :]) * carry[s] + drive[s] * xa
         new.append(st)
-        if wanted:
+        if out:
             ya.append(out[s] * st)
     for j in range(states // 2):
         b = jnp.where(half, drive[2 * j], drive[2 * j + 1])
-        st = jnp.exp2(lb * rates_b[j]) * carry[states + j] + b * xb
+        at = (states + j) * SUB
+        st = jnp.exp2(lb * rates[at : at + shape[0], :]) * carry[states + j] + b * xb
         new.append(st)
-        if wanted:
+        if out:
             yb.append(jnp.where(half, out[2 * j], out[2 * j + 1]) * st)
-    if not wanted:
-        return tuple(new), None, None
 
     def tree(v):
         while len(v) > 1:
             v = [v[i] + v[i + 1] for i in range(0, len(v) - 1, 2)] + v[len(v) & ~1 :]
-        return v[0]
+        return v[0] if v else None
 
     yb = tree(yb)
-    return tuple(new), tree(ya), yb + pltpu.roll(yb, LANES // 2, 1)
+    return tuple(new), tree(ya), None if yb is None else yb + pltpu.roll(yb, LANES // 2, 1)
+
+
+def spread(coeff, column):
+    return jnp.broadcast_to(coeff[:, column : column + 1], (coeff.shape[0], LANES))
+
+
+def spread_all(cf_ref, count, matrix, permute):
+    for (column, to, rows), (column2, to2, rows2) in zip(matrix[::2], matrix[1::2]):
+        v = cf_ref[:rows, : 3 * count]
+        lane = lax.broadcasted_iota(jnp.int32, v.shape, 1)
+        hi = v.astype(BF16).astype(F32)
+        mid = (v - hi).astype(BF16).astype(F32)
+        parts = jnp.where(lane < count, hi, jnp.where(lane < 2 * count, mid, v - hi - mid)).astype(BF16)
+        shape = (3 * count, 2 * LANES)
+        source = lax.broadcasted_iota(jnp.int32, shape, 0) % count
+        wanted = jnp.where(lax.broadcasted_iota(jnp.int32, shape, 1) < LANES, column, column2)
+        wide = dot(parts, (source == wanted).astype(BF16))
+        to[...] = wide[:, :LANES]
+        to2[...] = wide[:, LANES:]
+    for column, to, rows in permute:
+        to[...] = spread(cf_ref[:rows, :], column)
+
+
+def thrice(v):
+    return jnp.concatenate([v, v, v], axis=-1)
 
 
 def row_kernel(dims, dest, *refs):
@@ -84,41 +127,73 @@
     hots = refs[1 + 2 * tiles : 1 + 3 * tiles]
     table_ref, proj_ref, proj2_ref, skip_ref = refs[1 + 3 * tiles : 5 + 3 * tiles]
     outs = refs[5 + 3 * tiles : 5 + 3 * tiles + strips]
-    xa_ref, xb_ref, la_ref, lb_ref, cf_ref, ya_ref, yb_ref = refs[5 + 3 * tiles + strips :]
+    scratch = refs[5 + 3 * tiles + strips :]
+    raw, xa_ref, xb_ref, la_ref, lb_ref, cf_ref, drives, weights, ya_ref, yb_ref, rates = scratch[:3], *scratch[3:]
     states = rate_ref.shape[0]
     cells = height * width
+    pitch = pitch_of(width)
     col = lax.axis_index("cols")
     row = lax.axis_index("rows")
 
     ta, tb = tables(table_ref)
+    proj, proj2 = thrice(proj_ref[...]), thrice(proj2_ref[...])
     for d in range(tiles):
         x = own[d][...].reshape(cells, -1)
         part = pl.ds(d * cells, cells)
-        cf_ref[part, : 2 * states] = dot(x, proj_ref[...]) + dot(
-            other[d][...].reshape(cells, -1), proj2_ref[...]
-        )
+        coeff = dot(x, proj) + dot(other[d][...].reshape(cells, -1), proj2)
         xf = x.astype(F32)
-        xa_ref[part, :] = xf[:, :LANES]
-        xb_ref[part, :] = twice(xf[:, LANES:])
+        xa, xb = xf[:, :LANES], twice(xf[:, LANES:])
+        if 0 < d < tiles - 1:
+            there = (col >= d).astype(F32)
+            xa, xb = xa * there, xb * there
+        for h in range(height):
+            to, cut = pl.ds((d * height + h) * pitch, width), slice(h * width, (h + 1) * width)
+            raw[0][to, :] = xa[cut]
+            raw[1][to, :] = xb[cut]
+            raw[2][to, : 6 * states] = coeff[cut]
         hot = hots[d][...]
         la_ref[part, :] = dot(hot, ta)
         lb_ref[part, :] = dot(hot, tb)
 
-    rates_b = pair_rates(rate_ref, SUB)
+    fill_rates(rate_ref, rates)
+    for d in range(tiles):
+
+        def order(w, unused, d=d):
+            for g in range(height // SUB):
+                place = pl.ds((d * height + g * SUB) * pitch + w, SUB, stride=pitch)
+                to = pl.ds(pl.multiple_of(d * cells + w * height + g * SUB, SUB), SUB)
+                for old, new in zip(raw, (xa_ref, xb_ref, cf_ref)):
+                    new[to, :] = old[place, :]
+            return unused
+
+        steps(width, order, 0)
+    size = tiles * cells
+    every = [(s, drives.at[s * size : (s + 1) * size, :], size) for s in range(states)]
+    every += [(states + s, weights.at[s * cells : (s + 1) * cells, :], cells) for s in range(states)]
+    cut = states * 7 // 8 // 2 * 2
+    spread_all(cf_ref, 2 * states, every[:cut], every[cut:])
+
     skip = skip_ref[...]
     skip_a, skip_b = skip[:, :LANES], twice(skip[:, LANES:])
     last_left = (col >= tiles - 1).astype(F32)
 
     for g in range(height // SUB):
 
-        def step(carry, d, w, scale, wanted, g=g):
-            place = pl.ds(d * cells + g * SUB * width + w, SUB, stride=width)
-            ordered = pl.ds(pl.multiple_of(d * cells + w * height + g * SUB, SUB), SUB)
-            xa, xb = xa_ref[place, :], xb_ref[place, :]
-            if scale is not None:
-                xa, xb = xa * scale, xb * scale
+        def step(carry, d, w, wanted, g=g):
+            here = w * height + g * SUB
+            at = pl.ds(pl.multiple_of(d * cells + here, SUB), SUB)
+            xa, xb = xa_ref[at, :], xb_ref[at, :]
+
+            def drive(s):
+                return drives[pl.ds(pl.multiple_of((s * tiles + d) * cells + here, SUB), SUB), :]
+
+            def out(s):
+                if d:
+                    return spread(cf_ref[at, :], states + s)
+                return weights[pl.ds(pl.multiple_of(s * cells + here, SUB), SUB), :]
+
             carry, ya, yb = advance(
-                carry, xa, xb, la_ref[ordered, :], lb_ref[ordered, :], cf_ref[place, :], rate_ref, rates_b, wanted
+                carry, xa, xb, la_ref[at, :], lb_ref[at, :], drive, out if wanted else None, rates
             )
             if wanted:
                 ya, yb = ya + skip_a * xa, yb + skip_b * xb
@@ -131,23 +206,22 @@
 
         carry = tuple(jnp.zeros((SUB, LANES), F32) for _ in range(states + states // 2))
         for d in range(tiles - 1, 0, -1):
-            scale = (col >= d).astype(F32)
-            carry = lax.fori_loop(
-                0,
-                width - (d == 1),
-                lambda w, s, d=d, scale=scale: step(s, d, w, scale, False)[0],
-                carry,
-            )
-        carry, ya, yb = step(carry, 1, width - 1, (col >= 1).astype(F32), True)
+            carry = steps(width - (d == 1), lambda w, s, d=d: step(s, d, w, False)[0], carry)
+            if d == tiles - 1:
+                carry = tuple(v * last_left for v in carry)
+        carry, ya, yb = step(carry, 1, width - 1, True)
+        if tiles == 2:
+            carry = tuple(v * last_left for v in carry)
+            ya, yb = ya * last_left, yb * last_left
         put(0, ya, yb)
 
         def body(w, s):
-            s, ya, yb = step(s, 0, w, None, True)
+            s, ya, yb = step(s, 0, w, True)
             put(w + 1, ya, yb)
             return s
 
-        carry = lax.fori_loop(0, width, body, carry)
-        _, ya, yb = step(carry, tiles - 1, 0, None, True)
+        carry = steps(width, body, carry)
+        _, ya, yb = step(carry, tiles - 1, 0, True)
         inside = 1.0 - last_left
         put(width + 1, ya * inside, yb * inside)
 
@@ -179,12 +253,16 @@
     conv_bs = refs[at + 6 : at + 8]
     skip_ref = refs[at + 8]
     outs = refs[at + 9 : at + 9 + strips]
-    ra_ref, rb_ref, ma_ref, mb_ref, la_ref, lb_ref, cf_ref, ya_ref, yb_ref = refs[at + 9 + strips :]
+    scratch = refs[at + 9 + strips :]
+    ra_ref, rb_ref, raw = *scratch[:2], scratch[2:5]
+    xa_ref, xb_ref, cf_ref, la_ref, lb_ref, ya_ref, yb_ref, drives, weights, rates = scratch[5:]
     states = rate_ref.shape[0]
     row = lax.axis_index("rows")
     total = strips * height
     pitch = total + 2 * SUB
+    leap = pitch_of(total)
     count = strip + 2
+    fill_rates(rate_ref, rates)
 
     ta, tb = tables(table_ref)
     hot = hot_ref[...]
@@ -196,7 +274,6 @@
             ref[pl.ds(k * pitch, SUB), :] = zero
             ref[pl.ds(k * pitch + SUB + total, SUB), :] = zero
 
-    coeff = None
     for side in (1, 0):
         for d in range(strips):
             base = pl.multiple_of(dest(row, d) * height, SUB) + SUB
@@ -211,51 +288,73 @@
         taps = conv_ws[side][...]
         bias = conv_bs[side][...]
         for src, dst, cut in (
-            (ra_ref, ma_ref, lambda v: v[..., :LANES]),
-            (rb_ref, mb_ref, lambda v: twice(v[..., LANES:])),
+            (ra_ref, raw[0], lambda v: v[..., :LANES]),
+            (rb_ref, raw[1], lambda v: twice(v[..., LANES:])),
         ):
-            weights, add = cut(taps), cut(bias)
-            spread = [[jnp.broadcast_to(weights[a, b][None, :], (SUB, LANES)) for b in range(3)] for a in range(3)]
+            cut_taps, add = cut(taps), cut(bias)
+            taps_wide = [[jnp.broadcast_to(cut_taps[a, b][None, :], (SUB, LANES)) for b in range(3)] for a in range(3)]
             start = jnp.broadcast_to(add, (SUB, LANES))
 
-            def conv(i, unused, src=src, dst=dst, spread=spread, start=start):
+            def conv(i, unused, src=src, dst=dst, taps_wide=taps_wide, start=start):
                 sums = [start] * strip
                 for k in range(count):
                     for a in range(3):
                         v = src[pl.ds(k * pitch + i * SUB + SUB - 1 + a, SUB), :]
                         for b in range(3):
                             if 0 <= k - b < strip:
-                                sums[k - b] = sums[k - b] + spread[a][b] * v
+                                sums[k - b] = sums[k - b] + taps_wide[a][b] * v
                 for k in range(strip):
                     v = sums[k] / (1.0 + jnp.exp(-sums[k]))
-                    dst[pl.ds(pl.multiple_of(k * total + i * SUB, SUB), SUB), :] = v.astype(BF16).astype(F32)
+                    dst[pl.ds(k * leap + i * SUB, SUB), :] = v.astype(BF16).astype(F32)
                 return unused
 
             lax.fori_loop(0, total // SUB, conv, 0)
-        proj = projs[side][...]
-        part = dot(ma_ref[...].astype(BF16), proj[:LANES]) + dot(
-            mb_ref[:, : LANES // 2].astype(BF16), proj[LANES:]
-        )
-        coeff = part if coeff is None else coeff + part
-    cf_ref[:, : 2 * states] = coeff
-
-    rates_b = pair_rates(rate_ref, strip)
+        proj = thrice(projs[side][...])
+        for k in range(strip):
+            at = pl.ds(k * leap, total)
+            part = dot(raw[0][at, :].astype(BF16), proj[:LANES]) + dot(
+                raw[1][at, : LANES // 2].astype(BF16), proj[LANES:]
+            )
+            raw[2][at, : 6 * states] = part if side else part + raw[2][at, : 6 * states]
+
     skip = skip_ref[...]
     skip_a, skip_b = skip[:, :LANES], twice(skip[:, LANES:])
 
+    def here(h, base=0):
+        at = base + h * strip
+        return pl.ds(at if strip % SUB else pl.multiple_of(at, SUB), strip)
+
+    def order(h, unused):
+        for old, new in zip(raw, (xa_ref, xb_ref, cf_ref)):
+            new[here(h), :] = old[pl.ds(h, strip, stride=leap), :]
+        return unused
+
+    steps(total, order, 0)
+    cells = total * strip
+    every = [(s, drives.at[s * cells : (s + 1) * cells, :], cells) for s in range(states)]
+    every += [(states + s, weights.at[s * cells : (s + 1) * cells, :], cells) for s in range(states)]
+    cut = states * 5 // 4 // 2 * 2
+    spread_all(cf_ref, 2 * states, every[:cut], every[cut:])
+
     def body(h, carry):
-        place = pl.ds(h, strip, stride=total)
-        ordered = pl.ds(h * strip if strip % SUB else pl.multiple_of(h * strip, SUB), strip)
-        xa, xb = ma_ref[place, :], mb_ref[place, :]
+        at = here(h)
+        xa, xb = xa_ref[at, :], xb_ref[at, :]
         carry, ya, yb = advance(
-            carry, xa, xb, la_ref[ordered, :], lb_ref[ordered, :], cf_ref[place, :], rate_ref, rates_b, True
+            carry,
+            xa,
+            xb,
+            la_ref[at, :],
+            lb_ref[at, :],
+            lambda s: drives[here(h, s * cells), :],
+            lambda s: weights[here(h, s * cells), :],
+            rates,
         )
-        ya_ref[ordered, :] = ya + skip_a * xa
-        yb_ref[ordered, :] = yb + skip_b * xb
+        ya_ref[at, :] = ya + skip_a * xa
+        yb_ref[at, :] = yb + skip_b * xb
         return carry
 
     zeros = tuple(jnp.zeros((strip, LANES), F32) for _ in range(states + states // 2))
-    lax.fori_loop(0, total, body, zeros)
+    steps(total, body, zeros)
 
     cells = height * strip
     for d in range(strips):
@@ -297,14 +396,13 @@
     return pl.BlockSpec(memory_space=pltpu.VMEM)
 
 
-def call(kernel, args, outs, scratch, name):
+def call(kernel, args, outs, scratch):
     return pl.pallas_call(
         kernel,
         out_shape=outs,
         in_specs=[smem() if a.ndim == 1 else vmem() for a in args],
         out_specs=jax.tree.map(lambda _: vmem(), outs),
         scratch_shapes=[pltpu.VMEM(s, F32) for s in scratch],
-        name=name,
     )(*args)
 
 
@@ -341,7 +439,8 @@
         rounds = [[(i, (i + d) % tiles) for i in range(tiles)] for d in range(1, tiles)]
         own = [features] + [lax.ppermute(features, "cols", pairs) for pairs in rounds]
         idx = [decay_idx] + [lax.ppermute(decay_idx, "cols", pairs) for pairs in rounds]
-        other = [across(f) for f in own]
+        other = [across(features)]
+        other += [across(f) for f in own[1:]]
         proj_row2, proj_col2 = across(proj_row), across(proj_col)
         conv_w2, bias2 = across(conv_w), across(bias)
         hots = [onehot(i.T, entries) for i in idx]
@@ -365,8 +464,11 @@
             lambda *r: row_kernel((tiles, strips, height, width, strip), dest, *r),
             [rate, *own, *other, *hots, log_table, proj_row, proj_row2, skip],
             [block] * strips,
-            [(tiles * cells, LANES)] * 5 + [((width + 2) * height, LANES)] * 2,
-            "rows",
+            [(tiles * height * pitch_of(width), LANES)] * 3
+            + [(tiles * cells, LANES)] * 5
+            + [(states * tiles * cells, LANES), (states * cells, LANES)]
+            + [((width + 2) * height, LANES)] * 2
+            + [(states * 3 // 2 * SUB, LANES)],
         )
         got = exchange(sent)
         got2 = [across(b) for b in got]
@@ -376,8 +478,11 @@
             lambda *r: column_kernel((strips, height, strip), dest, *r),
             [rate, *got, *got2, hot_strip, log_table, proj_col, proj_col2, conv_w, conv_w2, bias, bias2, skip],
             [back] * strips,
-            [(count * pitch, LANES)] * 2 + [(total * strip, LANES)] * 7,
-            "columns",
+            [(count * pitch, LANES)] * 2
+            + [(strip * pitch_of(total), LANES)] * 3
+            + [(total * strip, LANES)] * 7
+            + [(states * total * strip, LANES)] * 2
+            + [(states * 3 // 2 * SUB, LANES)],
         )
         got = exchange(sent)
         return call(
@@ -385,7 +490,6 @@
             [*got, gate],
             jax.ShapeDtypeStruct(features.shape, BF16),
             [(cells, LANES)] * 2,
-            "gate",
         )
 
     return shards
@@ -404,10 +508,8 @@
         P("chan"),
         P("chan"),
     )
+    shards = make_shards(mesh.shape["rows"], mesh.shape["cols"])
+
     return jax.shard_map(
-        make_shards(mesh.shape["rows"], mesh.shape["cols"]),
-        mesh=mesh,
-        in_specs=placed,
-        out_specs=P(("slides", "rows"), "cols", "chan"),
-        check_vma=False,
+        shards, mesh=mesh, in_specs=placed, out_specs=P(("slides", "rows"), "cols", "chan"), check_vma=False
     )

time: 83 us -> 58.7 us (0.71)
  Pallas kernels: 42.3 us -> 18.1 us
    pallas_call x3, Pallas kernels: 42.3 us -> 18.1 us  [call(): pl.pallas_call(kernel, out_shape=outs, in_specs=[smem() if a.ndim == 1 el...]
  transfers between devices with their start and end apart: 21 -> 21, of which waited for: 10 -> 10; matrix products, arithmetic and copies ran while one was open for 3% -> 4% of each run, Pallas kernels for 0% -> 0%
where the time goes in v2:
time: 58.7 us; the launch traced here: 58.5 us
  starting transfers between devices  18.5 us (32%)
  Pallas kernels  18.1 us (31%)
  waiting for transfers between devices  16.7 us (28%)
  local copies, waits for them, and re-layouts  3.87 us (7%)
  other arithmetic  1.14 us (2%)
    pallas_call x3, Pallas kernels, call(): pl.pallas_call(kernel, out_shape=outs, in_specs=[smem() if a.ndim == 1 el...  18.1 us
    ppermute x9, starting transfers between devices, exchange(): lax.ppermute(blocks[d], axis, [(i, i ^ d) for i in range(strips)])  14.2 us
    ppermute x9, waiting for transfers between devices, exchange(): lax.ppermute(blocks[d], axis, [(i, i ^ d) for i in range(strips)])  11.3 us
    unnamed x51, local copies, waits for them, and re-layouts  2.95 us
    ppermute x10, waiting for transfers between devices, across(): return lax.ppermute(v, 'chan', swap)  2.79 us
    ppermute x1, waiting for transfers between devices, shards(): lax.ppermute(features, 'cols', pairs)  2.6 us
    ppermute x10, starting transfers between devices, across(): return lax.ppermute(v, 'chan', swap)  2.27 us
    ppermute x1, starting transfers between devices, shards(): lax.ppermute(decay_idx, 'cols', pairs)  1.71 us
  transfers between devices with their start and end apart: 21, of which 10 were waited for; matrix products, arithmetic and copies ran while one was open for 4% of the time, Pallas kernels for 0%

profile of v2, /device:TPU:0, one launch (start us, length us, event | category | flops | bytes accessed | tf_op | source)
XLA Modules:
  0.0 58.5 jit_solution(7102565988783235840)
XLA Ops:
  0.0 3.1 %collective-permute-start.12 = (s32[16,32]{1,0:T(8,128)}, s32[16,32]{1,0:T(8,128)S(1)}, u32[]{:S(2)}, u32[]{:S(2)}) collective-permute-start(s32[16,32]{1,0:T(8,128)} %param.12), channel_id=1, source_target_pairs={{0,4},{4,0},{8,12},{12,8},{1,5},{5,1},{9,13},{13,9},{2,6},{6,2},{1... | collective-permute-start | bytes 6152 | tf_op jit(solution)/shard_map/ppermute | solution.py:424
  3.1 2.6 %collective-permute-start.13 = (s32[16,32]{1,0:T(8,128)}, s32[16,32]{1,0:T(8,128)S(1)}, u32[]{:S(2)}, u32[]{:S(2)}) collective-permute-start(s32[16,32]{1,0:T(8,128)} %param.12), channel_id=1, source_target_pairs={{0,8},{4,12},{8,0},{12,4},{1,9},{5,13},{9,1},{13,5},{2,10},{6,14},... | collective-permute-start | bytes 6152 | tf_op jit(solution)/shard_map/ppermute | solution.py:424
  5.6 1.7 %collective-permute-start.3 = (s32[16,32]{1,0:T(8,128)}, s32[16,32]{1,0:T(8,128)S(1)}, u32[]{:S(2)}, u32[]{:S(2)}) collective-permute-start(s32[16,32]{1,0:T(8,128)} %param.12), channel_id=1, source_target_pairs={{0,2},{2,0},{1,3},{3,1},{4,6},{6,4},{5,7},{7,5},{8,10},{10,8},{9,1... | collective-permute-start | bytes 6152 | tf_op jit(solution)/shard_map/ppermute | solution.py:441
  7.4 0.3 collective-permute-start
  7.7 0.1 copy.27
  7.8 0.1 copy.23
  7.9 0.1 eq.75
  7.9 0.6 copy-done.18
  8.5 0.1 copy.26.r_8_
  8.7 0.1 copy.28
  8.8 0.5 collective-permute-start.4
  9.3 0.1 copy.29
  9.4 1.9 %collective-permute-done.14 = s32[16,32]{1,0:T(8,128)S(1)} collective-permute-done((s32[16,32]{1,0:T(8,128)}, s32[16,32]{1,0:T(8,128)S(1)}, u32[]{:S(2)}, u32[]{:S(2)}) %collective-permute-start.14) | collective-permute-done | bytes 2080 | tf_op jit(solution)/shard_map/ppermute | solution.py:424
  11.3 0.1 copy.30
  11.7 0.1 select_add_fusion
  11.8 0.1 add.53
  11.9 0.1 copy.24
  12.0 0.1 eq.79
  12.0 2.6 %collective-permute-done.r_2_ = bf16[16,32,192]{2,1,0:T(8,128)(2,1)S(1)} collective-permute-done((bf16[16,32,192]{2,1,0:T(8,128)(2,1)}, bf16[16,32,192]{2,1,0:T(8,128)(2,1)S(1)}, u32[]{:S(2)}, u32[]{:S(2)}) %collective-permute-start) | collective-permute-done | bytes 196640 | tf_op jit(solution)/shard_map/ppermute | solution.py:440
  14.6 1.0 %compare_convert_fusion = (bf16[512,48]{1,0:T(8,128)(2,1)}, bf16[512,48]{1,0:T(8,128)(2,1)}, bf16[512,48]{1,0:T(8,128)(2,1)}) fusion(s32[48]{0:T(128)S(1)} %and_select_fusion, s32[512]{0:T(512)S(1)} %add.53, s32[512]{0:T(512)S(1)} %eq.79, s32[512]{0:T(512)S(1)} %eq.75), kind=kLoop, calls=%fused_computation | loop fusion | flops 147456 | bytes 153792 | tf_op jit(solution)/shard_map/convert_element_type | solution.py:411
  15.7 0.5 collective-permute-done.2.r_4_
  16.2 0.1 copy-done.12
  16.3 0.1 copy-done.1
  16.4 0.5 copy-done.2
  16.9 8.5 %shard_map.100 = (bf16[240,128]{1,0:T(8,128)(2,1)}, bf16[240,128]{1,0:T(8,128)(2,1)}, bf16[240,128]{1,0:T(8,128)(2,1)}, bf16[240,128]{1,0:T(8,128)(2,1)}) custom-call(f32[16]{0:T(128)} %r_0_.3, bf16[16,32,192]{2,1,0:T(8,128)(2,1)} %r_1_.1, bf16[16,32,192]{2,1,0:T(8,128)(2,1)} %copy-done, bf16[16,32,192]{2,1,0:T(8,128)(2,1)} %copy-done.1, ...), custom_call_target="tpu_custom_call" | custom-call | tf_op jit(solution)/shard_map/pallas_call | solution.py:400
  25.3 1.6 %collective-permute-start.6 = (bf16[240,128]{1,0:T(8,128)(2,1)}, bf16[240,128]{1,0:T(8,128)(2,1)S(1)}, u32[]{:S(2)}, u32[]{:S(2)}) collective-permute-start(bf16[240,128]{1,0:T(8,128)(2,1)} %get-tuple-element.15), channel_id=1, source_target_pairs={{0,8},{4,12},{8,0},{12,4},{1,9},{5,13},{9,1},{13,5},{2,10},{6,14},... | collective-permute-start | bytes 184328 | tf_op jit(solution)/shard_map/ppermute | solution.py:424
  27.0 2.0 %collective-permute-start.7 = (bf16[240,128]{1,0:T(8,128)(2,1)}, bf16[240,128]{1,0:T(8,128)(2,1)S(1)}, u32[]{:S(2)}, u32[]{:S(2)}) collective-permute-start(bf16[240,128]{1,0:T(8,128)(2,1)} %get-tuple-element.16), channel_id=1, source_target_pairs={{0,12},{4,8},{8,4},{12,0},{1,13},{5,9},{9,5},{13,1},{2,14},{6,10},... | collective-permute-start | bytes 184328 | tf_op jit(solution)/shard_map/ppermute | solution.py:424
  29.0 0.5 collective-permute-start.5
  29.5 4.3 %collective-permute-done.6.r_3_ = bf16[240,128]{1,0:T(8,128)(2,1)S(1)} collective-permute-done((bf16[240,128]{1,0:T(8,128)(2,1)}, bf16[240,128]{1,0:T(8,128)(2,1)S(1)}, u32[]{:S(2)}, u32[]{:S(2)}) %collective-permute-start.6) | collective-permute-done | bytes 61472 | tf_op jit(solution)/shard_map/ppermute | solution.py:424
  33.8 0.5 collective-permute-start.11
  34.3 0.3 collective-permute-done.5.r_2_
  34.6 0.5 collective-permute-start.17
  35.1 0.8 %collective-permute-done.17.r_16_ = f32[1,192]{1,0:T(1,128)S(1)} collective-permute-done((f32[1,192]{1,0:T(1,128)S(1)}, f32[1,192]{1,0:T(1,128)S(1)}, u32[]{:S(2)}, u32[]{:S(2)}) %collective-permute-start.17) | collective-permute-done | bytes 800 | tf_op jit(solution)/shard_map/ppermute | solution.py:430
  36.0 0.3 collective-permute-start.16
  36.3 0.1 copy.36.r_11_
  36.4 0.1 copy-done.23
  36.6 0.6 %collective-permute-done.16.r_14_ = f32[3,3,192]{2,1,0:T(4,128)S(1)} collective-permute-done((f32[3,3,192]{2,1,0:T(4,128)S(1)}, f32[3,3,192]{2,1,0:T(4,128)S(1)}, u32[]{:S(2)}, u32[]{:S(2)}) %collective-permute-start.16) | collective-permute-done | bytes 6944 | tf_op jit(solution)/shard_map/ppermute | solution.py:430
  37.2 0.3 collective-permute-start.15
  37.5 0.9 %collective-permute-done.15.r_12_ = bf16[192,32]{1,0:T(8,128)(2,1)S(1)} collective-permute-done((bf16[192,32]{1,0:T(8,128)(2,1)S(1)}, bf16[192,32]{1,0:T(8,128)(2,1)S(1)}, u32[]{:S(2)}, u32[]{:S(2)}) %collective-permute-start.15) | collective-permute-done | bytes 12320 | tf_op jit(solution)/shard_map/ppermute | solution.py:430
  38.5 0.5 copy-done.16
  39.1 7.6 %shard_map.101 = (bf16[192,128]{1,0:T(8,128)(2,1)}, bf16[192,128]{1,0:T(8,128)(2,1)}, bf16[192,128]{1,0:T(8,128)(2,1)}, bf16[192,128]{1,0:T(8,128)(2,1)}) custom-call(f32[16]{0:T(128)} %r_0_.3, bf16[240,128]{1,0:T(8,128)(2,1)} %get-tuple-element.13.r_1_, bf16[240,128]{1,0:T(8,128)(2,1)} %copy-done.7, bf16[240,128]{1,0:T(8,128)(2,1)} %copy-done.5, ...), custom_call_target="tpu_custom_call" | custom-call | tf_op jit(solution)/shard_map/pallas_call | solution.py:400
  46.7 1.0 %collective-permute-start.18 = (bf16[192,128]{1,0:T(8,128)(2,1)}, bf16[192,128]{1,0:T(8,128)(2,1)S(1)}, u32[]{:S(2)}, u32[]{:S(2)}) collective-permute-start(bf16[192,128]{1,0:T(8,128)(2,1)} %get-tuple-element.18), channel_id=1, source_target_pairs={{0,4},{4,0},{8,12},{12,8},{1,5},{5,1},{9,13},{13,9},{2,6},{6,2},{1... | collective-permute-start | bytes 147464 | tf_op jit(solution)/shard_map/ppermute | solution.py:424
  47.6 2.1 %collective-permute-start.19 = (bf16[192,128]{1,0:T(8,128)(2,1)}, bf16[192,128]{1,0:T(8,128)(2,1)S(1)}, u32[]{:S(2)}, u32[]{:S(2)}) collective-permute-start(bf16[192,128]{1,0:T(8,128)(2,1)} %get-tuple-element.19), channel_id=1, source_target_pairs={{0,8},{4,12},{8,0},{12,4},{1,9},{5,13},{9,1},{13,5},{2,10},{6,14},... | collective-permute-start | bytes 147464 | tf_op jit(solution)/shard_map/ppermute | solution.py:424
  49.7 1.4 %collective-permute-start.20 = (bf16[192,128]{1,0:T(8,128)(2,1)}, bf16[192,128]{1,0:T(8,128)(2,1)S(1)}, u32[]{:S(2)}, u32[]{:S(2)}) collective-permute-start(bf16[192,128]{1,0:T(8,128)(2,1)} %get-tuple-element.20), channel_id=1, source_target_pairs={{0,12},{4,8},{8,4},{12,0},{1,13},{5,9},{9,5},{13,1},{2,14},{6,10},... | collective-permute-start | bytes 147464 | tf_op jit(solution)/shard_map/ppermute | solution.py:424
  51.1 3.0 %collective-permute-done.19.r_2_ = bf16[192,128]{1,0:T(8,128)(2,1)S(1)} collective-permute-done((bf16[192,128]{1,0:T(8,128)(2,1)}, bf16[192,128]{1,0:T(8,128)(2,1)S(1)}, u32[]{:S(2)}, u32[]{:S(2)}) %collective-permute-start.19) | collective-permute-done | bytes 49184 | tf_op jit(solution)/shard_map/ppermute | solution.py:424
  54.1 1.8 %collective-permute-done.20.r_3_ = bf16[192,128]{1,0:T(8,128)(2,1)S(1)} collective-permute-done((bf16[192,128]{1,0:T(8,128)(2,1)}, bf16[192,128]{1,0:T(8,128)(2,1)S(1)}, u32[]{:S(2)}, u32[]{:S(2)}) %collective-permute-start.20) | collective-permute-done | bytes 49184 | tf_op jit(solution)/shard_map/ppermute | solution.py:424
  55.8 0.6 %copy-done.15 = bf16[192,128]{1,0:T(8,128)(2,1)} copy-done((bf16[192,128]{1,0:T(8,128)(2,1)}, bf16[192,128]{1,0:T(8,128)(2,1)S(1)}, u32[]{:S(2)}) %copy-start.15) | copy-done | bytes 49176
  56.4 2.0 %shard_map.102 = bf16[16,32,192]{2,1,0:T(8,128)(2,1)} custom-call(bf16[192,128]{1,0:T(8,128)(2,1)} %get-tuple-element.17.r_0_, bf16[192,128]{1,0:T(8,128)(2,1)} %copy-done.13, bf16[192,128]{1,0:T(8,128)(2,1)} %copy-done.14, bf16[192,128]{1,0:T(8,128)(2,1)} %copy-done.15, bf16[16,32,192]{2,1,0:T(8,128)(2,1)} %r_4_.1), custom_call_target="tpu_custom_call" | custom-call | tf_op jit(solution)/shard_map/pallas_call | solution.py:400
  (67 shorter events, 0.6 us)
Async XLA Ops:
  0.0 7.7 %copy-start.17 = (s32[16,32]{1,0:T(8,128)S(1)}, s32[16,32]{1,0:T(8,128)}, u32[]{:S(2)}) copy-start(s32[16,32]{1,0:T(8,128)} %param.12) | copy-start | bytes 6148
  0.0 8.6 %collective-permute-start.12 = (s32[16,32]{1,0:T(8,128)}, s32[16,32]{1,0:T(8,128)S(1)}, u32[]{:S(2)}, u32[]{:S(2)}) collective-permute-start(s32[16,32]{1,0:T(8,128)} %param.12), channel_id=1, source_target_pairs={{0,4},{4,0},{8,12},{12,8},{1,5},{5,1},{9,13},{13,9},{2,6},{6,2},{1... | collective-permute-start | bytes 6152 | tf_op jit(solution)/shard_map/ppermute | solution.py:424
  3.1 5.7 %collective-permute-start.13 = (s32[16,32]{1,0:T(8,128)}, s32[16,32]{1,0:T(8,128)S(1)}, u32[]{:S(2)}, u32[]{:S(2)}) collective-permute-start(s32[16,32]{1,0:T(8,128)} %param.12), channel_id=1, source_target_pairs={{0,8},{4,12},{8,0},{12,4},{1,9},{5,13},{9,1},{13,5},{2,10},{6,14},... | collective-permute-start | bytes 6152 | tf_op jit(solution)/shard_map/ppermute | solution.py:424
  5.6 5.7 %collective-permute-start.14 = (s32[16,32]{1,0:T(8,128)}, s32[16,32]{1,0:T(8,128)S(1)}, u32[]{:S(2)}, u32[]{:S(2)}) collective-permute-start(s32[16,32]{1,0:T(8,128)} %param.12), channel_id=1, source_target_pairs={{0,12},{4,8},{8,4},{12,0},{1,13},{5,9},{9,5},{13,1},{2,14},{6,10},... | collective-permute-start | bytes 6152 | tf_op jit(solution)/shard_map/ppermute | solution.py:424
  5.6 6.2 %collective-permute-start.3 = (s32[16,32]{1,0:T(8,128)}, s32[16,32]{1,0:T(8,128)S(1)}, u32[]{:S(2)}, u32[]{:S(2)}) collective-permute-start(s32[16,32]{1,0:T(8,128)} %param.12), channel_id=1, source_target_pairs={{0,2},{2,0},{1,3},{3,1},{4,6},{6,4},{5,7},{7,5},{8,10},{10,8},{9,1... | collective-permute-start | bytes 6152 | tf_op jit(solution)/shard_map/ppermute | solution.py:441
  7.4 7.3 %collective-permute-start = (bf16[16,32,192]{2,1,0:T(8,128)(2,1)}, bf16[16,32,192]{2,1,0:T(8,128)(2,1)S(1)}, u32[]{:S(2)}, u32[]{:S(2)}) collective-permute-start(bf16[16,32,192]{2,1,0:T(8,128)(2,1)} %r_1_.1), channel_id=1, source_target_pairs={{0,2},{2,0},{1,3},{3,1},{4,6},{6,4},{5,7},{7,5},{8,10},{10,8},{9,1... | collective-permute-start | bytes 589832 | tf_op jit(solution)/shard_map/ppermute | solution.py:440
  7.8 0.7 %copy-start.18 = (bf16[192,32]{0,1:T(8,128)(2,1)S(1)}, bf16[192,32]{0,1:T(8,128)(2,1)}, u32[]{:S(2)}) copy-start(bf16[192,32]{0,1:T(8,128)(2,1)} %param.15) | copy-start | bytes 36868
  8.6 2.8 %copy-start.3 = (bf16[192,32]{1,0:T(8,128)(2,1)}, bf16[192,32]{1,0:T(8,128)(2,1)S(1)}, u32[]{:S(2)}) copy-start(bf16[192,32]{1,0:T(8,128)(2,1)S(1)} %copy.26.r_8_) | copy-start | bytes 36868
  8.6 7.1 %collective-permute-start.1 = (bf16[16,32,192]{2,1,0:T(8,128)(2,1)}, bf16[16,32,192]{2,1,0:T(8,128)(2,1)S(1)}, u32[]{:S(2)}, u32[]{:S(2)}) collective-permute-start(bf16[16,32,192]{2,1,0:T(8,128)(2,1)} %r_1_.1), channel_id=1, source_target_pairs={{0,1},{1,0},{2,3},{3,2},{4,5},{5,4},{6,7},{7,6},{8,9},{9,8},{10,11... | collective-permute-start | bytes 589832 | tf_op jit(solution)/shard_map/ppermute | solution.py:430
  8.8 6.9 %collective-permute-start.4 = (bf16[192,32]{1,0:T(8,128)(2,1)S(1)}, bf16[192,32]{1,0:T(8,128)(2,1)S(1)}, u32[]{:S(2)}, u32[]{:S(2)}) collective-permute-start(bf16[192,32]{1,0:T(8,128)(2,1)S(1)} %copy.26.r_8_), channel_id=1, source_target_pairs={{0,1},{1,0},{2,3},{3,2},{4,5},{5,4},{6,7},{7,6},{8,9},{9,8},{10,11... | collective-permute-start | bytes 36872 | tf_op jit(solution)/shard_map/ppermute | solution.py:430
  14.6 1.5 %copy-start = (bf16[16,32,192]{2,1,0:T(8,128)(2,1)}, bf16[16,32,192]{2,1,0:T(8,128)(2,1)S(1)}, u32[]{:S(2)}) copy-start(bf16[16,32,192]{2,1,0:T(8,128)(2,1)S(1)} %collective-permute-done.r_2_) | copy-start | bytes 589828
  14.6 1.5 %collective-permute-start.2 = (bf16[16,32,192]{2,1,0:T(8,128)(2,1)S(1)}, bf16[16,32,192]{2,1,0:T(8,128)(2,1)S(1)}, u32[]{:S(2)}, u32[]{:S(2)}) collective-permute-start(bf16[16,32,192]{2,1,0:T(8,128)(2,1)S(1)} %collective-permute-done.r_2_), channel_id=1, source_target_pairs={{0,1},{1,0},{2,3},{3,2},{4,5},{5,4},{6,7},{7,6},{8,9},{9,8},{10,11... | collective-permute-start | bytes 589832 | tf_op jit(solution)/shard_map/ppermute | solution.py:430
  15.7 0.6 %copy-start.12 = (bf16[192,32]{1,0:T(8,128)(2,1)}, bf16[192,32]{1,0:T(8,128)(2,1)S(1)}, u32[]{:S(2)}) copy-start(bf16[192,32]{1,0:T(8,128)(2,1)S(1)} %collective-permute-done.4.r_9_) | copy-start | bytes 36868
  15.7 0.7 %copy-start.1 = (bf16[16,32,192]{2,1,0:T(8,128)(2,1)}, bf16[16,32,192]{2,1,0:T(8,128)(2,1)S(1)}, u32[]{:S(2)}) copy-start(bf16[16,32,192]{2,1,0:T(8,128)(2,1)S(1)} %collective-permute-done.1.r_3_) | copy-start | bytes 589828
  16.2 0.7 %copy-start.2 = (bf16[16,32,192]{2,1,0:T(8,128)(2,1)}, bf16[16,32,192]{2,1,0:T(8,128)(2,1)S(1)}, u32[]{:S(2)}) copy-start(bf16[16,32,192]{2,1,0:T(8,128)(2,1)S(1)} %collective-permute-done.2.r_4_) | copy-start | bytes 589828
  16.9 19.1 %copy-start.20 = (f32[3,3,192]{2,1,0:T(4,128)S(1)}, f32[3,3,192]{2,1,0:T(4,128)}, u32[]{:S(2)}) copy-start(f32[3,3,192]{2,1,0:T(4,128)} %r_13_.1) | copy-start | bytes 20740
  16.9 19.4 %copy-start.19 = (bf16[192,32]{0,1:T(8,128)(2,1)S(1)}, bf16[192,32]{0,1:T(8,128)(2,1)}, u32[]{:S(2)}) copy-start(bf16[192,32]{0,1:T(8,128)(2,1)} %param.16) | copy-start | bytes 36868
  25.3 8.5 %collective-permute-start.6 = (bf16[240,128]{1,0:T(8,128)(2,1)}, bf16[240,128]{1,0:T(8,128)(2,1)S(1)}, u32[]{:S(2)}, u32[]{:S(2)}) collective-permute-start(bf16[240,128]{1,0:T(8,128)(2,1)} %get-tuple-element.15), channel_id=1, source_target_pairs={{0,8},{4,12},{8,0},{12,4},{1,9},{5,13},{9,1},{13,5},{2,10},{6,14},... | collective-permute-start | bytes 184328 | tf_op jit(solution)/shard_map/ppermute | solution.py:424
  27.0 6.8 %collective-permute-start.7 = (bf16[240,128]{1,0:T(8,128)(2,1)}, bf16[240,128]{1,0:T(8,128)(2,1)S(1)}, u32[]{:S(2)}, u32[]{:S(2)}) collective-permute-start(bf16[240,128]{1,0:T(8,128)(2,1)} %get-tuple-element.16), channel_id=1, source_target_pairs={{0,12},{4,8},{8,4},{12,0},{1,13},{5,9},{9,5},{13,1},{2,14},{6,10},... | collective-permute-start | bytes 184328 | tf_op jit(solution)/shard_map/ppermute | solution.py:424
  29.0 5.7 %collective-permute-start.5 = (bf16[240,128]{1,0:T(8,128)(2,1)}, bf16[240,128]{1,0:T(8,128)(2,1)S(1)}, u32[]{:S(2)}, u32[]{:S(2)}) collective-permute-start(bf16[240,128]{1,0:T(8,128)(2,1)} %get-tuple-element.14), channel_id=1, source_target_pairs={{0,4},{4,0},{8,12},{12,8},{1,5},{5,1},{9,13},{13,9},{2,6},{6,2},{1... | collective-permute-start | bytes 184328 | tf_op jit(solution)/shard_map/ppermute | solution.py:424
  29.5 5.2 %copy-start.22 = (f32[192]{0:T(256)S(1)}, f32[192]{0:T(256)}, u32[]{:S(2)}) copy-start(f32[192]{0:T(256)} %param.18) | copy-start | bytes 2308
  29.5 8.9 %collective-permute-start.8 = (bf16[240,128]{1,0:T(8,128)(2,1)}, bf16[240,128]{1,0:T(8,128)(2,1)S(1)}, u32[]{:S(2)}, u32[]{:S(2)}) collective-permute-start(bf16[240,128]{1,0:T(8,128)(2,1)} %get-tuple-element.13.r_1_), channel_id=1, source_target_pairs={{0,1},{1,0},{2,3},{3,2},{4,5},{5,4},{6,7},{7,6},{8,9},{9,8},{10,11... | collective-permute-start | bytes 184328 | tf_op jit(solution)/shard_map/ppermute | solution.py:430
  33.8 4.6 %copy-start.5 = (bf16[240,128]{1,0:T(8,128)(2,1)}, bf16[240,128]{1,0:T(8,128)(2,1)S(1)}, u32[]{:S(2)}) copy-start(bf16[240,128]{1,0:T(8,128)(2,1)S(1)} %collective-permute-done.6.r_3_) | copy-start | bytes 184324
  33.8 4.6 %collective-permute-start.10 = (bf16[240,128]{1,0:T(8,128)(2,1)S(1)}, bf16[240,128]{1,0:T(8,128)(2,1)S(1)}, u32[]{:S(2)}, u32[]{:S(2)}) collective-permute-start(bf16[240,128]{1,0:T(8,128)(2,1)S(1)} %collective-permute-done.6.r_3_), channel_id=1, source_target_pairs={{0,1},{1,0},{2,3},{3,2},{4,5},{5,4},{6,7},{7,6},{8,9},{9,8},{10,11... | collective-permute-start | bytes 184328 | tf_op jit(solution)/shard_map/ppermute | solution.py:430
  33.8 4.6 %copy-start.6 = (bf16[240,128]{1,0:T(8,128)(2,1)}, bf16[240,128]{1,0:T(8,128)(2,1)S(1)}, u32[]{:S(2)}) copy-start(bf16[240,128]{1,0:T(8,128)(2,1)S(1)} %collective-permute-done.7.r_4_) | copy-start | bytes 184324
  33.8 4.6 %collective-permute-start.11 = (bf16[240,128]{1,0:T(8,128)(2,1)S(1)}, bf16[240,128]{1,0:T(8,128)(2,1)S(1)}, u32[]{:S(2)}, u32[]{:S(2)}) collective-permute-start(bf16[240,128]{1,0:T(8,128)(2,1)S(1)} %collective-permute-done.7.r_4_), channel_id=1, source_target_pairs={{0,1},{1,0},{2,3},{3,2},{4,5},{5,4},{6,7},{7,6},{8,9},{9,8},{10,11... | collective-permute-start | bytes 184328 | tf_op jit(solution)/shard_map/ppermute | solution.py:430
  34.6 3.8 %copy-start.7 = (bf16[240,128]{1,0:T(8,128)(2,1)}, bf16[240,128]{1,0:T(8,128)(2,1)S(1)}, u32[]{:S(2)}) copy-start(bf16[240,128]{1,0:T(8,128)(2,1)S(1)} %collective-permute-done.5.r_2_) | copy-start | bytes 184324
  34.6 3.8 %collective-permute-start.9 = (bf16[240,128]{1,0:T(8,128)(2,1)S(1)}, bf16[240,128]{1,0:T(8,128)(2,1)S(1)}, u32[]{:S(2)}, u32[]{:S(2)}) collective-permute-start(bf16[240,128]{1,0:T(8,128)(2,1)S(1)} %collective-permute-done.5.r_2_), channel_id=1, source_target_pairs={{0,1},{1,0},{2,3},{3,2},{4,5},{5,4},{6,7},{7,6},{8,9},{9,8},{10,11... | collective-permute-start | bytes 184328 | tf_op jit(solution)/shard_map/ppermute | solution.py:430
  34.6 1.3 %collective-permute-start.17 = (f32[1,192]{1,0:T(1,128)S(1)}, f32[1,192]{1,0:T(1,128)S(1)}, u32[]{:S(2)}, u32[]{:S(2)}) collective-permute-start(f32[1,192]{1,0:T(1,128)S(1)} %bitcast.25), channel_id=1, source_target_pairs={{0,1},{1,0},{2,3},{3,2},{4,5},{5,4},{6,7},{7,6},{8,9},{9,8},{10,11... | collective-permute-start | bytes 2312 | tf_op jit(solution)/shard_map/ppermute | solution.py:430
  36.0 0.6 %copy-start.23 = (f32[1,192]{1,0:T(1,128)}, f32[1,192]{1,0:T(1,128)S(1)}, u32[]{:S(2)}) copy-start(f32[1,192]{1,0:T(1,128)S(1)} %collective-permute-done.17.r_16_) | copy-start | bytes 2308
  36.0 1.2 %collective-permute-start.16 = (f32[3,3,192]{2,1,0:T(4,128)S(1)}, f32[3,3,192]{2,1,0:T(4,128)S(1)}, u32[]{:S(2)}, u32[]{:S(2)}) collective-permute-start(f32[3,3,192]{2,1,0:T(4,128)S(1)} %copy-done.20), channel_id=1, source_target_pairs={{0,1},{1,0},{2,3},{3,2},{4,5},{5,4},{6,7},{7,6},{8,9},{9,8},{10,11... | collective-permute-start | bytes 20744 | tf_op jit(solution)/shard_map/ppermute | solution.py:430
  36.6 1.9 %copy-start.4 = (bf16[192,32]{1,0:T(8,128)(2,1)}, bf16[192,32]{1,0:T(8,128)(2,1)S(1)}, u32[]{:S(2)}) copy-start(bf16[192,32]{1,0:T(8,128)(2,1)S(1)} %copy.36.r_11_) | copy-start | bytes 36868
  37.1 1.3 %copy-start.21 = (f32[3,3,192]{2,1,0:T(4,128)}, f32[3,3,192]{2,1,0:T(4,128)S(1)}, u32[]{:S(2)}) copy-start(f32[3,3,192]{2,1,0:T(4,128)S(1)} %collective-permute-done.16.r_14_) | copy-start | bytes 20740
  37.2 1.2 %collective-permute-start.15 = (bf16[192,32]{1,0:T(8,128)(2,1)S(1)}, bf16[192,32]{1,0:T(8,128)(2,1)S(1)}, u32[]{:S(2)}, u32[]{:S(2)}) collective-permute-start(bf16[192,32]{1,0:T(8,128)(2,1)S(1)} %copy.36.r_11_), channel_id=1, source_target_pairs={{0,1},{1,0},{2,3},{3,2},{4,5},{5,4},{6,7},{7,6},{8,9},{9,8},{10,11... | collective-permute-start | bytes 36872 | tf_op jit(solution)/shard_map/ppermute | solution.py:430
  38.4 0.6 %copy-start.16 = (bf16[192,32]{1,0:T(8,128)(2,1)}, bf16[192,32]{1,0:T(8,128)(2,1)S(1)}, u32[]{:S(2)}) copy-start(bf16[192,32]{1,0:T(8,128)(2,1)S(1)} %collective-permute-done.15.r_12_) | copy-start | bytes 36868
  38.4 0.6 %copy-start.8 = (bf16[240,128]{1,0:T(8,128)(2,1)}, bf16[240,128]{1,0:T(8,128)(2,1)S(1)}, u32[]{:S(2)}) copy-start(bf16[240,128]{1,0:T(8,128)(2,1)S(1)} %collective-permute-done.8.r_5_) | copy-start | bytes 184324
  38.4 0.7 %copy-start.9 = (bf16[240,128]{1,0:T(8,128)(2,1)}, bf16[240,128]{1,0:T(8,128)(2,1)S(1)}, u32[]{:S(2)}) copy-start(bf16[240,128]{1,0:T(8,128)(2,1)S(1)} %collective-permute-done.10.r_7_) | copy-start | bytes 184324
  38.4 0.7 %copy-start.10 = (bf16[240,128]{1,0:T(8,128)(2,1)}, bf16[240,128]{1,0:T(8,128)(2,1)S(1)}, u32[]{:S(2)}) copy-start(bf16[240,128]{1,0:T(8,128)(2,1)S(1)} %collective-permute-done.11.r_8_) | copy-start | bytes 184324
  38.4 0.7 %copy-start.11 = (bf16[240,128]{1,0:T(8,128)(2,1)}, bf16[240,128]{1,0:T(8,128)(2,1)S(1)}, u32[]{:S(2)}) copy-start(bf16[240,128]{1,0:T(8,128)(2,1)S(1)} %collective-permute-done.9.r_6_) | copy-start | bytes 184324
  46.7 4.4 %collective-permute-start.18 = (bf16[192,128]{1,0:T(8,128)(2,1)}, bf16[192,128]{1,0:T(8,128)(2,1)S(1)}, u32[]{:S(2)}, u32[]{:S(2)}) collective-permute-start(bf16[192,128]{1,0:T(8,128)(2,1)} %get-tuple-element.18), channel_id=1, source_target_pairs={{0,4},{4,0},{8,12},{12,8},{1,5},{5,1},{9,13},{13,9},{2,6},{6,2},{1... | collective-permute-start | bytes 147464 | tf_op jit(solution)/shard_map/ppermute | solution.py:424
  47.6 6.4 %collective-permute-start.19 = (bf16[192,128]{1,0:T(8,128)(2,1)}, bf16[192,128]{1,0:T(8,128)(2,1)S(1)}, u32[]{:S(2)}, u32[]{:S(2)}) collective-permute-start(bf16[192,128]{1,0:T(8,128)(2,1)} %get-tuple-element.19), channel_id=1, source_target_pairs={{0,8},{4,12},{8,0},{12,4},{1,9},{5,13},{9,1},{13,5},{2,10},{6,14},... | collective-permute-start | bytes 147464 | tf_op jit(solution)/shard_map/ppermute | solution.py:424
  49.7 6.1 %collective-permute-start.20 = (bf16[192,128]{1,0:T(8,128)(2,1)}, bf16[192,128]{1,0:T(8,128)(2,1)S(1)}, u32[]{:S(2)}, u32[]{:S(2)}) collective-permute-start(bf16[192,128]{1,0:T(8,128)(2,1)} %get-tuple-element.20), channel_id=1, source_target_pairs={{0,12},{4,8},{8,4},{12,0},{1,13},{5,9},{9,5},{13,1},{2,14},{6,10},... | collective-permute-start | bytes 147464 | tf_op jit(solution)/shard_map/ppermute | solution.py:424
  51.1 4.7 %copy-start.13 = (bf16[192,128]{1,0:T(8,128)(2,1)}, bf16[192,128]{1,0:T(8,128)(2,1)S(1)}, u32[]{:S(2)}) copy-start(bf16[192,128]{1,0:T(8,128)(2,1)S(1)} %collective-permute-done.18.r_1_) | copy-start | bytes 147460
  54.1 1.8 %copy-start.14 = (bf16[192,128]{1,0:T(8,128)(2,1)}, bf16[192,128]{1,0:T(8,128)(2,1)S(1)}, u32[]{:S(2)}) copy-start(bf16[192,128]{1,0:T(8,128)(2,1)S(1)} %collective-permute-done.19.r_2_) | copy-start | bytes 147460
  55.8 0.6 %copy-start.15 = (bf16[192,128]{1,0:T(8,128)(2,1)}, bf16[192,128]{1,0:T(8,128)(2,1)S(1)}, u32[]{:S(2)}) copy-start(bf16[192,128]{1,0:T(8,128)(2,1)S(1)} %collective-permute-done.20.r_3_) | copy-start | bytes 147460

commit v3 on v2

--- a/solution.py
+++ b/solution.py
@@ -32,11 +32,21 @@
 
 def tables(table_ref):
     t = table_ref[...] * LOG2E
-    return split3(t[:, :LANES]), split3(twice(t[:, LANES:]))
+    return split3(jnp.concatenate([t[:, :LANES], twice(t[:, LANES:])], axis=-1))
+
+
+def mark(entry, entries):
+    lane = lax.broadcasted_iota(jnp.int32, entry.shape, 1)
+    spot = jnp.where(lane < 3 * entries, lane % entries, -1).astype(F32)
+    return (entry == spot).astype(F32).astype(BF16)
 
 
 def dot(a, b):
     return jnp.dot(a, b, preferred_element_type=F32)
+
+
+def dot_t(a, b):
+    return lax.dot_general(a, b, (((1,), (1,)), ((), ())), preferred_element_type=F32)
 
 
 def fill_rates(rate_ref, rates):
@@ -99,13 +109,16 @@
     return jnp.broadcast_to(coeff[:, column : column + 1], (coeff.shape[0], LANES))
 
 
+def thirds(v, count):
+    lane = lax.broadcasted_iota(jnp.int32, v.shape, 1)
+    hi = v.astype(BF16).astype(F32)
+    mid = (v - hi).astype(BF16).astype(F32)
+    return jnp.where(lane < count, hi, jnp.where(lane < 2 * count, mid, v - hi - mid))
+
+
 def spread_all(cf_ref, count, matrix, permute):
     for (column, to, rows), (column2, to2, rows2) in zip(matrix[::2], matrix[1::2]):
-        v = cf_ref[:rows, : 3 * count]
-        lane = lax.broadcasted_iota(jnp.int32, v.shape, 1)
-        hi = v.astype(BF16).astype(F32)
-        mid = (v - hi).astype(BF16).astype(F32)
-        parts = jnp.where(lane < count, hi, jnp.where(lane < 2 * count, mid, v - hi - mid)).astype(BF16)
+        parts = thirds(cf_ref[:rows, : 3 * count], count).astype(BF16)
         shape = (3 * count, 2 * LANES)
         source = lax.broadcasted_iota(jnp.int32, shape, 0) % count
         wanted = jnp.where(lax.broadcasted_iota(jnp.int32, shape, 1) < LANES, column, column2)
@@ -117,30 +130,33 @@
 
 
 def thrice(v):
-    return jnp.concatenate([v, v, v], axis=-1)
+    return jnp.concatenate([v, v, v], axis=0)
 
 
 def row_kernel(dims, dest, *refs):
     tiles, strips, height, width, strip = dims
     rate_ref = refs[0]
     own, other = refs[1 : 1 + tiles], refs[1 + tiles : 1 + 2 * tiles]
-    hots = refs[1 + 2 * tiles : 1 + 3 * tiles]
+    idxs = refs[1 + 2 * tiles : 1 + 3 * tiles]
     table_ref, proj_ref, proj2_ref, skip_ref = refs[1 + 3 * tiles : 5 + 3 * tiles]
     outs = refs[5 + 3 * tiles : 5 + 3 * tiles + strips]
     scratch = refs[5 + 3 * tiles + strips :]
-    raw, xa_ref, xb_ref, la_ref, lb_ref, cf_ref, drives, weights, ya_ref, yb_ref, rates = scratch[:3], *scratch[3:]
+    raw, xa_ref, xb_ref, la_ref, lb_ref, cf_ref, drives, weights, ya_ref, yb_ref, rates = scratch[:3], *scratch[3:13]
+    entry_ref, hot_ref = scratch[13:]
     states = rate_ref.shape[0]
     cells = height * width
     pitch = pitch_of(width)
     col = lax.axis_index("cols")
     row = lax.axis_index("rows")
 
-    ta, tb = tables(table_ref)
+    table = tables(table_ref)
+    entries = table_ref.shape[0]
+    entry_ref[...] = jnp.zeros(entry_ref.shape, F32)
     proj, proj2 = thrice(proj_ref[...]), thrice(proj2_ref[...])
     for d in range(tiles):
         x = own[d][...].reshape(cells, -1)
         part = pl.ds(d * cells, cells)
-        coeff = dot(x, proj) + dot(other[d][...].reshape(cells, -1), proj2)
+        coeff = dot_t(x, proj) + dot_t(other[d][...].reshape(cells, -1), proj2)
         xf = x.astype(F32)
         xa, xb = xf[:, :LANES], twice(xf[:, LANES:])
         if 0 < d < tiles - 1:
@@ -151,9 +167,14 @@
             raw[0][to, :] = xa[cut]
             raw[1][to, :] = xb[cut]
             raw[2][to, : 6 * states] = coeff[cut]
-        hot = hots[d][...]
-        la_ref[part, :] = dot(hot, ta)
-        lb_ref[part, :] = dot(hot, tb)
+        entry = idxs[d][...].astype(F32)
+        if d == 0:
+            entry_ref[:, :width] = entry
+        for w in range(width):
+            hot_ref[w * height : (w + 1) * height, :] = mark(spread(entry, w), entries)
+        logs = dot(hot_ref[:, : 3 * entries], table)
+        la_ref[part, :] = logs[:, :LANES]
+        lb_ref[part, :] = logs[:, LANES:]
 
     fill_rates(rate_ref, rates)
     for d in range(tiles):
@@ -225,15 +246,248 @@
         inside = 1.0 - last_left
         put(width + 1, ya * inside, yb * inside)
 
+    pack_blocks(outs, dest, row, strip, height, ya_ref, yb_ref, entry_ref)
+
+
+def pack_blocks(outs, dest, row, strip, height, ya_ref, yb_ref, entry_ref):
     count = strip + 2
-    for d in range(strips):
+    rows = count * height * 3 // 2
+    for d in range(len(outs)):
         start = pl.multiple_of(dest(row, d) * strip * height, SUB)
         from_ = pl.ds(start, count * height)
         outs[d][: count * height, :] = ya_ref[from_, :].astype(BF16)
         yb = yb_ref[from_, :].reshape(count, 2, height // 2, LANES)
         low, high = yb[:, 0], yb[:, 1]
         packed = jnp.where(low_half(low.shape), low, high).reshape(count * height // 2, LANES)
-        outs[d][count * height :, :] = packed.astype(BF16)
+        outs[d][count * height : rows, :] = packed.astype(BF16)
+        entry = pltpu.roll(entry_ref[...], LANES - dest(row, d) * strip, 1)
+        outs[d][rows:, :] = entry.astype(BF16)
+
+
+def split2(v):
+    hi = v.astype(BF16).astype(F32)
+    return hi, v - hi
+
+
+def own_kernel(dims, *refs):
+    height, width = dims
+    inputs, (xa_ref, xb_ref, la_ref, lb_ref, cf_ref, rates, skips, entry_ref, marks) = refs[:6], refs[6:15]
+    raw, hot_ref, held, arrived = refs[15:18], refs[18], refs[19:25], refs[25]
+    copies = [pltpu.make_async_copy(a, b, arrived.at[i]) for i, (a, b) in enumerate(zip(inputs, held))]
+    for copy in copies:
+        copy.start()
+    for copy in copies:
+        copy.wait()
+    rate_ref, own_ref, idx_ref, table_ref, proj_ref, skip_ref = held
+    states = rate_ref.shape[0]
+    cells = height * width
+    pitch = pitch_of(width)
+
+    table = tables(table_ref)
+    marks[...] = table
+    entries = table_ref.shape[0]
+    x = own_ref[...].reshape(cells, -1)
+    coeff = dot_t(x, thrice(proj_ref[...]))
+    xf = x.astype(F32)
+    xa, xb = xf[:, :LANES], twice(xf[:, LANES:])
+    for h in range(height):
+        to, cut = pl.ds(h * pitch, width), slice(h * width, (h + 1) * width)
+        raw[0][to, :] = xa[cut]
+        raw[1][to, :] = xb[cut]
+        raw[2][to, : 6 * states] = coeff[cut]
+    entry = idx_ref[...].astype(F32)
+    entry_ref[...] = jnp.zeros(entry_ref.shape, F32)
+    entry_ref[:, :width] = entry
+    for w in range(width):
+        hot_ref[w * height : (w + 1) * height, :] = mark(spread(entry, w), entries)
+    logs = dot(hot_ref[:, : 3 * entries], table)
+    la_ref[...] = logs[:, :LANES]
+    lb_ref[...] = logs[:, LANES:]
+    fill_rates(rate_ref, rates)
+    skip = skip_ref[...]
+    skips[:SUB, :] = jnp.broadcast_to(skip[:, :LANES], (SUB, LANES))
+    skips[SUB:, :] = jnp.broadcast_to(twice(skip[:, LANES:]), (SUB, LANES))
+    in_order(dims, raw, (xa_ref, xb_ref, cf_ref))
+
+
+def in_order(dims, olds, news, add=None):
+    height, width = dims
+    pitch = pitch_of(width)
+
+    def order(w, unused):
+        for g in range(height // SUB):
+            place = pl.ds(g * SUB * pitch + w, SUB, stride=pitch)
+            to = pl.ds(pl.multiple_of(w * height + g * SUB, SUB), SUB)
+            for old, new in zip(olds, news):
+                new[to, :] = old[place, :] if add is None else old[place, :] + add[to, :]
+        return unused
+
+    steps(width, order, 0)
+
+
+def add_up(v):
+    while len(v) > 1:
+        v = [v[i] + v[i + 1] for i in range(0, len(v) - 1, 2)] + v[len(v) & ~1 :]
+    return v[0]
+
+
+def at_step(ref, i, cells, here):
+    return ref[pl.ds(pl.multiple_of(i * cells + here, SUB), SUB), :]
+
+
+def tile_kernel(dims, *refs):
+    height, width = dims
+    other_ref, proj2_ref, xa_ref, xb_ref, la_ref, lb_ref, half_ref, rates, skips, entry_ref = refs[:10]
+    note_ref, ya_ref, yb_ref, sa_ref, sb_ref, cf_ref = refs[10:16]
+    raw, drives, weights = refs[16:]
+    kinds = rates.shape[0] // SUB
+    states = kinds * 2 // 3
+    cells = height * width
+    pitch = pitch_of(width)
+
+    coeff = dot_t(other_ref[...].reshape(cells, -1), thrice(proj2_ref[...]))
+    for h in range(height):
+        raw[h * pitch : h * pitch + width, : 6 * states] = coeff[h * width : (h + 1) * width]
+    in_order(dims, (raw,), (cf_ref,), half_ref)
+    every = [(s, drives.at[s * cells : (s + 1) * cells, :], cells) for s in range(states)]
+    every += [(states + s, weights.at[s * cells : (s + 1) * cells, :], cells) for s in range(states)]
+    cut = states * 5 // 4 // 2 * 2
+    spread_all(cf_ref, 2 * states, every[:cut], every[cut:])
+
+    skip_a, skip_b = skips[:SUB, :], skips[SUB:, :]
+    for g in range(height // SUB):
+
+        def step(w, carry, g=g):
+            carry, sum_a, sum_b = carry
+            here = w * height + g * SUB
+            at = pl.ds(pl.multiple_of(here, SUB), SUB)
+            xa, xb, la, lb = xa_ref[at, :], xb_ref[at, :], la_ref[at, :], lb_ref[at, :]
+            carry, ya, yb = advance(
+                carry,
+                xa,
+                xb,
+                la,
+                lb,
+                lambda s: at_step(drives, s, cells, here),
+                lambda s: at_step(weights, s, cells, here),
+                rates,
+            )
+            sum_a, sum_b = sum_a + la, sum_b + lb
+            ya_ref[at, :] = ya + skip_a * xa
+            yb_ref[at, :] = yb + skip_b * xb
+            sa_ref[at, :] = sum_a
+            sb_ref[at, :] = sum_b
+            return carry, sum_a, sum_b
+
+        zero = jnp.zeros((SUB, LANES), F32)
+        carry, _, _ = steps(width, step, ((zero,) * kinds, zero, zero))
+        for i in range(0, kinds, 2):
+            at = (g * kinds + i) * SUB
+            note_ref[at : at + 2 * SUB, :] = jnp.concatenate(carry[i : i + 2], axis=0).astype(BF16)
+
+    lane = lax.broadcasted_iota(jnp.int32, (height, LANES), 1)
+    first = jnp.where(lane < 6 * states, thirds(cf_ref[:height, :], 2 * states), 0.0)
+    a, a2 = split2(ya_ref[:height, :])
+    b, b2 = split2(yb_ref[:height, :])
+    extra = [
+        jnp.where(lane == 6 * states, spread(entry_ref[...], 0), first),
+        a,
+        a2,
+        jnp.where(low_half(b.shape), b, b2),
+        ya_ref[cells - height :, :],
+        yb_ref[cells - height :, :],
+    ]
+    for i, v in enumerate(extra):
+        at = kinds * height + i * height
+        note_ref[at : at + height, :] = v.astype(BF16)
+
+
+def weigh_kernel(*refs):
+    cf_ref, sa_ref, sb_ref, rates, out_ref, weights = refs
+    kinds = rates.shape[0] // SUB
+    states = kinds * 2 // 3
+    cells = cf_ref.shape[0]
+    half = low_half((SUB, LANES))
+    every = [(states + s, weights.at[s * cells : (s + 1) * cells, :], cells) for s in range(states)]
+    cut = states * 5 // 8 // 2 * 2
+    spread_all(cf_ref, 2 * states, every[:cut], every[cut:])
+
+    def step(i, unused):
+        here = i * SUB
+        at = pl.ds(pl.multiple_of(here, SUB), SUB)
+        sum_a, sum_b = sa_ref[at, :], sb_ref[at, :]
+        wide = [at_step(weights, s, cells, here) for s in range(states)]
+        for k in range(kinds):
+            j = k - states
+            log, weight = (sum_a, wide[k]) if j < 0 else (sum_b, jnp.where(half, wide[2 * j], wide[2 * j + 1]))
+            to = pl.ds(pl.multiple_of(k * cells + here, SUB), SUB)
+            out_ref[to, :] = weight * jnp.exp2(log * rates[k * SUB : (k + 1) * SUB, :])
+        return unused
+
+    steps(cells // SUB, step, 0)
+
+
+def join_kernel(dims, dest, *refs):
+    strips, height, width, strip = dims
+    own_ref, came_ref, ta_ref, tb_ref, brings, entry_ref, marks, rates = refs[:8]
+    outs = refs[8 : 8 + strips]
+    ya_ref, yb_ref = refs[8 + strips :]
+    kinds = rates.shape[0] // SUB
+    states = kinds * 2 // 3
+    cells = height * width
+    row = lax.axis_index("rows")
+    right = (lax.axis_index("cols") == 1).astype(F32)
+    half = low_half((SUB, LANES))
+
+    def extra(i):
+        at = (kinds + i) * height
+        return came_ref[at : at + height, :].astype(F32)
+
+    first = extra(0)
+    log = dot(mark(spread(first, 6 * states), marks.shape[0] // 3)[:, : marks.shape[0]], marks[...])
+    group = 2 * states
+    coeff = first + pltpu.roll(first, LANES - group, 1) + pltpu.roll(first, LANES - 2 * group, 1)
+    near_b = extra(3)
+    near_b = near_b + pltpu.roll(near_b, LANES // 2, 1)
+    near_a = extra(1) + extra(2)
+    ya_ref[:height, :] = extra(4) * right
+    yb_ref[:height, :] = extra(5) * right
+
+    for g in range(height // SUB):
+
+        def inflow(ref, scale, g=g):
+            new = []
+            for i in range(0, kinds, 2):
+                at = (g * kinds + i) * SUB
+                v = ref[at : at + 2 * SUB, :].astype(F32) * scale
+                new += [v[:SUB], v[SUB:]]
+            return tuple(new)
+
+        def step(w, state, g=g):
+            here = w * height + g * SUB
+            at = pl.ds(pl.multiple_of(here, SUB), SUB)
+            to = pl.ds(pl.multiple_of(here + height, SUB), SUB)
+            terms = [at_step(brings, k, cells, here) * state[k] for k in range(kinds)]
+            b = add_up(terms[states:])
+            ya_ref[to, :] = ta_ref[at, :] + add_up(terms[:states])
+            yb_ref[to, :] = tb_ref[at, :] + b + pltpu.roll(b, LANES // 2, 1)
+            return state
+
+        steps(width, step, inflow(came_ref, right))
+        cut = slice(g * SUB, (g + 1) * SUB)
+        state = inflow(own_ref, 1.0)
+        wide = [spread(coeff[cut], states + s) for s in range(states)]
+        wide += [jnp.where(half, wide[2 * j], wide[2 * j + 1]) for j in range(states // 2)]
+        terms = []
+        for k in range(kinds):
+            part = log[cut, :LANES] if k < states else log[cut, LANES:]
+            terms.append(wide[k] * (jnp.exp2(part * rates[k * SUB : (k + 1) * SUB, :]) * state[k]))
+        b = add_up(terms[states:])
+        at = slice((width + 1) * height + g * SUB, (width + 1) * height + (g + 1) * SUB)
+        ya_ref[at, :] = (near_a[cut] + add_up(terms[:states])) * (1.0 - right)
+        yb_ref[at, :] = (near_b[cut] + b + pltpu.roll(b, LANES // 2, 1)) * (1.0 - right)
+
+    pack_blocks(outs, dest, row, strip, height, ya_ref, yb_ref, entry_ref)
 
 
 def unpack(v):
@@ -247,15 +501,15 @@
     rate_ref = refs[0]
     blocks = (refs[1 : 1 + strips], refs[1 + strips : 1 + 2 * strips])
     at = 1 + 2 * strips
-    hot_ref, table_ref = refs[at : at + 2]
-    projs = refs[at + 2 : at + 4]
-    conv_ws = refs[at + 4 : at + 6]
-    conv_bs = refs[at + 6 : at + 8]
-    skip_ref = refs[at + 8]
-    outs = refs[at + 9 : at + 9 + strips]
-    scratch = refs[at + 9 + strips :]
-    ra_ref, rb_ref, raw = *scratch[:2], scratch[2:5]
-    xa_ref, xb_ref, cf_ref, la_ref, lb_ref, ya_ref, yb_ref, drives, weights, rates = scratch[5:]
+    table_ref = refs[at]
+    projs = refs[at + 1 : at + 3]
+    conv_ws = refs[at + 3 : at + 5]
+    conv_bs = refs[at + 5 : at + 7]
+    skip_ref = refs[at + 7]
+    outs = refs[at + 8 : at + 8 + strips]
+    scratch = refs[at + 8 + strips :]
+    ra_ref, rb_ref, raw = *scratch[:2], scratch[2:7]
+    xa_ref, xb_ref, cf_ref, la_ref, lb_ref, ya_ref, yb_ref, drives, weights, rates, hot_ref = scratch[7:]
     states = rate_ref.shape[0]
     row = lax.axis_index("rows")
     total = strips * height
@@ -264,10 +518,19 @@
     count = strip + 2
     fill_rates(rate_ref, rates)
 
-    ta, tb = tables(table_ref)
-    hot = hot_ref[...]
-    la_ref[...] = dot(hot, ta)
-    lb_ref[...] = dot(hot, tb)
+    table = tables(table_ref)
+    entries = table_ref.shape[0]
+    rows = count * height * 3 // 2
+    for d in range(strips):
+        entry = blocks[0][d][rows:, :].astype(F32)
+        base = pl.multiple_of(dest(row, d) * height, 2 * SUB)
+        for k in range(strip):
+            hot_ref[pl.ds(pl.multiple_of(base + k * total, 2 * SUB), height), :] = mark(spread(entry, k), entries)
+    logs = dot(hot_ref[:, : 3 * entries], table)
+    for k in range(strip):
+        cut = logs[k * total : (k + 1) * total]
+        raw[3][k * leap : k * leap + total, :] = cut[:, :LANES]
+        raw[4][k * leap : k * leap + total, :] = cut[:, LANES:]
     zero = jnp.zeros((SUB, LANES), F32)
     for k in range(count):
         for ref in (ra_ref, rb_ref):
@@ -278,7 +541,7 @@
         for d in range(strips):
             base = pl.multiple_of(dest(row, d) * height, SUB) + SUB
             va = blocks[side][d][: count * height, :].astype(F32)
-            low, high = unpack(blocks[side][d][count * height :, :].astype(F32))
+            low, high = unpack(blocks[side][d][count * height : rows, :].astype(F32))
             h2 = height // 2
             for k in range(count):
                 to = pl.multiple_of(base + k * pitch, SUB)
@@ -312,8 +575,8 @@
         proj = thrice(projs[side][...])
         for k in range(strip):
             at = pl.ds(k * leap, total)
-            part = dot(raw[0][at, :].astype(BF16), proj[:LANES]) + dot(
-                raw[1][at, : LANES // 2].astype(BF16), proj[LANES:]
+            part = dot_t(raw[0][at, :].astype(BF16), proj[:, :LANES]) + dot_t(
+                raw[1][at, : LANES // 2].astype(BF16), proj[:, LANES:]
             )
             raw[2][at, : 6 * states] = part if side else part + raw[2][at, : 6 * states]
 
@@ -325,7 +588,7 @@
         return pl.ds(at if strip % SUB else pl.multiple_of(at, SUB), strip)
 
     def order(h, unused):
-        for old, new in zip(raw, (xa_ref, xb_ref, cf_ref)):
+        for old, new in zip(raw, (xa_ref, xb_ref, cf_ref, la_ref, lb_ref)):
             new[here(h), :] = old[pl.ds(h, strip, stride=leap), :]
         return unused
 
@@ -392,23 +655,28 @@
     return pl.BlockSpec(memory_space=pltpu.SMEM)
 
 
+def hbm():
+    return pl.BlockSpec(memory_space=pltpu.HBM)
+
+
 def vmem():
     return pl.BlockSpec(memory_space=pltpu.VMEM)
 
 
-def call(kernel, args, outs, scratch):
+def call(kernel, args, outs, scratch, limit, left=False):
+    held = []
+    if left:
+        args = [pltpu.with_memory_space_constraint(a, pltpu.HBM) for a in args]
+        held = [(pltpu.SMEM if a.ndim == 1 else pltpu.VMEM)(a.shape, a.dtype) for a in args]
+        held += [pltpu.SemaphoreType.DMA((len(args),))]
     return pl.pallas_call(
         kernel,
         out_shape=outs,
-        in_specs=[smem() if a.ndim == 1 else vmem() for a in args],
+        in_specs=[hbm() if left else smem() if a.ndim == 1 else vmem() for a in args],
         out_specs=jax.tree.map(lambda _: vmem(), outs),
-        scratch_shapes=[pltpu.VMEM(s, F32) for s in scratch],
+        scratch_shapes=[pltpu.VMEM(getattr(s, "shape", s), getattr(s, "dtype", F32)) for s in scratch] + held,
+        compiler_params=pltpu.CompilerParams(vmem_limit_bytes=limit),
     )(*args)
-
-
-def onehot(idx, entries):
-    spots = jnp.arange(3 * entries, dtype=jnp.int32) % entries
-    return (idx.reshape(-1, 1) == spots).astype(BF16)
 
 
 def make_shards(strips, tiles):
@@ -420,9 +688,10 @@
 
     def exchange(blocks, axis="rows"):
         if few:
-            return [blocks[0]] + [
-                lax.ppermute(blocks[d], axis, [(i, i ^ d) for i in range(strips)]) for d in range(1, strips)
-            ]
+            moved = [blocks[0]]
+            for d in range(1, strips):
+                moved.append(lax.ppermute(blocks[d], axis, [(i, i ^ d) for i in range(strips)]))
+            return moved
         moved = lax.all_to_all(jnp.stack(blocks), axis, 0, 0)
         return [moved[d] for d in range(strips)]
 
@@ -431,58 +700,89 @@
 
     def shards(features, gate, decay_idx, log_table, rate, proj_row, proj_col, conv_w, conv_b, d_skip):
         height, width, channels = features.shape
-        entries, states = log_table.shape[0], rate.shape[0]
+        states = rate.shape[0]
         strip = width // strips
         cells, total, count = height * width, strips * height, strip + 2
         skip, bias = d_skip.reshape(1, channels), conv_b.reshape(1, channels)
-
-        rounds = [[(i, (i + d) % tiles) for i in range(tiles)] for d in range(1, tiles)]
-        own = [features] + [lax.ppermute(features, "cols", pairs) for pairs in rounds]
-        idx = [decay_idx] + [lax.ppermute(decay_idx, "cols", pairs) for pairs in rounds]
+        proj_row, proj_col = proj_row.T, proj_col.T
+
+        block = jax.ShapeDtypeStruct((count * height * 3 // 2 + height, LANES), BF16)
+        kinds = states * 3 // 2
+        rate_rows = (kinds * SUB, LANES)
+        high = pitch_of(width) * height
         other = [across(features)]
-        other += [across(f) for f in own[1:]]
-        proj_row2, proj_col2 = across(proj_row), across(proj_col)
-        conv_w2, bias2 = across(conv_w), across(bias)
-        hots = [onehot(i.T, entries) for i in idx]
-        if few:
-            whole = exchange([decay_idx] * strips)
-            row = lax.axis_index("rows")
-            order = jnp.arange(strips) ^ row
-            parts = jnp.stack([w.reshape(height, strips, strip) for w in whole])
-            mine = lax.dynamic_index_in_dim(parts, row, 2, keepdims=False)
-            mine = sum(
-                jnp.where((order == k)[:, None, None], mine[k][None], 0) for k in range(strips)
+        proj_row2 = across(proj_row)
+        if tiles == 2:
+            wide = jax.ShapeDtypeStruct((cells, LANES), F32)
+            rates = jax.ShapeDtypeStruct(rate_rows, F32)
+            entries = log_table.shape[0]
+            xa, xb, la, lb, half, rates, skips, entry, marks = call(
+                lambda *r: own_kernel((height, width), *r),
+                [rate, features, decay_idx, log_table, proj_row, skip],
+                [wide] * 5
+                + [
+                    rates,
+                    jax.ShapeDtypeStruct((2 * SUB, LANES), F32),
+                    jax.ShapeDtypeStruct((height, LANES), F32),
+                    jax.ShapeDtypeStruct((3 * entries, 2 * LANES), BF16),
+                ],
+                [(high, LANES)] * 3 + [jax.ShapeDtypeStruct((cells, LANES), BF16)],
+                8 << 20,
+                left=True,
+            )
+            note, ta, tb, sa, sb, cf = call(
+                lambda *r: tile_kernel((height, width), *r),
+                [other[0], proj_row2, xa, xb, la, lb, half, rates, skips, entry],
+                [jax.ShapeDtypeStruct(((kinds + 6) * height, LANES), BF16)] + [wide] * 5,
+                [(high, LANES)] + [(states * cells, LANES)] * 2,
+                16 << 20,
+            )
+            came = lax.ppermute(note, "cols", swap)
+            brings = call(
+                lambda *r: weigh_kernel(*r),
+                [cf, sa, sb, rates],
+                jax.ShapeDtypeStruct((kinds * cells, LANES), F32),
+                [(states * cells, LANES)],
+                16 << 20,
+            )
+            sent = call(
+                lambda *r: join_kernel((strips, height, width, strip), dest, *r),
+                [note, came, ta, tb, brings, entry, marks, rates],
+                [block] * strips,
+                [((width + 2) * height, LANES)] * 2,
+                8 << 20,
             )
         else:
-            mine = lax.all_to_all(
-                decay_idx.reshape(height, strips, strip).transpose(1, 0, 2), "rows", 0, 0
+            rounds = [[(i, (i + d) % tiles) for i in range(tiles)] for d in range(1, tiles)]
+            own = [features] + [lax.ppermute(features, "cols", pairs) for pairs in rounds]
+            idx = [decay_idx] + [lax.ppermute(decay_idx, "cols", pairs) for pairs in rounds]
+            other += [across(f) for f in own[1:]]
+            sent = call(
+                lambda *r: row_kernel((tiles, strips, height, width, strip), dest, *r),
+                [rate, *own, *other, *idx, log_table, proj_row, proj_row2, skip],
+                [block] * strips,
+                [(tiles * high, LANES)] * 3
+                + [(tiles * cells, LANES)] * 5
+                + [(states * tiles * cells, LANES), (states * cells, LANES)]
+                + [((width + 2) * height, LANES)] * 2
+                + [rate_rows, (height, LANES), jax.ShapeDtypeStruct((cells, LANES), BF16)],
+                40 << 20,
             )
-        hot_strip = onehot(mine, entries)
-
-        block = jax.ShapeDtypeStruct((count * height * 3 // 2, LANES), BF16)
-        sent = call(
-            lambda *r: row_kernel((tiles, strips, height, width, strip), dest, *r),
-            [rate, *own, *other, *hots, log_table, proj_row, proj_row2, skip],
-            [block] * strips,
-            [(tiles * height * pitch_of(width), LANES)] * 3
-            + [(tiles * cells, LANES)] * 5
-            + [(states * tiles * cells, LANES), (states * cells, LANES)]
-            + [((width + 2) * height, LANES)] * 2
-            + [(states * 3 // 2 * SUB, LANES)],
-        )
+        proj_col2, conv_w2, bias2 = across(proj_col), across(conv_w), across(bias)
         got = exchange(sent)
         got2 = [across(b) for b in got]
         back = jax.ShapeDtypeStruct((height * strip * 3 // 2, LANES), BF16)
         pitch = total + 2 * SUB
         sent = call(
             lambda *r: column_kernel((strips, height, strip), dest, *r),
-            [rate, *got, *got2, hot_strip, log_table, proj_col, proj_col2, conv_w, conv_w2, bias, bias2, skip],
+            [rate, *got, *got2, log_table, proj_col, proj_col2, conv_w, conv_w2, bias, bias2, skip],
             [back] * strips,
             [(count * pitch, LANES)] * 2
-            + [(strip * pitch_of(total), LANES)] * 3
+            + [(strip * pitch_of(total), LANES)] * 5
             + [(total * strip, LANES)] * 7
             + [(states * total * strip, LANES)] * 2
-            + [(states * 3 // 2 * SUB, LANES)],
+            + [(states * 3 // 2 * SUB, LANES), jax.ShapeDtypeStruct((total * strip, LANES), BF16)],
+            20 << 20,
         )
         got = exchange(sent)
         return call(
@@ -490,6 +790,7 @@
             [*got, gate],
             jax.ShapeDtypeStruct(features.shape, BF16),
             [(cells, LANES)] * 2,
+            8 << 20,
         )
 
     return shards

time: 58.7 us -> 43.8 us (0.75)
  starting transfers between devices: 18.5 us -> 14.1 us
  local copies, waits for them, and re-layouts: 3.87 us -> 0.03 us
  waiting for transfers between devices: 16.7 us -> 13.5 us
  Pallas kernels: 18.1 us -> 15.8 us
  other arithmetic: 1.14 us -> 0 us
    ppermute x9 -> x6, starting transfers between devices: 14.2 us -> 8.93 us  [exchange(): lax.ppermute(blocks[d], axis, [(i, i ^ d) for i in range(strips)])]
    unnamed x51 -> x14, local copies, waits for them, and re-layouts: 2.95 us -> 0.03 us
    ppermute x9 -> x6, waiting for transfers between devices: 11.3 us -> 9.05 us  [exchange(): lax.ppermute(blocks[d], axis, [(i, i ^ d) for i in range(strips)])]
    pallas_call x3 -> x6, Pallas kernels: 18.1 us -> 15.8 us  [call(): pl.pallas_call(kernel, out_shape=outs, in_specs=[hbm() if left else smem(...]
    convert_element_type x1 -> x0, other arithmetic: 1.03 us -> none  [onehot(): return (idx.reshape(-1, 1) == spots).astype(BF16)]
    ppermute x2 -> x1, starting transfers between devices: 2.03 us -> 2.98 us  [shards(): came = lax.ppermute(note, 'cols', swap)]
    ppermute x2 -> x1, waiting for transfers between devices: 2.6 us -> 1.97 us  [shards(): came = lax.ppermute(note, 'cols', swap)]
    ppermute x10 -> x9, waiting for transfers between devices: 2.79 us -> 2.51 us  [across(): return lax.ppermute(v, 'chan', swap)]
  transfers between devices with their start and end apart: 21 -> 16, of which waited for: 10 -> 9; matrix products, arithmetic and copies ran while one was open for 4% -> 0% of each run, Pallas kernels for 0% -> 7%
where the time goes in v3:
time: 43.8 us; the launch traced here: 43.6 us
  Pallas kernels  15.8 us (36%)
  starting transfers between devices  14.1 us (32%)
  waiting for transfers between devices  13.5 us (31%)
    pallas_call x6, Pallas kernels, call(): pl.pallas_call(kernel, out_shape=outs, in_specs=[hbm() if left else smem(...  15.8 us
    ppermute x6, waiting for transfers between devices, exchange(): lax.ppermute(blocks[d], axis, [(i, i ^ d) for i in range(strips)])  9.05 us
    ppermute x6, starting transfers between devices, exchange(): lax.ppermute(blocks[d], axis, [(i, i ^ d) for i in range(strips)])  8.93 us
    ppermute x1, starting transfers between devices, shards(): came = lax.ppermute(note, 'cols', swap)  2.98 us
    ppermute x9, waiting for transfers between devices, across(): return lax.ppermute(v, 'chan', swap)  2.51 us
    ppermute x9, starting transfers between devices, across(): return lax.ppermute(v, 'chan', swap)  2.22 us
    ppermute x1, waiting for transfers between devices, shards(): came = lax.ppermute(note, 'cols', swap)  1.97 us
  transfers between devices with their start and end apart: 16, of which 9 were waited for; matrix products, arithmetic and copies ran while one was open for 0% of the time, Pallas kernels for 7%

profile of v3, /device:TPU:0, one launch (start us, length us, event | category | flops | bytes accessed | tf_op | source)
XLA Modules:
  0.0 43.6 jit_solution(5964997075943014614)
XLA Ops:
  0.0 0.5 %collective-permute-start = (bf16[16,32,192]{2,1,0:T(8,128)(2,1)}, bf16[16,32,192]{2,1,0:T(8,128)(2,1)S(1)}, u32[]{:S(2)}, u32[]{:S(2)}) collective-permute-start(bf16[16,32,192]{2,1,0:T(8,128)(2,1)} %r_1_.1), channel_id=1, source_target_pairs={{0,1},{1,0},{2,3},{3,2},{4,5},{5,4},{6,7},{7,6},{8,9},{9,8},{10,11... | collective-permute-start | bytes 589832 | tf_op jit(solution)/shard_map/ppermute | solution.py:699
  0.5 0.0 collective-permute-start.1
  0.5 1.4 %shard_map.100 = (f32[512,128]{1,0:T(8,128)S(1)}, f32[512,128]{1,0:T(8,128)S(1)}, f32[512,128]{1,0:T(8,128)S(1)}, f32[512,128]{1,0:T(8,128)S(1)}, f32[512,128]{1...) custom-call(f32[16]{0:T(128)} %r_0_.3, ...), custom_call_target="tpu_custom_call" | custom-call | tf_op jit(solution)/shard_map/pallas_call | solution.py:672
  2.0 0.0 collective-permute-done.1.r_1_
  2.0 0.0 collective-permute-done.r_0_
  2.0 3.5 %shard_map.101 = (bf16[480,128]{1,0:T(8,128)(2,1)S(1)}, f32[512,128]{1,0:T(8,128)S(1)}, f32[512,128]{1,0:T(8,128)S(1)}, f32[512,128]{1,0:T(8,128)S(1)}, f32[512,128]{1,0:T(8,128)S(1)}, /*index=5*/f32[512,128]{1,0:T(8,128)S(1)}) custom-call(bf16[16,32,192]{2,1,0:T(8,128)(2,1)S(1)} %collective-permute-done.r_0_, ...), custom_call_target="tpu_custom_call" | custom-call | tf_op jit(solution)/shard_map/pallas_call | solution.py:672
  5.5 3.0 %collective-permute-start.2 = (bf16[480,128]{1,0:T(8,128)(2,1)S(1)}, bf16[480,128]{1,0:T(8,128)(2,1)S(1)}, u32[]{:S(2)}, u32[]{:S(2)}) collective-permute-start(bf16[480,128]{1,0:T(8,128)(2,1)S(1)} %get-tuple-element.36.r_0_), channel_id=1, source_target_pairs={{0,2},{2,0},{1,3},{3,1},{4,6},{6,4},{5,7},{7,5},{8,10},{10,8},{9,1... | collective-permute-start | bytes 368648 | tf_op jit(solution)/shard_map/ppermute | solution.py:740
  8.4 0.0 copy-start.4
  8.5 0.0 copy-start.5
  8.5 0.0 copy-start
  8.5 1.5 %shard_map.102.r_4_ = f32[12288,128]{1,0:T(8,128)S(1)} custom-call(f32[512,128]{1,0:T(8,128)S(1)} %get-tuple-element.39.r_0_, f32[512,128]{1,0:T(8,128)S(1)} %get-tuple-element.40.r_1_, f32[512,128]{1,0:T(8,128)S(1)} %get-tuple-element.41.r_2_, f32[192,128]{1,0:T(8,128)S(1)} %get-tuple-element.33.r_7_.r_3_), custom_call_target="tpu_custom_call" | custom-call | tf_op jit(solution)/shard_map/pallas_call | solution.py:672
  10.0 2.0 %collective-permute-done.2.r_1_ = bf16[480,128]{1,0:T(8,128)(2,1)S(1)} collective-permute-done((bf16[480,128]{1,0:T(8,128)(2,1)S(1)}, bf16[480,128]{1,0:T(8,128)(2,1)S(1)}, u32[]{:S(2)}, u32[]{:S(2)}) %collective-permute-start.2) | collective-permute-done | bytes 122912 | tf_op jit(solution)/shard_map/ppermute | solution.py:740
  11.9 2.0 %shard_map.103 = (bf16[256,128]{1,0:T(8,128)(2,1)S(1)}, bf16[256,128]{1,0:T(8,128)(2,1)S(1)}, bf16[256,128]{1,0:T(8,128)(2,1)S(1)}, bf16[256,128]{1,0:T(8,128)(2,1)S(1)}) custom-call(bf16[480,128]{1,0:T(8,128)(2,1)S(1)} %get-tuple-element.36.r_0_, bf16[480,128]{1,0:T(8,128)(2,1)S(1)} %collective-permute-done.2.r_1_, f32[512,128]{1,0:T(8,128)S(1)} %get-tuple-element.37.r_2_, ...), custom_call_target="tpu_custom_call" | custom-call | tf_op jit(solution)/shard_map/pallas_call | solution.py:672
  14.0 1.9 %collective-permute-start.3 = (bf16[256,128]{1,0:T(8,128)(2,1)S(1)}, bf16[256,128]{1,0:T(8,128)(2,1)S(1)}, u32[]{:S(2)}, u32[]{:S(2)}) collective-permute-start(bf16[256,128]{1,0:T(8,128)(2,1)S(1)} %get-tuple-element.44), channel_id=1, source_target_pairs={{0,4},{4,0},{8,12},{12,8},{1,5},{5,1},{9,13},{13,9},{2,6},{6,2},{1... | collective-permute-start | bytes 196616 | tf_op jit(solution)/shard_map/ppermute | solution.py:693
  15.9 2.6 %collective-permute-start.4 = (bf16[256,128]{1,0:T(8,128)(2,1)S(1)}, bf16[256,128]{1,0:T(8,128)(2,1)S(1)}, u32[]{:S(2)}, u32[]{:S(2)}) collective-permute-start(bf16[256,128]{1,0:T(8,128)(2,1)S(1)} %get-tuple-element.45), channel_id=1, source_target_pairs={{0,8},{4,12},{8,0},{12,4},{1,9},{5,13},{9,1},{13,5},{2,10},{6,14},... | collective-permute-start | bytes 196616 | tf_op jit(solution)/shard_map/ppermute | solution.py:693
  18.4 0.0 collective-permute-start.5
  18.5 0.0 collective-permute-start.6
  18.5 0.0 collective-permute-done.3.r_2_
  18.5 0.5 %collective-permute-start.7 = (bf16[256,128]{1,0:T(8,128)(2,1)S(1)}, bf16[256,128]{1,0:T(8,128)(2,1)S(1)}, u32[]{:S(2)}, u32[]{:S(2)}) collective-permute-start(bf16[256,128]{1,0:T(8,128)(2,1)S(1)} %collective-permute-done.3.r_2_), channel_id=1, source_target_pairs={{0,1},{1,0},{2,3},{3,2},{4,5},{5,4},{6,7},{7,6},{8,9},{9,8},{10,11... | collective-permute-start | bytes 196616 | tf_op jit(solution)/shard_map/ppermute | solution.py:699
  19.0 3.5 %collective-permute-done.4.r_3_ = bf16[256,128]{1,0:T(8,128)(2,1)S(1)} collective-permute-done((bf16[256,128]{1,0:T(8,128)(2,1)S(1)}, bf16[256,128]{1,0:T(8,128)(2,1)S(1)}, u32[]{:S(2)}, u32[]{:S(2)}) %collective-permute-start.4) | collective-permute-done | bytes 65568 | tf_op jit(solution)/shard_map/ppermute | solution.py:693
  22.4 0.0 collective-permute-start.8
  22.4 2.1 %collective-permute-done.5.r_4_ = bf16[256,128]{1,0:T(8,128)(2,1)S(1)} collective-permute-done((bf16[256,128]{1,0:T(8,128)(2,1)S(1)}, bf16[256,128]{1,0:T(8,128)(2,1)S(1)}, u32[]{:S(2)}, u32[]{:S(2)}) %collective-permute-start.5) | collective-permute-done | bytes 65568 | tf_op jit(solution)/shard_map/ppermute | solution.py:693
  24.5 0.0 collective-permute-start.9
  24.5 0.0 copy-done.6
  24.5 0.5 %collective-permute-start.12 = (f32[1,192]{1,0:T(1,128)S(1)}, f32[1,192]{1,0:T(1,128)S(1)}, u32[]{:S(2)}, u32[]{:S(2)}) collective-permute-start(f32[1,192]{1,0:T(1,128)S(1)} %bitcast.8), channel_id=1, source_target_pairs={{0,1},{1,0},{2,3},{3,2},{4,5},{5,4},{6,7},{7,6},{8,9},{9,8},{10,11... | collective-permute-start | bytes 2312 | tf_op jit(solution)/shard_map/ppermute | solution.py:699
  25.0 0.8 %collective-permute-done.12.r_15_ = f32[1,192]{1,0:T(1,128)S(1)} collective-permute-done((f32[1,192]{1,0:T(1,128)S(1)}, f32[1,192]{1,0:T(1,128)S(1)}, u32[]{:S(2)}, u32[]{:S(2)}) %collective-permute-start.12) | collective-permute-done | bytes 800 | tf_op jit(solution)/shard_map/ppermute | solution.py:699
  25.8 0.0 copy-done.3
  25.8 0.3 collective-permute-start.11
  26.2 0.8 %collective-permute-done.11.r_13_ = f32[3,3,192]{2,1,0:T(4,128)S(1)} collective-permute-done((f32[3,3,192]{2,1,0:T(4,128)S(1)}, f32[3,3,192]{2,1,0:T(4,128)S(1)}, u32[]{:S(2)}, u32[]{:S(2)}) %collective-permute-start.11) | collective-permute-done | bytes 6944 | tf_op jit(solution)/shard_map/ppermute | solution.py:699
  27.0 0.0 copy-done.2
  27.0 0.3 collective-permute-start.10
  27.4 0.8 %collective-permute-done.10.r_11_ = bf16[32,192]{1,0:T(8,128)(2,1)S(1)} collective-permute-done((bf16[32,192]{1,0:T(8,128)(2,1)S(1)}, bf16[32,192]{1,0:T(8,128)(2,1)S(1)}, u32[]{:S(2)}, u32[]{:S(2)}) %collective-permute-start.10) | collective-permute-done | bytes 12320 | tf_op jit(solution)/shard_map/ppermute | solution.py:699
  28.2 0.0 collective-permute-done.6.r_5_
  28.2 0.0 collective-permute-done.7.r_6_
  28.2 0.0 collective-permute-done.8.r_7_
  28.2 0.0 collective-permute-done.9.r_8_
  28.2 0.0 copy-done.1
  28.2 0.0 copy-done.4
  28.3 0.0 copy-done.5
  28.3 6.4 %shard_map.104 = (bf16[192,128]{1,0:T(8,128)(2,1)S(1)}, bf16[192,128]{1,0:T(8,128)(2,1)S(1)}, bf16[192,128]{1,0:T(8,128)(2,1)S(1)}, bf16[192,128]{1,0:T(8,128)(2,1)S(1)}) custom-call(f32[16]{0:T(128)S(1)} %copy-done.5, bf16[256,128]{1,0:T(8,128)(2,1)S(1)} %get-tuple-element.43.r_1_, bf16[256,128]{1,0:T(8,128)(2,1)S(1)} %collective-permute-done.3.r_2_, ...), custom_call_target="tpu_custom_call" | custom-call | tf_op jit(solution)/shard_map/pallas_call | solution.py:672
  34.7 0.1 collective-permute-start.13
  34.8 2.0 %collective-permute-start.14 = (bf16[192,128]{1,0:T(8,128)(2,1)S(1)}, bf16[192,128]{1,0:T(8,128)(2,1)S(1)}, u32[]{:S(2)}, u32[]{:S(2)}) collective-permute-start(bf16[192,128]{1,0:T(8,128)(2,1)S(1)} %get-tuple-element.49), channel_id=1, source_target_pairs={{0,8},{4,12},{8,0},{12,4},{1,9},{5,13},{9,1},{13,5},{2,10},{6,14},... | collective-permute-start | bytes 147464 | tf_op jit(solution)/shard_map/ppermute | solution.py:693
  36.8 2.4 %collective-permute-start.15 = (bf16[192,128]{1,0:T(8,128)(2,1)S(1)}, bf16[192,128]{1,0:T(8,128)(2,1)S(1)}, u32[]{:S(2)}, u32[]{:S(2)}) collective-permute-start(bf16[192,128]{1,0:T(8,128)(2,1)S(1)} %get-tuple-element.50), channel_id=1, source_target_pairs={{0,12},{4,8},{8,4},{12,0},{1,13},{5,9},{9,5},{13,1},{2,14},{6,10},... | collective-permute-start | bytes 147464 | tf_op jit(solution)/shard_map/ppermute | solution.py:693
  39.1 0.5 %collective-permute-done.13.r_1_ = bf16[192,128]{1,0:T(8,128)(2,1)S(1)} collective-permute-done((bf16[192,128]{1,0:T(8,128)(2,1)S(1)}, bf16[192,128]{1,0:T(8,128)(2,1)S(1)}, u32[]{:S(2)}, u32[]{:S(2)}) %collective-permute-start.13) | collective-permute-done | bytes 49184 | tf_op jit(solution)/shard_map/ppermute | solution.py:693
  39.6 1.0 %collective-permute-done.14.r_2_ = bf16[192,128]{1,0:T(8,128)(2,1)S(1)} collective-permute-done((bf16[192,128]{1,0:T(8,128)(2,1)S(1)}, bf16[192,128]{1,0:T(8,128)(2,1)S(1)}, u32[]{:S(2)}, u32[]{:S(2)}) %collective-permute-start.14) | collective-permute-done | bytes 49184 | tf_op jit(solution)/shard_map/ppermute | solution.py:693
  40.7 2.0 %collective-permute-done.15.r_3_ = bf16[192,128]{1,0:T(8,128)(2,1)S(1)} collective-permute-done((bf16[192,128]{1,0:T(8,128)(2,1)S(1)}, bf16[192,128]{1,0:T(8,128)(2,1)S(1)}, u32[]{:S(2)}, u32[]{:S(2)}) %collective-permute-start.15) | collective-permute-done | bytes 49184 | tf_op jit(solution)/shard_map/ppermute | solution.py:693
  42.7 0.0 copy-done
  42.7 1.0 %shard_map.105 = bf16[16,32,192]{2,1,0:T(8,128)(2,1)} custom-call(bf16[192,128]{1,0:T(8,128)(2,1)S(1)} %get-tuple-element.47.r_0_, bf16[192,128]{1,0:T(8,128)(2,1)S(1)} %collective-permute-done.13.r_1_, bf16[192,128]{1,0:T(8,128)(2,1)S(1)} %collective-permute-done.14.r_2_, bf16[192,128]{1,0:T(8,128)(2,1)S(1)} %collective-permute-done.15.r_3_, ...), custom_call_target="tpu_custom_call" | custom-call | tf_op jit(solution)/shard_map/pallas_call | solution.py:672
  (4 shorter events, 0.0 us)
Async XLA Ops:
  0.0 2.0 %collective-permute-start = (bf16[16,32,192]{2,1,0:T(8,128)(2,1)}, bf16[16,32,192]{2,1,0:T(8,128)(2,1)S(1)}, u32[]{:S(2)}, u32[]{:S(2)}) collective-permute-start(bf16[16,32,192]{2,1,0:T(8,128)(2,1)} %r_1_.1), channel_id=1, source_target_pairs={{0,1},{1,0},{2,3},{3,2},{4,5},{5,4},{6,7},{7,6},{8,9},{9,8},{10,11... | collective-permute-start | bytes 589832 | tf_op jit(solution)/shard_map/ppermute | solution.py:699
  0.5 1.5 %collective-permute-start.1 = (bf16[32,192]{1,0:T(8,128)(2,1)}, bf16[32,192]{1,0:T(8,128)(2,1)S(1)}, u32[]{:S(2)}, u32[]{:S(2)}) collective-permute-start(bf16[32,192]{1,0:T(8,128)(2,1)} %bitcast.10), channel_id=1, source_target_pairs={{0,1},{1,0},{2,3},{3,2},{4,5},{5,4},{6,7},{7,6},{8,9},{9,8},{10,11... | collective-permute-start | bytes 36872 | tf_op jit(solution)/shard_map/ppermute | solution.py:699
  5.5 6.5 %collective-permute-start.2 = (bf16[480,128]{1,0:T(8,128)(2,1)S(1)}, bf16[480,128]{1,0:T(8,128)(2,1)S(1)}, u32[]{:S(2)}, u32[]{:S(2)}) collective-permute-start(bf16[480,128]{1,0:T(8,128)(2,1)S(1)} %get-tuple-element.36.r_0_), channel_id=1, source_target_pairs={{0,2},{2,0},{1,3},{3,1},{4,6},{6,4},{5,7},{7,5},{8,10},{10,8},{9,1... | collective-permute-start | bytes 368648 | tf_op jit(solution)/shard_map/ppermute | solution.py:740
  8.4 16.1 %copy-start.6 = (f32[192]{0:T(256)S(1)}, f32[192]{0:T(256)}, u32[]{:S(2)}) copy-start(f32[192]{0:T(256)} %param.18) | copy-start | bytes 2308
  8.4 17.4 %copy-start.3 = (f32[3,3,192]{2,1,0:T(4,128)S(1)}, f32[3,3,192]{2,1,0:T(4,128)}, u32[]{:S(2)}) copy-start(f32[3,3,192]{2,1,0:T(4,128)} %r_12_.1) | copy-start | bytes 20740
  8.4 18.6 %copy-start.2 = (bf16[192,32]{0,1:T(8,128)(2,1)S(1)}, bf16[192,32]{0,1:T(8,128)(2,1)}, u32[]{:S(2)}) copy-start(bf16[192,32]{0,1:T(8,128)(2,1)} %param.16) | copy-start | bytes 36868
  8.4 19.8 %copy-start.1 = (f32[16,192]{1,0:T(8,128)S(1)}, f32[16,192]{1,0:T(8,128)}, u32[]{:S(2)}) copy-start(f32[16,192]{1,0:T(8,128)} %r_9_.1) | copy-start | bytes 36868
  8.4 19.8 %copy-start.4 = (f32[192]{0:T(256)S(1)}, f32[192]{0:T(256)}, u32[]{:S(2)}) copy-start(f32[192]{0:T(256)} %param.19) | copy-start | bytes 2308
  8.5 19.8 %copy-start.5 = (f32[16]{0:T(128)S(1)}, f32[16]{0:T(128)}, u32[]{:S(2)}) copy-start(f32[16]{0:T(128)} %r_0_.3) | copy-start | bytes 196
  8.5 34.2 %copy-start = (bf16[16,32,192]{2,1,0:T(8,128)(2,1)S(1)}, bf16[16,32,192]{2,1,0:T(8,128)(2,1)}, u32[]{:S(2)}) copy-start(bf16[16,32,192]{2,1,0:T(8,128)(2,1)} %r_4_.1) | copy-start | bytes 589828
  14.0 4.5 %collective-permute-start.3 = (bf16[256,128]{1,0:T(8,128)(2,1)S(1)}, bf16[256,128]{1,0:T(8,128)(2,1)S(1)}, u32[]{:S(2)}, u32[]{:S(2)}) collective-permute-start(bf16[256,128]{1,0:T(8,128)(2,1)S(1)} %get-tuple-element.44), channel_id=1, source_target_pairs={{0,4},{4,0},{8,12},{12,8},{1,5},{5,1},{9,13},{13,9},{2,6},{6,2},{1... | collective-permute-start | bytes 196616 | tf_op jit(solution)/shard_map/ppermute | solution.py:693
  15.9 6.6 %collective-permute-start.4 = (bf16[256,128]{1,0:T(8,128)(2,1)S(1)}, bf16[256,128]{1,0:T(8,128)(2,1)S(1)}, u32[]{:S(2)}, u32[]{:S(2)}) collective-permute-start(bf16[256,128]{1,0:T(8,128)(2,1)S(1)} %get-tuple-element.45), channel_id=1, source_target_pairs={{0,8},{4,12},{8,0},{12,4},{1,9},{5,13},{9,1},{13,5},{2,10},{6,14},... | collective-permute-start | bytes 196616 | tf_op jit(solution)/shard_map/ppermute | solution.py:693
  18.4 6.1 %collective-permute-start.5 = (bf16[256,128]{1,0:T(8,128)(2,1)S(1)}, bf16[256,128]{1,0:T(8,128)(2,1)S(1)}, u32[]{:S(2)}, u32[]{:S(2)}) collective-permute-start(bf16[256,128]{1,0:T(8,128)(2,1)S(1)} %get-tuple-element.46), channel_id=1, source_target_pairs={{0,12},{4,8},{8,4},{12,0},{1,13},{5,9},{9,5},{13,1},{2,14},{6,10},... | collective-permute-start | bytes 196616 | tf_op jit(solution)/shard_map/ppermute | solution.py:693
  18.5 9.8 %collective-permute-start.6 = (bf16[256,128]{1,0:T(8,128)(2,1)S(1)}, bf16[256,128]{1,0:T(8,128)(2,1)S(1)}, u32[]{:S(2)}, u32[]{:S(2)}) collective-permute-start(bf16[256,128]{1,0:T(8,128)(2,1)S(1)} %get-tuple-element.43.r_1_), channel_id=1, source_target_pairs={{0,1},{1,0},{2,3},{3,2},{4,5},{5,4},{6,7},{7,6},{8,9},{9,8},{10,11... | collective-permute-start | bytes 196616 | tf_op jit(solution)/shard_map/ppermute | solution.py:699
  18.5 9.8 %collective-permute-start.7 = (bf16[256,128]{1,0:T(8,128)(2,1)S(1)}, bf16[256,128]{1,0:T(8,128)(2,1)S(1)}, u32[]{:S(2)}, u32[]{:S(2)}) collective-permute-start(bf16[256,128]{1,0:T(8,128)(2,1)S(1)} %collective-permute-done.3.r_2_), channel_id=1, source_target_pairs={{0,1},{1,0},{2,3},{3,2},{4,5},{5,4},{6,7},{7,6},{8,9},{9,8},{10,11... | collective-permute-start | bytes 196616 | tf_op jit(solution)/shard_map/ppermute | solution.py:699
  22.4 5.8 %collective-permute-start.8 = (bf16[256,128]{1,0:T(8,128)(2,1)S(1)}, bf16[256,128]{1,0:T(8,128)(2,1)S(1)}, u32[]{:S(2)}, u32[]{:S(2)}) collective-permute-start(bf16[256,128]{1,0:T(8,128)(2,1)S(1)} %collective-permute-done.4.r_3_), channel_id=1, source_target_pairs={{0,1},{1,0},{2,3},{3,2},{4,5},{5,4},{6,7},{7,6},{8,9},{9,8},{10,11... | collective-permute-start | bytes 196616 | tf_op jit(solution)/shard_map/ppermute | solution.py:699
  24.5 3.7 %collective-permute-start.9 = (bf16[256,128]{1,0:T(8,128)(2,1)S(1)}, bf16[256,128]{1,0:T(8,128)(2,1)S(1)}, u32[]{:S(2)}, u32[]{:S(2)}) collective-permute-start(bf16[256,128]{1,0:T(8,128)(2,1)S(1)} %collective-permute-done.5.r_4_), channel_id=1, source_target_pairs={{0,1},{1,0},{2,3},{3,2},{4,5},{5,4},{6,7},{7,6},{8,9},{9,8},{10,11... | collective-permute-start | bytes 196616 | tf_op jit(solution)/shard_map/ppermute | solution.py:699
  24.5 1.3 %collective-permute-start.12 = (f32[1,192]{1,0:T(1,128)S(1)}, f32[1,192]{1,0:T(1,128)S(1)}, u32[]{:S(2)}, u32[]{:S(2)}) collective-permute-start(f32[1,192]{1,0:T(1,128)S(1)} %bitcast.8), channel_id=1, source_target_pairs={{0,1},{1,0},{2,3},{3,2},{4,5},{5,4},{6,7},{7,6},{8,9},{9,8},{10,11... | collective-permute-start | bytes 2312 | tf_op jit(solution)/shard_map/ppermute | solution.py:699
  25.8 1.2 %collective-permute-start.11 = (f32[3,3,192]{2,1,0:T(4,128)S(1)}, f32[3,3,192]{2,1,0:T(4,128)S(1)}, u32[]{:S(2)}, u32[]{:S(2)}) collective-permute-start(f32[3,3,192]{2,1,0:T(4,128)S(1)} %copy-done.3), channel_id=1, source_target_pairs={{0,1},{1,0},{2,3},{3,2},{4,5},{5,4},{6,7},{7,6},{8,9},{9,8},{10,11... | collective-permute-start | bytes 20744 | tf_op jit(solution)/shard_map/ppermute | solution.py:699
  27.0 1.2 %collective-permute-start.10 = (bf16[32,192]{1,0:T(8,128)(2,1)S(1)}, bf16[32,192]{1,0:T(8,128)(2,1)S(1)}, u32[]{:S(2)}, u32[]{:S(2)}) collective-permute-start(bf16[32,192]{1,0:T(8,128)(2,1)S(1)} %bitcast.4), channel_id=1, source_target_pairs={{0,1},{1,0},{2,3},{3,2},{4,5},{5,4},{6,7},{7,6},{8,9},{9,8},{10,11... | collective-permute-start | bytes 36872 | tf_op jit(solution)/shard_map/ppermute | solution.py:699
  34.7 4.9 %collective-permute-start.13 = (bf16[192,128]{1,0:T(8,128)(2,1)S(1)}, bf16[192,128]{1,0:T(8,128)(2,1)S(1)}, u32[]{:S(2)}, u32[]{:S(2)}) collective-permute-start(bf16[192,128]{1,0:T(8,128)(2,1)S(1)} %get-tuple-element.48), channel_id=1, source_target_pairs={{0,4},{4,0},{8,12},{12,8},{1,5},{5,1},{9,13},{13,9},{2,6},{6,2},{1... | collective-permute-start | bytes 147464 | tf_op jit(solution)/shard_map/ppermute | solution.py:693
  34.8 5.9 %collective-permute-start.14 = (bf16[192,128]{1,0:T(8,128)(2,1)S(1)}, bf16[192,128]{1,0:T(8,128)(2,1)S(1)}, u32[]{:S(2)}, u32[]{:S(2)}) collective-permute-start(bf16[192,128]{1,0:T(8,128)(2,1)S(1)} %get-tuple-element.49), channel_id=1, source_target_pairs={{0,8},{4,12},{8,0},{12,4},{1,9},{5,13},{9,1},{13,5},{2,10},{6,14},... | collective-permute-start | bytes 147464 | tf_op jit(solution)/shard_map/ppermute | solution.py:693
  36.8 5.9 %collective-permute-start.15 = (bf16[192,128]{1,0:T(8,128)(2,1)S(1)}, bf16[192,128]{1,0:T(8,128)(2,1)S(1)}, u32[]{:S(2)}, u32[]{:S(2)}) collective-permute-start(bf16[192,128]{1,0:T(8,128)(2,1)S(1)} %get-tuple-element.50), channel_id=1, source_target_pairs={{0,12},{4,8},{8,4},{12,0},{1,13},{5,9},{9,5},{13,1},{2,14},{6,10},... | collective-permute-start | bytes 147464 | tf_op jit(solution)/shard_map/ppermute | solution.py:693

commit v4 on v3

--- a/solution.py
+++ b/solution.py
@@ -8,7 +8,7 @@
 
 LANES = 128
 SUB = 8
-UNROLL = 4
+UNROLL = 8
 LOG2E = 1.4426950408889634
 F32 = jnp.float32
 BF16 = jnp.bfloat16
@@ -76,22 +76,20 @@
     return rows + SUB // 2 if rows % SUB == 0 else rows
 
 
-def advance(carry, xa, xb, la, lb, drive, out, rates):
-    states = rates.shape[0] // SUB * 2 // 3
-    shape = xa.shape
-    half = low_half(shape)
+def advance(carry, xa, xb, decay, drive, out):
+    states = len(carry) * 2 // 3
+    half = low_half(xa.shape)
     drive = [drive(s) for s in range(states)]
     out = None if out is None else [out(s) for s in range(states)]
     new, ya, yb = [], [], []
     for s in range(states):
-        st = jnp.exp2(la * rates[s * SUB : s * SUB + shape[0], :]) * carry[s] + drive[s] * xa
+        st = decay(s) * carry[s] + drive[s] * xa
         new.append(st)
         if out:
             ya.append(out[s] * st)
     for j in range(states // 2):
         b = jnp.where(half, drive[2 * j], drive[2 * j + 1])
-        at = (states + j) * SUB
-        st = jnp.exp2(lb * rates[at : at + shape[0], :]) * carry[states + j] + b * xb
+        st = decay(states + j) * carry[states + j] + b * xb
         new.append(st)
         if out:
             yb.append(jnp.where(half, out[2 * j], out[2 * j + 1]) * st)
@@ -103,6 +101,12 @@
 
     yb = tree(yb)
     return tuple(new), tree(ya), None if yb is None else yb + pltpu.roll(yb, LANES // 2, 1)
+
+
+def decays(la, lb, rates):
+    kinds = rates.shape[0] // SUB
+    rows = la.shape[0]
+    return lambda k: jnp.exp2((la if k < kinds * 2 // 3 else lb) * rates[k * SUB : k * SUB + rows, :])
 
 
 def spread(coeff, column):
@@ -129,8 +133,8 @@
         to[...] = spread(cf_ref[:rows, :], column)
 
 
-def thrice(v):
-    return jnp.concatenate([v, v, v], axis=0)
+def fill(v):
+    return jnp.concatenate([v] * (LANES // v.shape[0]), axis=0)
 
 
 def row_kernel(dims, dest, *refs):
@@ -152,7 +156,7 @@
     table = tables(table_ref)
     entries = table_ref.shape[0]
     entry_ref[...] = jnp.zeros(entry_ref.shape, F32)
-    proj, proj2 = thrice(proj_ref[...]), thrice(proj2_ref[...])
+    proj, proj2 = fill(proj_ref[...]), fill(proj2_ref[...])
     for d in range(tiles):
         x = own[d][...].reshape(cells, -1)
         part = pl.ds(d * cells, cells)
@@ -166,7 +170,7 @@
             to, cut = pl.ds((d * height + h) * pitch, width), slice(h * width, (h + 1) * width)
             raw[0][to, :] = xa[cut]
             raw[1][to, :] = xb[cut]
-            raw[2][to, : 6 * states] = coeff[cut]
+            raw[2][to, :] = coeff[cut]
         entry = idxs[d][...].astype(F32)
         if d == 0:
             entry_ref[:, :width] = entry
@@ -214,7 +218,7 @@
                 return weights[pl.ds(pl.multiple_of(s * cells + here, SUB), SUB), :]
 
             carry, ya, yb = advance(
-                carry, xa, xb, la_ref[at, :], lb_ref[at, :], drive, out if wanted else None, rates
+                carry, xa, xb, decays(la_ref[at, :], lb_ref[at, :], rates), drive, out if wanted else None
             )
             if wanted:
                 ya, yb = ya + skip_a * xa, yb + skip_b * xb
@@ -279,7 +283,6 @@
     for copy in copies:
         copy.wait()
     rate_ref, own_ref, idx_ref, table_ref, proj_ref, skip_ref = held
-    states = rate_ref.shape[0]
     cells = height * width
     pitch = pitch_of(width)
 
@@ -287,14 +290,14 @@
     marks[...] = table
     entries = table_ref.shape[0]
     x = own_ref[...].reshape(cells, -1)
-    coeff = dot_t(x, thrice(proj_ref[...]))
+    coeff = dot_t(x, fill(proj_ref[...]))
     xf = x.astype(F32)
     xa, xb = xf[:, :LANES], twice(xf[:, LANES:])
     for h in range(height):
         to, cut = pl.ds(h * pitch, width), slice(h * width, (h + 1) * width)
         raw[0][to, :] = xa[cut]
         raw[1][to, :] = xb[cut]
-        raw[2][to, : 6 * states] = coeff[cut]
+        raw[2][to, :] = coeff[cut]
     entry = idx_ref[...].astype(F32)
     entry_ref[...] = jnp.zeros(entry_ref.shape, F32)
     entry_ref[:, :width] = entry
@@ -345,9 +348,9 @@
     cells = height * width
     pitch = pitch_of(width)
 
-    coeff = dot_t(other_ref[...].reshape(cells, -1), thrice(proj2_ref[...]))
+    coeff = dot_t(other_ref[...].reshape(cells, -1), fill(proj2_ref[...]))
     for h in range(height):
-        raw[h * pitch : h * pitch + width, : 6 * states] = coeff[h * width : (h + 1) * width]
+        raw[h * pitch : h * pitch + width, :] = coeff[h * width : (h + 1) * width]
     in_order(dims, (raw,), (cf_ref,), half_ref)
     every = [(s, drives.at[s * cells : (s + 1) * cells, :], cells) for s in range(states)]
     every += [(states + s, weights.at[s * cells : (s + 1) * cells, :], cells) for s in range(states)]
@@ -366,11 +369,9 @@
                 carry,
                 xa,
                 xb,
-                la,
-                lb,
+                decays(la, lb, rates),
                 lambda s: at_step(drives, s, cells, here),
                 lambda s: at_step(weights, s, cells, here),
-                rates,
             )
             sum_a, sum_b = sum_a + la, sum_b + lb
             ya_ref[at, :] = ya + skip_a * xa
@@ -496,133 +497,145 @@
     return jnp.where(half, v, turned), jnp.where(half, turned, v)
 
 
-def column_kernel(dims, dest, *refs):
+def conv_kernel(dims, dest, *refs):
     strips, height, strip = dims
-    rate_ref = refs[0]
-    blocks = (refs[1 : 1 + strips], refs[1 + strips : 1 + 2 * strips])
-    at = 1 + 2 * strips
-    table_ref = refs[at]
-    projs = refs[at + 1 : at + 3]
-    conv_ws = refs[at + 3 : at + 5]
-    conv_bs = refs[at + 5 : at + 7]
-    skip_ref = refs[at + 7]
-    outs = refs[at + 8 : at + 8 + strips]
-    scratch = refs[at + 8 + strips :]
-    ra_ref, rb_ref, raw = *scratch[:2], scratch[2:7]
-    xa_ref, xb_ref, cf_ref, la_ref, lb_ref, ya_ref, yb_ref, drives, weights, rates, hot_ref = scratch[7:]
-    states = rate_ref.shape[0]
+    blocks, (conv_ref, bias_ref, proj_ref) = refs[:strips], refs[strips : strips + 3]
+    mids, cf_ref, rows_refs = refs[strips + 3 : strips + 5], refs[strips + 5], refs[strips + 6 :]
     row = lax.axis_index("rows")
     total = strips * height
     pitch = total + 2 * SUB
     leap = pitch_of(total)
     count = strip + 2
-    fill_rates(rate_ref, rates)
-
-    table = tables(table_ref)
-    entries = table_ref.shape[0]
+    half = height // 2
     rows = count * height * 3 // 2
+
+    zero = jnp.zeros((SUB, LANES), F32)
+    for k in range(count):
+        for ref in rows_refs:
+            ref[pl.ds(k * pitch, SUB), :] = zero
+            ref[pl.ds(k * pitch + SUB + total, SUB), :] = zero
     for d in range(strips):
-        entry = blocks[0][d][rows:, :].astype(F32)
+        base = pl.multiple_of(dest(row, d) * height, SUB) + SUB
+        va = blocks[d][: count * height, :].astype(F32)
+        low, high = unpack(blocks[d][count * height : rows, :].astype(F32))
+        for k in range(count):
+            to = pl.multiple_of(base + k * pitch, SUB)
+            rows_refs[0][pl.ds(to, height), :] = va[k * height : (k + 1) * height]
+            rows_refs[1][pl.ds(to, half), :] = low[k * half : (k + 1) * half]
+            rows_refs[1][pl.ds(pl.multiple_of(to + half, SUB), half), :] = high[k * half : (k + 1) * half]
+    taps = conv_ref[...]
+    bias = bias_ref[...]
+    for src, dst, cut in zip(rows_refs, mids, (lambda v: v[..., :LANES], lambda v: twice(v[..., LANES:]))):
+        cut_taps, add = cut(taps), cut(bias)
+        taps_wide = [[jnp.broadcast_to(cut_taps[a, b][None, :], (SUB, LANES)) for b in range(3)] for a in range(3)]
+        start = jnp.broadcast_to(add, (SUB, LANES))
+
+        def conv(i, unused, src=src, dst=dst, taps_wide=taps_wide, start=start):
+            sums = [start] * strip
+            for k in range(count):
+                for a in range(3):
+                    v = src[pl.ds(k * pitch + i * SUB + SUB - 1 + a, SUB), :]
+                    for b in range(3):
+                        if 0 <= k - b < strip:
+                            sums[k - b] = sums[k - b] + taps_wide[a][b] * v
+            for k in range(strip):
+                v = sums[k] / (1.0 + jnp.exp(-sums[k]))
+                dst[pl.ds(k * leap + i * SUB, SUB), :] = v.astype(BF16).astype(F32)
+            return unused
+
+        lax.fori_loop(0, total // SUB, conv, 0)
+    proj = fill(proj_ref[...])
+    for k in range(strip):
+        at = pl.ds(k * leap, total)
+        cf_ref[at, :] = dot_t(mids[0][at, :].astype(BF16), proj[:, :LANES]) + dot_t(
+            mids[1][at, : LANES // 2].astype(BF16), proj[:, LANES:]
+        )
+
+
+def strip_at(h, strip, base=0):
+    at = base + h * strip
+    return pl.ds(at if strip % SUB else pl.multiple_of(at, SUB), strip)
+
+
+def decay_kernel(dims, dest, *refs):
+    strips, height, strip = dims
+    blocks, mids, marks, rates = refs[:strips], refs[strips : strips + 2], refs[strips + 2], refs[strips + 3]
+    xa_ref, xb_ref, out_ref = refs[strips + 4 : strips + 7]
+    raw, hot_ref = refs[strips + 7 : strips + 9], refs[strips + 9]
+    row = lax.axis_index("rows")
+    total = strips * height
+    leap = pitch_of(total)
+    cells = total * strip
+    kinds = rates.shape[0] // SUB
+    parts = marks.shape[0]
+    rows = (strip + 2) * height * 3 // 2
+    for d in range(strips):
+        entry = blocks[d][rows:, :].astype(F32)
         base = pl.multiple_of(dest(row, d) * height, 2 * SUB)
         for k in range(strip):
-            hot_ref[pl.ds(pl.multiple_of(base + k * total, 2 * SUB), height), :] = mark(spread(entry, k), entries)
-    logs = dot(hot_ref[:, : 3 * entries], table)
+            to = pl.ds(pl.multiple_of(base + k * total, 2 * SUB), height)
+            hot_ref[to, :] = mark(spread(entry, k), parts // 3)
+    logs = dot(hot_ref[:, :parts], marks[...])
     for k in range(strip):
-        cut = logs[k * total : (k + 1) * total]
-        raw[3][k * leap : k * leap + total, :] = cut[:, :LANES]
-        raw[4][k * leap : k * leap + total, :] = cut[:, LANES:]
-    zero = jnp.zeros((SUB, LANES), F32)
-    for k in range(count):
-        for ref in (ra_ref, rb_ref):
-            ref[pl.ds(k * pitch, SUB), :] = zero
-            ref[pl.ds(k * pitch + SUB + total, SUB), :] = zero
-
-    for side in (1, 0):
-        for d in range(strips):
-            base = pl.multiple_of(dest(row, d) * height, SUB) + SUB
-            va = blocks[side][d][: count * height, :].astype(F32)
-            low, high = unpack(blocks[side][d][count * height : rows, :].astype(F32))
-            h2 = height // 2
-            for k in range(count):
-                to = pl.multiple_of(base + k * pitch, SUB)
-                ra_ref[pl.ds(to, height), :] = va[k * height : (k + 1) * height]
-                rb_ref[pl.ds(to, h2), :] = low[k * h2 : (k + 1) * h2]
-                rb_ref[pl.ds(pl.multiple_of(to + h2, SUB), h2), :] = high[k * h2 : (k + 1) * h2]
-        taps = conv_ws[side][...]
-        bias = conv_bs[side][...]
-        for src, dst, cut in (
-            (ra_ref, raw[0], lambda v: v[..., :LANES]),
-            (rb_ref, raw[1], lambda v: twice(v[..., LANES:])),
-        ):
-            cut_taps, add = cut(taps), cut(bias)
-            taps_wide = [[jnp.broadcast_to(cut_taps[a, b][None, :], (SUB, LANES)) for b in range(3)] for a in range(3)]
-            start = jnp.broadcast_to(add, (SUB, LANES))
-
-            def conv(i, unused, src=src, dst=dst, taps_wide=taps_wide, start=start):
-                sums = [start] * strip
-                for k in range(count):
-                    for a in range(3):
-                        v = src[pl.ds(k * pitch + i * SUB + SUB - 1 + a, SUB), :]
-                        for b in range(3):
-                            if 0 <= k - b < strip:
-                                sums[k - b] = sums[k - b] + taps_wide[a][b] * v
-                for k in range(strip):
-                    v = sums[k] / (1.0 + jnp.exp(-sums[k]))
-                    dst[pl.ds(k * leap + i * SUB, SUB), :] = v.astype(BF16).astype(F32)
-                return unused
-
-            lax.fori_loop(0, total // SUB, conv, 0)
-        proj = thrice(projs[side][...])
-        for k in range(strip):
-            at = pl.ds(k * leap, total)
-            part = dot_t(raw[0][at, :].astype(BF16), proj[:, :LANES]) + dot_t(
-                raw[1][at, : LANES // 2].astype(BF16), proj[:, LANES:]
-            )
-            raw[2][at, : 6 * states] = part if side else part + raw[2][at, : 6 * states]
-
-    skip = skip_ref[...]
-    skip_a, skip_b = skip[:, :LANES], twice(skip[:, LANES:])
-
-    def here(h, base=0):
-        at = base + h * strip
-        return pl.ds(at if strip % SUB else pl.multiple_of(at, SUB), strip)
+        cut, at = logs[k * total : (k + 1) * total], pl.ds(k * leap, total)
+        raw[0][at, :] = cut[:, :LANES]
+        raw[1][at, :] = cut[:, LANES:]
+
+    def step(h, unused):
+        place = pl.ds(h, strip, stride=leap)
+        at = strip_at(h, strip)
+        xa_ref[at, :] = mids[0][place, :]
+        xb_ref[at, :] = mids[1][place, :]
+        decay = decays(raw[0][place, :], raw[1][place, :], rates)
+        for k in range(kinds):
+            out_ref[strip_at(h, strip, k * cells), :] = decay(k)
+        return unused
+
+    steps(total, step, 0)
+
+
+def column_kernel(dims, dest, *refs):
+    strips, height, strip = dims
+    own_ref, came_ref, xa_ref, xb_ref, decay_ref, skips = refs[:6]
+    outs = refs[6 : 6 + strips]
+    cf_ref, ya_ref, yb_ref, drives, weights = refs[6 + strips :]
+    row = lax.axis_index("rows")
+    total = strips * height
+    leap = pitch_of(total)
+    cells = total * strip
+    states = weights.shape[0] // cells
 
     def order(h, unused):
-        for old, new in zip(raw, (xa_ref, xb_ref, cf_ref, la_ref, lb_ref)):
-            new[here(h), :] = old[pl.ds(h, strip, stride=leap), :]
+        place = pl.ds(h, strip, stride=leap)
+        cf_ref[strip_at(h, strip), :] = own_ref[place, :] + came_ref[place, :]
         return unused
 
     steps(total, order, 0)
-    cells = total * strip
     every = [(s, drives.at[s * cells : (s + 1) * cells, :], cells) for s in range(states)]
     every += [(states + s, weights.at[s * cells : (s + 1) * cells, :], cells) for s in range(states)]
     cut = states * 5 // 4 // 2 * 2
     spread_all(cf_ref, 2 * states, every[:cut], every[cut:])
-
-    def body(h, carry):
-        at = here(h)
+    skip_a, skip_b = skips[:strip, :], skips[SUB : SUB + strip, :]
+
+    def step(h, carry):
+        at = strip_at(h, strip)
         xa, xb = xa_ref[at, :], xb_ref[at, :]
         carry, ya, yb = advance(
             carry,
             xa,
             xb,
-            la_ref[at, :],
-            lb_ref[at, :],
-            lambda s: drives[here(h, s * cells), :],
-            lambda s: weights[here(h, s * cells), :],
-            rates,
+            lambda k: decay_ref[strip_at(h, strip, k * cells), :],
+            lambda s: drives[strip_at(h, strip, s * cells), :],
+            lambda s: weights[strip_at(h, strip, s * cells), :],
         )
         ya_ref[at, :] = ya + skip_a * xa
         yb_ref[at, :] = yb + skip_b * xb
         return carry
 
-    zeros = tuple(jnp.zeros((strip, LANES), F32) for _ in range(states + states // 2))
-    steps(total, body, zeros)
-
+    steps(total, step, tuple(jnp.zeros((strip, LANES), F32) for _ in range(states * 3 // 2)))
     cells = height * strip
     for d in range(strips):
-        start = pl.multiple_of(dest(row, d) * cells, SUB)
-        from_ = pl.ds(start, cells)
+        from_ = pl.ds(pl.multiple_of(dest(row, d) * cells, SUB), cells)
         outs[d][:cells, :] = ya_ref[from_, :].astype(BF16)
         yb = yb_ref[from_, :]
         low, high = yb[: cells // 2], yb[cells // 2 :]
@@ -712,24 +725,24 @@
         high = pitch_of(width) * height
         other = [across(features)]
         proj_row2 = across(proj_row)
+        wide = jax.ShapeDtypeStruct((cells, LANES), F32)
+        rates = jax.ShapeDtypeStruct(rate_rows, F32)
+        entries = log_table.shape[0]
+        xa, xb, la, lb, half, rates, skips, entry, marks = call(
+            lambda *r: own_kernel((height, width), *r),
+            [rate, features, decay_idx, log_table, proj_row, skip],
+            [wide] * 5
+            + [
+                rates,
+                jax.ShapeDtypeStruct((2 * SUB, LANES), F32),
+                jax.ShapeDtypeStruct((height, LANES), F32),
+                jax.ShapeDtypeStruct((3 * entries, 2 * LANES), BF16),
+            ],
+            [(high, LANES)] * 3 + [jax.ShapeDtypeStruct((cells, LANES), BF16)],
+            8 << 20,
+            left=True,
+        )
         if tiles == 2:
-            wide = jax.ShapeDtypeStruct((cells, LANES), F32)
-            rates = jax.ShapeDtypeStruct(rate_rows, F32)
-            entries = log_table.shape[0]
-            xa, xb, la, lb, half, rates, skips, entry, marks = call(
-                lambda *r: own_kernel((height, width), *r),
-                [rate, features, decay_idx, log_table, proj_row, skip],
-                [wide] * 5
-                + [
-                    rates,
-                    jax.ShapeDtypeStruct((2 * SUB, LANES), F32),
-                    jax.ShapeDtypeStruct((height, LANES), F32),
-                    jax.ShapeDtypeStruct((3 * entries, 2 * LANES), BF16),
-                ],
-                [(high, LANES)] * 3 + [jax.ShapeDtypeStruct((cells, LANES), BF16)],
-                8 << 20,
-                left=True,
-            )
             note, ta, tb, sa, sb, cf = call(
                 lambda *r: tile_kernel((height, width), *r),
                 [other[0], proj_row2, xa, xb, la, lb, half, rates, skips, entry],
@@ -768,20 +781,31 @@
                 + [rate_rows, (height, LANES), jax.ShapeDtypeStruct((cells, LANES), BF16)],
                 40 << 20,
             )
-        proj_col2, conv_w2, bias2 = across(proj_col), across(conv_w), across(bias)
         got = exchange(sent)
-        got2 = [across(b) for b in got]
         back = jax.ShapeDtypeStruct((height * strip * 3 // 2, LANES), BF16)
-        pitch = total + 2 * SUB
+        dims = strips, height, strip
+        apart = jax.ShapeDtypeStruct((strip * pitch_of(total), LANES), F32)
+        mid_a, mid_b, part = call(
+            lambda *r: conv_kernel(dims, dest, *r),
+            [*got, conv_w, bias, proj_col],
+            [apart] * 3,
+            [(count * (total + 2 * SUB), LANES)] * 2,
+            8 << 20,
+        )
+        part2 = across(part)
+        wide = jax.ShapeDtypeStruct((total * strip, LANES), F32)
+        xa, xb, decay = call(
+            lambda *r: decay_kernel(dims, dest, *r),
+            [*got, mid_a, mid_b, marks, rates],
+            [wide] * 2 + [jax.ShapeDtypeStruct((kinds * total * strip, LANES), F32)],
+            [apart] * 2 + [jax.ShapeDtypeStruct((total * strip, LANES), BF16)],
+            8 << 20,
+        )
         sent = call(
-            lambda *r: column_kernel((strips, height, strip), dest, *r),
-            [rate, *got, *got2, log_table, proj_col, proj_col2, conv_w, conv_w2, bias, bias2, skip],
+            lambda *r: column_kernel(dims, dest, *r),
+            [part, part2, xa, xb, decay, skips],
             [back] * strips,
-            [(count * pitch, LANES)] * 2
-            + [(strip * pitch_of(total), LANES)] * 5
-            + [(total * strip, LANES)] * 7
-            + [(states * total * strip, LANES)] * 2
-            + [(states * 3 // 2 * SUB, LANES), jax.ShapeDtypeStruct((total * strip, LANES), BF16)],
+            [wide] * 3 + [(states * total * strip, LANES)] * 2,
             20 << 20,
         )
         got = exchange(sent)

time: 43.8 us -> 38.8 us (0.89)
  waiting for transfers between devices: 13.5 us -> 11.6 us
  starting transfers between devices: 14.1 us -> 12.4 us
  Pallas kernels: 15.8 us -> 14.5 us
    ppermute x9 -> x3, waiting for transfers between devices: 2.51 us -> 0.28 us  [across(): return lax.ppermute(v, 'chan', swap)]
    ppermute x9 -> x3, starting transfers between devices: 2.22 us -> 0.52 us  [across(): return lax.ppermute(v, 'chan', swap)]
    pallas_call x6 -> x8, Pallas kernels: 15.8 us -> 14.5 us  [call(): pl.pallas_call(kernel, out_shape=outs, in_specs=[hbm() if left else smem(...]
  transfers between devices with their start and end apart: 16 -> 10, of which waited for: 9 -> 6; matrix products, arithmetic and copies ran while one was open for 0% -> 0% of each run, Pallas kernels for 7% -> 11%
where the time goes in v4:
time: 38.8 us; the launch traced here: 38.6 us
  Pallas kernels  14.5 us (37%)
  starting transfers between devices  12.4 us (32%)
  waiting for transfers between devices  11.6 us (30%)
    pallas_call x8, Pallas kernels, call(): pl.pallas_call(kernel, out_shape=outs, in_specs=[hbm() if left else smem(...  14.5 us
    ppermute x6, waiting for transfers between devices, exchange(): lax.ppermute(blocks[d], axis, [(i, i ^ d) for i in range(strips)])  9.26 us
    ppermute x6, starting transfers between devices, exchange(): lax.ppermute(blocks[d], axis, [(i, i ^ d) for i in range(strips)])  8.93 us
    ppermute x1, starting transfers between devices, shards(): came = lax.ppermute(note, 'cols', swap)  2.98 us
    ppermute x1, waiting for transfers between devices, shards(): came = lax.ppermute(note, 'cols', swap)  2.04 us
  transfers between devices with their start and end apart: 10, of which 6 were waited for; matrix products, arithmetic and copies ran while one was open for 0% of the time, Pallas kernels for 11%

profile of v4, /device:TPU:0, one launch (start us, length us, event | category | flops | bytes accessed | tf_op | source)
XLA Modules:
  0.0 38.6 jit_solution(1900495381329186666)
XLA Ops:
  0.0 0.5 %collective-permute-start = (bf16[16,32,192]{2,1,0:T(8,128)(2,1)}, bf16[16,32,192]{2,1,0:T(8,128)(2,1)S(1)}, u32[]{:S(2)}, u32[]{:S(2)}) collective-permute-start(bf16[16,32,192]{2,1,0:T(8,128)(2,1)} %r_1_.1), channel_id=1, source_target_pairs={{0,1},{1,0},{2,3},{3,2},{4,5},{5,4},{6,7},{7,6},{8,9},{9,8},{10,11... | collective-permute-start | bytes 589832 | tf_op jit(solution)/shard_map/ppermute | solution.py:712
  0.5 0.0 collective-permute-start.1
  0.5 1.4 %shard_map.100 = (f32[512,128]{1,0:T(8,128)S(1)}, f32[512,128]{1,0:T(8,128)S(1)}, f32[512,128]{1,0:T(8,128)S(1)}, f32[512,128]{1,0:T(8,128)S(1)}, f32[512,128]{1...) custom-call(f32[16]{0:T(128)} %r_0_.1, ...), custom_call_target="tpu_custom_call" | custom-call | tf_op jit(solution)/shard_map/pallas_call | solution.py:685
  1.9 0.0 collective-permute-done.1.r_1_
  2.0 0.0 collective-permute-done.r_0_
  2.0 3.3 %shard_map.101 = (bf16[480,128]{1,0:T(8,128)(2,1)S(1)}, f32[512,128]{1,0:T(8,128)S(1)}, f32[512,128]{1,0:T(8,128)S(1)}, f32[512,128]{1,0:T(8,128)S(1)}, f32[512,128]{1,0:T(8,128)S(1)}, /*index=5*/f32[512,128]{1,0:T(8,128)S(1)}) custom-call(bf16[16,32,192]{2,1,0:T(8,128)(2,1)S(1)} %collective-permute-done.r_0_, ...), custom_call_target="tpu_custom_call" | custom-call | tf_op jit(solution)/shard_map/pallas_call | solution.py:685
  5.2 3.0 %collective-permute-start.2 = (bf16[480,128]{1,0:T(8,128)(2,1)S(1)}, bf16[480,128]{1,0:T(8,128)(2,1)S(1)}, u32[]{:S(2)}, u32[]{:S(2)}) collective-permute-start(bf16[480,128]{1,0:T(8,128)(2,1)S(1)} %get-tuple-element.42.r_0_), channel_id=1, source_target_pairs={{0,2},{2,0},{1,3},{3,1},{4,6},{6,4},{5,7},{7,5},{8,10},{10,8},{9,1... | collective-permute-start | bytes 368648 | tf_op jit(solution)/shard_map/ppermute | solution.py:753
  8.2 0.0 copy-start.1
  8.2 0.0 copy-start.2
  8.2 0.0 copy-start.3
  8.2 1.4 %shard_map.102.r_4_ = f32[12288,128]{1,0:T(8,128)S(1)} custom-call(f32[512,128]{1,0:T(8,128)S(1)} %get-tuple-element.45.r_0_, f32[512,128]{1,0:T(8,128)S(1)} %get-tuple-element.46.r_1_, f32[512,128]{1,0:T(8,128)S(1)} %get-tuple-element.47.r_2_, f32[192,128]{1,0:T(8,128)S(1)} %get-tuple-element.39.r_7_.r_3_), custom_call_target="tpu_custom_call" | custom-call | tf_op jit(solution)/shard_map/pallas_call | solution.py:685
  9.7 2.0 %collective-permute-done.2.r_1_ = bf16[480,128]{1,0:T(8,128)(2,1)S(1)} collective-permute-done((bf16[480,128]{1,0:T(8,128)(2,1)S(1)}, bf16[480,128]{1,0:T(8,128)(2,1)S(1)}, u32[]{:S(2)}, u32[]{:S(2)}) %collective-permute-start.2) | collective-permute-done | bytes 122912 | tf_op jit(solution)/shard_map/ppermute | solution.py:753
  11.7 0.0 copy-start
  11.7 1.4 %shard_map.103 = (bf16[256,128]{1,0:T(8,128)(2,1)S(1)}, bf16[256,128]{1,0:T(8,128)(2,1)S(1)}, bf16[256,128]{1,0:T(8,128)(2,1)S(1)}, bf16[256,128]{1,0:T(8,128)(2,1)S(1)}) custom-call(bf16[480,128]{1,0:T(8,128)(2,1)S(1)} %get-tuple-element.42.r_0_, bf16[480,128]{1,0:T(8,128)(2,1)S(1)} %collective-permute-done.2.r_1_, f32[512,128]{1,0:T(8,128)S(1)} %get-tuple-element.43.r_2_, ...), custom_call_target="tpu_custom_call" | custom-call | tf_op jit(solution)/shard_map/pallas_call | solution.py:685
  13.1 1.9 %collective-permute-start.3 = (bf16[256,128]{1,0:T(8,128)(2,1)S(1)}, bf16[256,128]{1,0:T(8,128)(2,1)S(1)}, u32[]{:S(2)}, u32[]{:S(2)}) collective-permute-start(bf16[256,128]{1,0:T(8,128)(2,1)S(1)} %get-tuple-element.50), channel_id=1, source_target_pairs={{0,4},{4,0},{8,12},{12,8},{1,5},{5,1},{9,13},{13,9},{2,6},{6,2},{1... | collective-permute-start | bytes 196616 | tf_op jit(solution)/shard_map/ppermute | solution.py:706
  15.0 2.6 %collective-permute-start.4 = (bf16[256,128]{1,0:T(8,128)(2,1)S(1)}, bf16[256,128]{1,0:T(8,128)(2,1)S(1)}, u32[]{:S(2)}, u32[]{:S(2)}) collective-permute-start(bf16[256,128]{1,0:T(8,128)(2,1)S(1)} %get-tuple-element.51), channel_id=1, source_target_pairs={{0,8},{4,12},{8,0},{12,4},{1,9},{5,13},{9,1},{13,5},{2,10},{6,14},... | collective-permute-start | bytes 196616 | tf_op jit(solution)/shard_map/ppermute | solution.py:706
  17.6 0.0 collective-permute-start.5
  17.6 0.0 collective-permute-done.3.r_1_
  17.6 4.0 %collective-permute-done.4.r_2_ = bf16[256,128]{1,0:T(8,128)(2,1)S(1)} collective-permute-done((bf16[256,128]{1,0:T(8,128)(2,1)S(1)}, bf16[256,128]{1,0:T(8,128)(2,1)S(1)}, u32[]{:S(2)}, u32[]{:S(2)}) %collective-permute-start.4) | collective-permute-done | bytes 65568 | tf_op jit(solution)/shard_map/ppermute | solution.py:706
  21.6 2.1 %collective-permute-done.5.r_3_ = bf16[256,128]{1,0:T(8,128)(2,1)S(1)} collective-permute-done((bf16[256,128]{1,0:T(8,128)(2,1)S(1)}, bf16[256,128]{1,0:T(8,128)(2,1)S(1)}, u32[]{:S(2)}, u32[]{:S(2)}) %collective-permute-start.5) | collective-permute-done | bytes 65568 | tf_op jit(solution)/shard_map/ppermute | solution.py:706
  23.7 0.0 copy-done.1
  23.7 0.0 copy-done.2
  23.7 0.0 copy-done.3
  23.7 1.3 %shard_map.104 = (f32[544,128]{1,0:T(8,128)S(1)}, f32[544,128]{1,0:T(8,128)S(1)}, f32[544,128]{1,0:T(8,128)S(1)}) custom-call(bf16[256,128]{1,0:T(8,128)(2,1)S(1)} %get-tuple-element.49.r_0_, bf16[256,128]{1,0:T(8,128)(2,1)S(1)} %collective-permute-done.3.r_1_, bf16[256,128]{1,0:T(8,128)(2,1)S(1)} %collective-permute-done.4.r_2_, ...), custom_call_target="tpu_custom_call" | custom-call | tf_op jit(solution)/shard_map/pallas_call | solution.py:685
  25.0 0.0 collective-permute-start.6
  25.0 1.3 %shard_map.105 = (f32[512,128]{1,0:T(8,128)S(1)}, f32[512,128]{1,0:T(8,128)S(1)}, f32[12288,128]{1,0:T(8,128)S(1)}) custom-call(bf16[256,128]{1,0:T(8,128)(2,1)S(1)} %get-tuple-element.49.r_0_, bf16[256,128]{1,0:T(8,128)(2,1)S(1)} %collective-permute-done.3.r_1_, bf16[256,128]{1,0:T(8,128)(2,1)S(1)} %collective-permute-done.4.r_2_, ...), custom_call_target="tpu_custom_call" | custom-call | tf_op jit(solution)/shard_map/pallas_call | solution.py:685
  26.3 0.3 collective-permute-done.6.r_1_
  26.6 3.4 %shard_map.106 = (bf16[192,128]{1,0:T(8,128)(2,1)S(1)}, bf16[192,128]{1,0:T(8,128)(2,1)S(1)}, bf16[192,128]{1,0:T(8,128)(2,1)S(1)}, bf16[192,128]{1,0:T(8,128)(2,1)S(1)}) custom-call(f32[544,128]{1,0:T(8,128)S(1)} %get-tuple-element.53.r_0_, f32[544,128]{1,0:T(8,128)S(1)} %collective-permute-done.6.r_1_, f32[512,128]{1,0:T(8,128)S(1)} %get-tuple-element.56.r_2_, ...), custom_call_target="tpu_custom_call" | custom-call | tf_op jit(solution)/shard_map/pallas_call | solution.py:685
  30.0 0.1 collective-permute-start.7
  30.1 1.7 %collective-permute-start.8 = (bf16[192,128]{1,0:T(8,128)(2,1)S(1)}, bf16[192,128]{1,0:T(8,128)(2,1)S(1)}, u32[]{:S(2)}, u32[]{:S(2)}) collective-permute-start(bf16[192,128]{1,0:T(8,128)(2,1)S(1)} %get-tuple-element.61), channel_id=1, source_target_pairs={{0,8},{4,12},{8,0},{12,4},{1,9},{5,13},{9,1},{13,5},{2,10},{6,14},... | collective-permute-start | bytes 147464 | tf_op jit(solution)/shard_map/ppermute | solution.py:706
  31.7 2.7 %collective-permute-start.9 = (bf16[192,128]{1,0:T(8,128)(2,1)S(1)}, bf16[192,128]{1,0:T(8,128)(2,1)S(1)}, u32[]{:S(2)}, u32[]{:S(2)}) collective-permute-start(bf16[192,128]{1,0:T(8,128)(2,1)S(1)} %get-tuple-element.62), channel_id=1, source_target_pairs={{0,12},{4,8},{8,4},{12,0},{1,13},{5,9},{9,5},{13,1},{2,14},{6,10},... | collective-permute-start | bytes 147464 | tf_op jit(solution)/shard_map/ppermute | solution.py:706
  34.5 0.4 %collective-permute-done.7.r_1_ = bf16[192,128]{1,0:T(8,128)(2,1)S(1)} collective-permute-done((bf16[192,128]{1,0:T(8,128)(2,1)S(1)}, bf16[192,128]{1,0:T(8,128)(2,1)S(1)}, u32[]{:S(2)}, u32[]{:S(2)}) %collective-permute-start.7) | collective-permute-done | bytes 49184 | tf_op jit(solution)/shard_map/ppermute | solution.py:706
  34.9 2.8 %collective-permute-done.8.r_2_ = bf16[192,128]{1,0:T(8,128)(2,1)S(1)} collective-permute-done((bf16[192,128]{1,0:T(8,128)(2,1)S(1)}, bf16[192,128]{1,0:T(8,128)(2,1)S(1)}, u32[]{:S(2)}, u32[]{:S(2)}) %collective-permute-start.8) | collective-permute-done | bytes 49184 | tf_op jit(solution)/shard_map/ppermute | solution.py:706
  37.7 0.0 collective-permute-done.9.r_3_
  37.7 0.0 copy-done
  37.7 1.0 %shard_map.107 = bf16[16,32,192]{2,1,0:T(8,128)(2,1)} custom-call(bf16[192,128]{1,0:T(8,128)(2,1)S(1)} %get-tuple-element.59.r_0_, bf16[192,128]{1,0:T(8,128)(2,1)S(1)} %collective-permute-done.7.r_1_, bf16[192,128]{1,0:T(8,128)(2,1)S(1)} %collective-permute-done.8.r_2_, bf16[192,128]{1,0:T(8,128)(2,1)S(1)} %collective-permute-done.9.r_3_, ...), custom_call_target="tpu_custom_call" | custom-call | tf_op jit(solution)/shard_map/pallas_call | solution.py:685
Async XLA Ops:
  0.0 2.0 %collective-permute-start = (bf16[16,32,192]{2,1,0:T(8,128)(2,1)}, bf16[16,32,192]{2,1,0:T(8,128)(2,1)S(1)}, u32[]{:S(2)}, u32[]{:S(2)}) collective-permute-start(bf16[16,32,192]{2,1,0:T(8,128)(2,1)} %r_1_.1), channel_id=1, source_target_pairs={{0,1},{1,0},{2,3},{3,2},{4,5},{5,4},{6,7},{7,6},{8,9},{9,8},{10,11... | collective-permute-start | bytes 589832 | tf_op jit(solution)/shard_map/ppermute | solution.py:712
  0.5 1.5 %collective-permute-start.1 = (bf16[32,192]{1,0:T(8,128)(2,1)}, bf16[32,192]{1,0:T(8,128)(2,1)S(1)}, u32[]{:S(2)}, u32[]{:S(2)}) collective-permute-start(bf16[32,192]{1,0:T(8,128)(2,1)} %bitcast.6), channel_id=1, source_target_pairs={{0,1},{1,0},{2,3},{3,2},{4,5},{5,4},{6,7},{7,6},{8,9},{9,8},{10,11... | collective-permute-start | bytes 36872 | tf_op jit(solution)/shard_map/ppermute | solution.py:712
  5.2 6.5 %collective-permute-start.2 = (bf16[480,128]{1,0:T(8,128)(2,1)S(1)}, bf16[480,128]{1,0:T(8,128)(2,1)S(1)}, u32[]{:S(2)}, u32[]{:S(2)}) collective-permute-start(bf16[480,128]{1,0:T(8,128)(2,1)S(1)} %get-tuple-element.42.r_0_), channel_id=1, source_target_pairs={{0,2},{2,0},{1,3},{3,1},{4,6},{6,4},{5,7},{7,5},{8,10},{10,8},{9,1... | collective-permute-start | bytes 368648 | tf_op jit(solution)/shard_map/ppermute | solution.py:753
  8.2 15.5 %copy-start.1 = (bf16[192,32]{0,1:T(8,128)(2,1)S(1)}, bf16[192,32]{0,1:T(8,128)(2,1)}, u32[]{:S(2)}) copy-start(bf16[192,32]{0,1:T(8,128)(2,1)} %param.16) | copy-start | bytes 36868
  8.2 15.5 %copy-start.2 = (f32[3,3,192]{2,1,0:T(4,128)S(1)}, f32[3,3,192]{2,1,0:T(4,128)}, u32[]{:S(2)}) copy-start(f32[3,3,192]{2,1,0:T(4,128)} %r_4_.2) | copy-start | bytes 20740
  8.2 15.5 %copy-start.3 = (f32[192]{0:T(256)S(1)}, f32[192]{0:T(256)}, u32[]{:S(2)}) copy-start(f32[192]{0:T(256)} %param.18) | copy-start | bytes 2308
  11.7 26.0 %copy-start = (bf16[16,32,192]{2,1,0:T(8,128)(2,1)S(1)}, bf16[16,32,192]{2,1,0:T(8,128)(2,1)}, u32[]{:S(2)}) copy-start(bf16[16,32,192]{2,1,0:T(8,128)(2,1)} %r_4_.3) | copy-start | bytes 589828
  13.1 4.5 %collective-permute-start.3 = (bf16[256,128]{1,0:T(8,128)(2,1)S(1)}, bf16[256,128]{1,0:T(8,128)(2,1)S(1)}, u32[]{:S(2)}, u32[]{:S(2)}) collective-permute-start(bf16[256,128]{1,0:T(8,128)(2,1)S(1)} %get-tuple-element.50), channel_id=1, source_target_pairs={{0,4},{4,0},{8,12},{12,8},{1,5},{5,1},{9,13},{13,9},{2,6},{6,2},{1... | collective-permute-start | bytes 196616 | tf_op jit(solution)/shard_map/ppermute | solution.py:706
  15.0 6.6 %collective-permute-start.4 = (bf16[256,128]{1,0:T(8,128)(2,1)S(1)}, bf16[256,128]{1,0:T(8,128)(2,1)S(1)}, u32[]{:S(2)}, u32[]{:S(2)}) collective-permute-start(bf16[256,128]{1,0:T(8,128)(2,1)S(1)} %get-tuple-element.51), channel_id=1, source_target_pairs={{0,8},{4,12},{8,0},{12,4},{1,9},{5,13},{9,1},{13,5},{2,10},{6,14},... | collective-permute-start | bytes 196616 | tf_op jit(solution)/shard_map/ppermute | solution.py:706
  17.6 6.1 %collective-permute-start.5 = (bf16[256,128]{1,0:T(8,128)(2,1)S(1)}, bf16[256,128]{1,0:T(8,128)(2,1)S(1)}, u32[]{:S(2)}, u32[]{:S(2)}) collective-permute-start(bf16[256,128]{1,0:T(8,128)(2,1)S(1)} %get-tuple-element.52), channel_id=1, source_target_pairs={{0,12},{4,8},{8,4},{12,0},{1,13},{5,9},{9,5},{13,1},{2,14},{6,10},... | collective-permute-start | bytes 196616 | tf_op jit(solution)/shard_map/ppermute | solution.py:706
  25.0 1.6 %collective-permute-start.6 = (f32[544,128]{1,0:T(8,128)S(1)}, f32[544,128]{1,0:T(8,128)S(1)}, u32[]{:S(2)}, u32[]{:S(2)}) collective-permute-start(f32[544,128]{1,0:T(8,128)S(1)} %get-tuple-element.53.r_0_), channel_id=1, source_target_pairs={{0,1},{1,0},{2,3},{3,2},{4,5},{5,4},{6,7},{7,6},{8,9},{9,8},{10,11... | collective-permute-start | bytes 835592 | tf_op jit(solution)/shard_map/ppermute | solution.py:712
  30.0 4.9 %collective-permute-start.7 = (bf16[192,128]{1,0:T(8,128)(2,1)S(1)}, bf16[192,128]{1,0:T(8,128)(2,1)S(1)}, u32[]{:S(2)}, u32[]{:S(2)}) collective-permute-start(bf16[192,128]{1,0:T(8,128)(2,1)S(1)} %get-tuple-element.60), channel_id=1, source_target_pairs={{0,4},{4,0},{8,12},{12,8},{1,5},{5,1},{9,13},{13,9},{2,6},{6,2},{1... | collective-permute-start | bytes 147464 | tf_op jit(solution)/shard_map/ppermute | solution.py:706
  30.1 7.6 %collective-permute-start.8 = (bf16[192,128]{1,0:T(8,128)(2,1)S(1)}, bf16[192,128]{1,0:T(8,128)(2,1)S(1)}, u32[]{:S(2)}, u32[]{:S(2)}) collective-permute-start(bf16[192,128]{1,0:T(8,128)(2,1)S(1)} %get-tuple-element.61), channel_id=1, source_target_pairs={{0,8},{4,12},{8,0},{12,4},{1,9},{5,13},{9,1},{13,5},{2,10},{6,14},... | collective-permute-start | bytes 147464 | tf_op jit(solution)/shard_map/ppermute | solution.py:706
  31.7 5.9 %collective-permute-start.9 = (bf16[192,128]{1,0:T(8,128)(2,1)S(1)}, bf16[192,128]{1,0:T(8,128)(2,1)S(1)}, u32[]{:S(2)}, u32[]{:S(2)}) collective-permute-start(bf16[192,128]{1,0:T(8,128)(2,1)S(1)} %get-tuple-element.62), channel_id=1, source_target_pairs={{0,12},{4,8},{8,4},{12,0},{1,13},{5,9},{9,5},{13,1},{2,14},{6,10},... | collective-permute-start | bytes 147464 | tf_op jit(solution)/shard_map/ppermute | solution.py:706
